TPU v7x, 128 devices: a whole 4x4x4 slice. The times are simulated.
128 devices in a mesh: view: 8 (over y_hi, x), gz: 16 (over z, y_lo, core).
Axes of the slice: x: 4, y: 4 (y_hi: 2, y_lo: 2; y = y_hi * 2 + y_lo), z: 4, core: 2. Of those that a mesh axis runs over, the one named last changes fastest.
Arguments:
- views_data: float32 [8, 256, 96, 1024], P('view', 'gz'), may hold values from 0.2 to 40
- estimate: float32 [256, 96, 1024], P('gz'), may hold values from 0.5 to 1.5
- kernels: float32 [8, 3, 31], P('view'), may hold values from 0.001 to 3
Outputs:
- deconvolved: float32 [256, 96, 1024], P('gz')
All inputs are finite; a program needn't handle non-finite values.
Results may differ from a plain program's by a relative error of at most 0.0001.
Values sent between devices are 32-bit elements; how exact they have to be, the bound alone decides.
No kernel may reach another device: no remote copies, remote signals or barrier semaphores. Data moves between devices by JAX's collectives and lax.ppermute only.
A program may use at most 128 MiB of HBM per device.

v0:
```python
import jax
import jax.numpy as jnp
from jax import lax
from jax.sharding import PartitionSpec as P

TAPS = 31
ITERS = 2
RADIUS = 15


def padded_2(value, sides, width):
    for axis, dim in sides:
        size, length = (lax.axis_size(axis), value.shape[dim])
        up = [(i, (i + 1) % size) for i in range(size - 1)]
        down = [(j, i) for i, j in up]
        last = lax.slice_in_dim(value, length - width, length, axis=dim)
        initial = lax.slice_in_dim(value, 0, width, axis=dim)
        before = lax.ppermute(last, axis, up)
        after = lax.ppermute(initial, axis, down)
        value = jnp.concatenate([before, value, after], axis=dim)
    return value


def toeplitz(tap_values, count):
    row_pos = jnp.arange(count)[:, None]
    col_pos = jnp.arange(count)[None, :]
    offsets = row_pos - col_pos + RADIUS
    matrix = jnp.zeros((count, count), jnp.float32)
    for offset in range(TAPS):
        matrix = matrix + jnp.where(offsets == offset, tap_values[offset], 0.0)
    return matrix


def tap_sum(padded, tap_values, flipped, depth):
    result = jnp.zeros((depth,) + padded.shape[1:], jnp.float32)
    for offset in range(TAPS):
        start = 2 * RADIUS - offset if flipped else offset
        result = result + tap_values[offset] * padded[start : start + depth]
    return result


def z_pass(volume, tap_values, flipped):
    padded = padded_2(volume, (("gz", 0),), RADIUS)
    return tap_sum(padded, tap_values, flipped, volume.shape[0])


def xy_pass(volume, mat_x, mat_y):
    passed = jnp.dot(volume, mat_x, precision=lax.Precision.HIGHEST)
    return jnp.einsum("zyx,yw->zwx", passed, mat_y, precision=lax.Precision.HIGHEST)


def per_device(views_data, estimate, kernels):
    tap_norm = kernels[0] / jnp.sum(kernels[0], axis=-1, keepdims=True)
    data_slab = views_data[0]
    mat_x = toeplitz(tap_norm[0], estimate.shape[2])
    mat_y = toeplitz(tap_norm[1], estimate.shape[1])
    views_count = lax.axis_size("view")
    for number in range(ITERS):
        blurred = z_pass(xy_pass(estimate, mat_x, mat_y), tap_norm[2], False)
        ratio = data_slab / blurred
        back = z_pass(xy_pass(ratio, mat_x.T, mat_y.T), tap_norm[2], True)
        logs = jnp.log(back)
        logsum = lax.psum(logs, "view")
        estimate = estimate * jnp.exp(logsum / views_count)
    return estimate


def solution(mesh):
    return jax.shard_map(
        per_device,
        mesh=mesh,
        in_specs=(P("view", "gz", None, None), P("gz", None, None), P("view", None, None)),
        out_specs=P("gz", None, None),
        check_vma=False,
    )
```

profile of v0, /device:TPU:1, one launch (start us, length us, event | category | flops | bytes accessed | tf_op | source)
XLA Modules:
  0.0 1528.6 jit_solution(3375969861306123260)
XLA Ops:
  11.0 45.9 %fusion.432 = f32[1024,16,96]{0,2,1:T(8,128)S(1)} fusion(f32[16,96,1024]{2,1,0:T(8,128)} %param.4, f32[]{:T(128)} %bitcast.65, f32[]{:T(128)} %bitcast.64, f32[]{:T(128)} %bitcast.63, f32[]{:T(128)} %bitcast.62, f32[]{:T(128)} %bitcast.61, f32[]{:T(128)} %bitcast.60, f32[]{:T(128)} %bitcast.59, f32[]{:T(128)} %bitcast.58, f32[]{:T(128)} %bitcast.57, ...), kind=kOutput, calls=%fused_computation.606 | convolution fusion | flops 19425918976 | bytes 12583036 | tf_op jit(solution)/shard_map/dot_general | solution.py:48
  56.9 26.1 %fusion.527 = f32[16,96,1024]{2,1,0:T(8,128)S(1)} fusion(f32[1024,16,96]{0,2,1:T(8,128)S(1)} %fusion.432, f32[]{:T(128)} %bitcast.31, f32[]{:T(128)} %bitcast.30, f32[]{:T(128)} %bitcast.29, f32[]{:T(128)} %bitcast.28, f32[]{:T(128)} %bitcast.27, f32[]{:T(128)} %bitcast.26, f32[]{:T(128)} %bitcast.25, f32[]{:T(128)} %bitcast.24, f32[]{:T(128)} %bitcast.23, ...), kind=kOutput, calls=%fused_computation.703 | convolution fusion | flops 1812805632 | bytes 12583036 | tf_op jit(solution)/shard_map/zyx,yw->zwx/dot_general | solution.py:49
  83.0 6.4 fusion.827
  89.4 4.6 collective-permute-start
  97.2 60.8 %collective-permute-done = f32[15,96,1024]{2,1,0:T(8,128)} collective-permute-done((f32[15,96,1024]{2,1,0:T(8,128)}, f32[15,96,1024]{2,1,0:T(8,128)}, u32[]{:S(2)}, u32[]{:S(2)}) %collective-permute-start) | collective-permute-done | bytes 5898272 | tf_op jit(solution)/shard_map/ppermute | solution.py:18
  158.0 65.2 %collective-permute-done.1 = f32[15,96,1024]{2,1,0:T(8,128)} collective-permute-done((f32[15,96,1024]{2,1,0:T(8,128)}, f32[15,96,1024]{2,1,0:T(8,128)}, u32[]{:S(2)}, u32[]{:S(2)}) %collective-permute-start.1) | collective-permute-done | bytes 5898272 | tf_op jit(solution)/shard_map/ppermute | solution.py:19
  223.1 153.6 %fusion.295 = f32[16,96,1024]{2,1,0:T(8,128)} fusion(f32[16,96,1024]{2,1,0:T(8,128)} %copy-done.1, f32[15,96,1024]{2,1,0:T(8,128)} %collective-permute-done.1, f32[15,96,1024]{2,1,0:T(8,128)} %collective-permute-done, f32[1,16,96,1024]{3,2,1,0:T(8,128)} %param.3, f32[]{:T(128)} %bitcast.98, f32[]{:T(128)} %bitcast.97, f32[]{:T(128)} %bitcast.96, ...), kind=kOutput, calls=%fused_computation.491 | convolution fusion | flops 19570622464 | bytes 30671096 | tf_op jit(solution)/shard_map/dot_general | solution.py:48
  376.7 27.5 %convolution_bitcast_fusion.2 = f32[16,96,1024]{2,1,0:T(8,128)S(1)} fusion(f32[16,96,1024]{2,1,0:T(8,128)} %fusion.295, f32[]{:T(128)} %bitcast.31, f32[]{:T(128)} %bitcast.30, f32[]{:T(128)} %bitcast.29, f32[]{:T(128)} %bitcast.28, f32[]{:T(128)} %bitcast.27, f32[]{:T(128)} %bitcast.26, f32[]{:T(128)} %bitcast.25, f32[]{:T(128)} %bitcast.24, ...), kind=kOutput, calls=%fused_computation.706 | convolution fusion | flops 1812805632 | bytes 12583036 | tf_op jit(solution)/shard_map/zyx,yw->zwx/dot_general | solution.py:49
  404.2 6.0 fusion.826
  415.9 121.8 %collective-permute-done.2 = f32[15,96,1024]{2,1,0:T(8,128)} collective-permute-done((f32[15,96,1024]{2,1,0:T(8,128)}, f32[15,96,1024]{2,1,0:T(8,128)}, u32[]{:S(2)}, u32[]{:S(2)}) %collective-permute-start.2) | collective-permute-done | bytes 5898272 | tf_op jit(solution)/shard_map/ppermute | solution.py:19
  537.7 64.1 %fusion.207 = f32[16,96,1024]{2,1,0:T(8,128)} fusion(f32[16,96,1024]{2,1,0:T(8,128)S(1)} %convolution_bitcast_fusion.2, f32[15,96,1024]{2,1,0:T(8,128)} %collective-permute-done.3, f32[15,96,1024]{2,1,0:T(8,128)} %collective-permute-done.2, f32[]{:T(128)} %bitcast.98, f32[]{:T(128)} %bitcast.97, f32[]{:T(128)} %bitcast.96, f32[]{:T(128)} %bitcast.95, ...), kind=kLoop, calls=%fused_computation.403 | loop fusion | flops 143130624 | bytes 24379516 | tf_op jit(solution)/shard_map/log | solution.py:62
  601.9 152.4 %all-reduce.3.cloned.1.call-done = f32[16,96,1024]{2,1,0:T(8,128)} async-done(((f32[16,96,1024]{2,1,0:T(8,128)}), f32[16,96,1024]{2,1,0:T(8,128)}) %all-reduce.3.cloned.1.call-update) | async-done | bytes 6291472 | tf_op jit(solution)/shard_map/psum | solution.py:63
  754.3 66.6 %fusion.429 = f32[16,96,1024]{2,1,0:T(8,128)S(1)} fusion(f32[]{:T(128)} %bitcast.65, f32[]{:T(128)} %bitcast.64, f32[]{:T(128)} %bitcast.63, f32[]{:T(128)} %bitcast.62, f32[]{:T(128)} %bitcast.61, f32[]{:T(128)} %bitcast.60, f32[]{:T(128)} %bitcast.59, f32[]{:T(128)} %bitcast.58, f32[]{:T(128)} %bitcast.57, f32[]{:T(128)} %bitcast.56, f32[]{:T(128)} %bitcast.55, ...), kind=kOutput, calls=%fused_computation.603 | convolution fusion | flops 19429064704 | bytes 18874492 | tf_op jit(solution)/shard_map/dot_general | solution.py:48
  820.9 25.7 %convolution_bitcast_fusion.1 = f32[16,96,1024]{2,1,0:T(8,128)S(1)} fusion(f32[16,96,1024]{2,1,0:T(8,128)S(1)} %fusion.429, f32[]{:T(128)} %bitcast.31, f32[]{:T(128)} %bitcast.30, f32[]{:T(128)} %bitcast.29, f32[]{:T(128)} %bitcast.28, f32[]{:T(128)} %bitcast.27, f32[]{:T(128)} %bitcast.26, f32[]{:T(128)} %bitcast.25, f32[]{:T(128)} %bitcast.24, ...), kind=kOutput, calls=%fused_computation.705 | convolution fusion | flops 1812805632 | bytes 12583036 | tf_op jit(solution)/shard_map/zyx,yw->zwx/dot_general | solution.py:49
  846.7 6.4 fusion.825
  859.8 60.0 %collective-permute-done.4 = f32[15,96,1024]{2,1,0:T(8,128)} collective-permute-done((f32[15,96,1024]{2,1,0:T(8,128)}, f32[15,96,1024]{2,1,0:T(8,128)}, u32[]{:S(2)}, u32[]{:S(2)}) %collective-permute-start.4) | collective-permute-done | bytes 5898272 | tf_op jit(solution)/shard_map/ppermute | solution.py:18
  919.8 65.8 %collective-permute-done.5 = f32[15,96,1024]{2,1,0:T(8,128)} collective-permute-done((f32[15,96,1024]{2,1,0:T(8,128)}, f32[15,96,1024]{2,1,0:T(8,128)}, u32[]{:S(2)}, u32[]{:S(2)}) %collective-permute-start.5) | collective-permute-done | bytes 5898272 | tf_op jit(solution)/shard_map/ppermute | solution.py:19
  985.6 153.0 %fusion.92 = f32[16,96,1024]{2,1,0:T(8,128)} fusion(f32[16,96,1024]{2,1,0:T(8,128)} %copy-done, f32[15,96,1024]{2,1,0:T(8,128)} %collective-permute-done.5, f32[15,96,1024]{2,1,0:T(8,128)} %collective-permute-done.4, f32[1,16,96,1024]{3,2,1,0:T(8,128)} %param.3, f32[]{:T(128)} %bitcast.98, f32[]{:T(128)} %bitcast.97, f32[]{:T(128)} %bitcast.96, ...), kind=kOutput, calls=%fused_computation.316 | convolution fusion | flops 19570622464 | bytes 30671096 | tf_op jit(solution)/shard_map/dot_general | solution.py:48
  1138.6 27.5 %convolution_bitcast_fusion = f32[16,96,1024]{2,1,0:T(8,128)S(1)} fusion(f32[16,96,1024]{2,1,0:T(8,128)} %fusion.92, f32[]{:T(128)} %bitcast.31, f32[]{:T(128)} %bitcast.30, f32[]{:T(128)} %bitcast.29, f32[]{:T(128)} %bitcast.28, f32[]{:T(128)} %bitcast.27, f32[]{:T(128)} %bitcast.26, f32[]{:T(128)} %bitcast.25, f32[]{:T(128)} %bitcast.24, f32[]{:T(128)} %bitcast.23, ...), kind=kOutput, calls=%fused_computation.704 | convolution fusion | flops 1812805632 | bytes 12583036 | tf_op jit(solution)/shard_map/zyx,yw->zwx/dot_general | solution.py:49
  1166.1 6.0 fusion.824
  1177.9 122.6 %collective-permute-done.6 = f32[15,96,1024]{2,1,0:T(8,128)} collective-permute-done((f32[15,96,1024]{2,1,0:T(8,128)}, f32[15,96,1024]{2,1,0:T(8,128)}, u32[]{:S(2)}, u32[]{:S(2)}) %collective-permute-start.6) | collective-permute-done | bytes 5898272 | tf_op jit(solution)/shard_map/ppermute | solution.py:19
  1300.5 64.0 %fusion.4 = f32[16,96,1024]{2,1,0:T(8,128)} fusion(f32[16,96,1024]{2,1,0:T(8,128)S(1)} %convolution_bitcast_fusion, f32[15,96,1024]{2,1,0:T(8,128)} %collective-permute-done.7, f32[15,96,1024]{2,1,0:T(8,128)} %collective-permute-done.6, f32[]{:T(128)} %bitcast.98, f32[]{:T(128)} %bitcast.97, f32[]{:T(128)} %bitcast.96, f32[]{:T(128)} %bitcast.95, ...), kind=kLoop, calls=%fused_computation.228 | loop fusion | flops 143130624 | bytes 24379516 | tf_op jit(solution)/shard_map/log | solution.py:62
  1364.5 146.9 %all-reduce.5.cloned.1.call-done = f32[16,96,1024]{2,1,0:T(8,128)} async-done(((f32[16,96,1024]{2,1,0:T(8,128)}), f32[16,96,1024]{2,1,0:T(8,128)}) %all-reduce.5.cloned.1.call-update) | async-done | bytes 6291472 | tf_op jit(solution)/shard_map/psum | solution.py:63
  1511.4 9.9 exponential_multiply_fusion
  (24 shorter events, 26.1 us)
Async XLA Ops:
  6.5 747.8 %all-reduce.3.cloned.1.call-start = ((), (), s32[]{:S(2)}) async-start(), calls=%async_computation | async-start | bytes 12582912 | tf_op jit(solution)/shard_map/psum | solution.py:63
  83.0 6.4 copy-start.1
  89.4 68.6 %collective-permute-start = (f32[15,96,1024]{2,1,0:T(8,128)}, f32[15,96,1024]{2,1,0:T(8,128)}, u32[]{:S(2)}, u32[]{:S(2)}) collective-permute-start(f32[15,96,1024]{2,1,0:T(8,128)} %get-tuple-element.11), channel_id=1, source_target_pairs={{0,1},{1,2},{2,3},{3,4},{4,5},{5,6},{6,7},{7,8},{8,9},{9,10},{10,1... | collective-permute-start | bytes 17694728 | tf_op jit(solution)/shard_map/ppermute | solution.py:18
  94.0 129.2 %collective-permute-start.1 = (f32[15,96,1024]{2,1,0:T(8,128)}, f32[15,96,1024]{2,1,0:T(8,128)}, u32[]{:S(2)}, u32[]{:S(2)}) collective-permute-start(f32[15,96,1024]{2,1,0:T(8,128)} %get-tuple-element.12), channel_id=1, source_target_pairs={{1,0},{2,1},{3,2},{4,3},{5,4},{6,5},{7,6},{8,7},{9,8},{10,9},{11,1... | collective-permute-start | bytes 17694728 | tf_op jit(solution)/shard_map/ppermute | solution.py:19
  410.2 127.5 %collective-permute-start.2 = (f32[15,96,1024]{2,1,0:T(8,128)}, f32[15,96,1024]{2,1,0:T(8,128)}, u32[]{:S(2)}, u32[]{:S(2)}) collective-permute-start(f32[15,96,1024]{2,1,0:T(8,128)} %get-tuple-element.9), channel_id=1, source_target_pairs={{1,0},{2,1},{3,2},{4,3},{5,4},{6,5},{7,6},{8,7},{9,8},{10,9},{11,1... | collective-permute-start | bytes 17694728 | tf_op jit(solution)/shard_map/ppermute | solution.py:19
  412.3 125.4 %collective-permute-start.3 = (f32[15,96,1024]{2,1,0:T(8,128)}, f32[15,96,1024]{2,1,0:T(8,128)}, u32[]{:S(2)}, u32[]{:S(2)}) collective-permute-start(f32[15,96,1024]{2,1,0:T(8,128)} %get-tuple-element.10), channel_id=1, source_target_pairs={{0,1},{1,2},{2,3},{3,4},{4,5},{5,6},{6,7},{7,8},{8,9},{9,10},{10,1... | collective-permute-start | bytes 17694728 | tf_op jit(solution)/shard_map/ppermute | solution.py:18
  601.9 909.5 %all-reduce.5.cloned.1.call-start = ((), (), s32[]{:S(2)}) async-start(), calls=%async_computation.1 | async-start | bytes 12582912 | tf_op jit(solution)/shard_map/psum | solution.py:63
  846.6 6.4 copy-start
  853.0 66.8 %collective-permute-start.4 = (f32[15,96,1024]{2,1,0:T(8,128)}, f32[15,96,1024]{2,1,0:T(8,128)}, u32[]{:S(2)}, u32[]{:S(2)}) collective-permute-start(f32[15,96,1024]{2,1,0:T(8,128)} %get-tuple-element.7), channel_id=1, source_target_pairs={{0,1},{1,2},{2,3},{3,4},{4,5},{5,6},{6,7},{7,8},{8,9},{9,10},{10,1... | collective-permute-start | bytes 17694728 | tf_op jit(solution)/shard_map/ppermute | solution.py:18
  855.8 129.8 %collective-permute-start.5 = (f32[15,96,1024]{2,1,0:T(8,128)}, f32[15,96,1024]{2,1,0:T(8,128)}, u32[]{:S(2)}, u32[]{:S(2)}) collective-permute-start(f32[15,96,1024]{2,1,0:T(8,128)} %get-tuple-element.8), channel_id=1, source_target_pairs={{1,0},{2,1},{3,2},{4,3},{5,4},{6,5},{7,6},{8,7},{9,8},{10,9},{11,1... | collective-permute-start | bytes 17694728 | tf_op jit(solution)/shard_map/ppermute | solution.py:19
  1172.0 128.4 %collective-permute-start.6 = (f32[15,96,1024]{2,1,0:T(8,128)}, f32[15,96,1024]{2,1,0:T(8,128)}, u32[]{:S(2)}, u32[]{:S(2)}) collective-permute-start(f32[15,96,1024]{2,1,0:T(8,128)} %get-tuple-element.5), channel_id=1, source_target_pairs={{1,0},{2,1},{3,2},{4,3},{5,4},{6,5},{7,6},{8,7},{9,8},{10,9},{11,1... | collective-permute-start | bytes 17694728 | tf_op jit(solution)/shard_map/ppermute | solution.py:19
  1174.2 126.3 %collective-permute-start.7 = (f32[15,96,1024]{2,1,0:T(8,128)}, f32[15,96,1024]{2,1,0:T(8,128)}, u32[]{:S(2)}, u32[]{:S(2)}) collective-permute-start(f32[15,96,1024]{2,1,0:T(8,128)} %get-tuple-element.6), channel_id=1, source_target_pairs={{0,1},{1,2},{2,3},{3,4},{4,5},{5,6},{6,7},{7,8},{8,9},{9,10},{10,1... | collective-permute-start | bytes 17694728 | tf_op jit(solution)/shard_map/ppermute | solution.py:18
Sparse Core Ops, SparseCore 0:
  602.0 152.2 all-reduce.2
  1364.6 146.7 all-reduce.4
where the time goes:
time: 1540 us; the launch traced here: 1530 us
  waiting for transfers between devices  795 us (52%)
  matrix products  526 us (34%)
  other arithmetic  140 us (9%)
  local copies, waits for them, and re-layouts  28.3 us (2%)
  starting transfers between devices  25.4 us (2%)
    dot_general x4, matrix products, xy_pass(): passed = jnp.dot(volume, mat_x, precision=lax.Precision.HIGHEST)  419 us
    ppermute x4, waiting for transfers between devices, padded_2(): after = lax.ppermute(initial, axis, down)  375 us
    psum x2, waiting for transfers between devices, per_device(): logsum = lax.psum(logs, 'view')  299 us
    log x2, other arithmetic, per_device(): logs = jnp.log(back)  128 us
    ppermute x4, waiting for transfers between devices, padded_2(): before = lax.ppermute(last, axis, up)  121 us
    dot_general x4, matrix products, xy_pass(): jnp.einsum('zyx,yw->zwx', passed, mat_y, precision=lax.Precision.HIGHEST)  107 us
  transfers between devices with their start and end apart: 10, of which 8 were waited for; matrix products, arithmetic and copies ran while one was open for 0% of the time, Pallas kernels for 0%

commit v1 on v0

v1 whole, which is shorter than its diff:
```python
import jax
import jax.numpy as jnp
from jax import lax
from jax.experimental import pallas as pl
from jax.experimental.pallas import tpu as pltpu
from jax.sharding import Mesh
from jax.sharding import PartitionSpec as P

TAPS = 31
ITERS = 2
RADIUS = 15
HALO = 16
VIEWS = 8
ZC = 64
YC = 24
XC = 128
YW = 64
ZW = ZC + 2 * HALO
SLABS = 4
V = ("yh", "x")
S = ("yl", "co")
F32 = jnp.float32
BF16 = jnp.bfloat16
LIMIT = 58 * 1024 * 1024


def split(value):
    hi = value.astype(BF16)
    return hi, (value - hi.astype(F32)).astype(BF16)


def split_constant(value):
    hi = lax.reduce_precision(value, 8, 7)
    return hi.astype(BF16), (value - hi).astype(BF16)


def dot(a, b):
    return jnp.dot(a, b, preferred_element_type=F32)


def banded(taps, offsets):
    result = jnp.zeros((taps.shape[0],) + offsets.shape, F32)
    for t in range(TAPS):
        result = result + jnp.where(offsets == t, taps[:, t, None, None], 0.0)
    return result


def neighbours(axis, size):
    up = [(i, i + 1) for i in range(size - 1)]
    return up, [(j, i) for i, j in up]


def exchange(low, high, axis, size):
    up, down = neighbours(axis, size)
    return lax.ppermute(high, axis, up), lax.ppermute(low, axis, down)


def z_sum(win, taps, v, store):
    @pl.loop(0, ZC // 16)
    def _(b):
        z0 = pl.multiple_of(b * 16, 16)
        for y0 in range(0, YC, 8):
            acc = jnp.zeros((16, 8, XC), F32)
            for t in range(TAPS):
                acc = acc + taps[v, t] * win[pl.ds(z0 + t + 1, 16), y0 : y0 + 8, :]
            store(z0, y0, acc)


def forward_kernel(taps, est, data, wy, wxa, wxb, ratio, left, right, yhi, ylo, win):
    v = pl.program_id(0)

    @pl.when(v == 0)
    def _():
        @pl.loop(0, ZW // 2)
        def _(b):
            both = []
            for k in range(2):
                hi, lo = split(est[2 * b + k])
                stacked = jnp.concatenate([hi, lo, hi], axis=0)
                both.append(dot(wy[...], stacked))
            rows = pl.ds(pl.multiple_of(b * 2 * YC, 16), 2 * YC)
            for u in range(VIEWS):
                pair = jnp.concatenate([o[u * YC : (u + 1) * YC] for o in both], axis=0)
                hi, lo = split(pair)
                yhi[u, rows, :] = hi
                ylo[u, rows, :] = lo

    planes = 16

    @pl.loop(0, ZW // planes)
    def _(b):
        rows = pl.ds(pl.multiple_of(b * planes * YC, 16), planes * YC)
        two = dot(yhi[v, rows, :], wxa[0])
        out = two[:, :XC] + two[:, XC:] + dot(ylo[v, rows, :], wxb[0])
        win[pl.ds(pl.multiple_of(b * planes, planes), planes)] = out.reshape(planes, YC, XC)

    mine = lax.broadcasted_iota(jnp.int32, (16, 8, XC), 2) // HALO == v

    def store(z0, y0, blurred):
        zs = pl.ds(z0, 16)
        value = data[0, zs, y0 : y0 + 8, :] / blurred
        ratio[0, zs, y0 : y0 + 8, :] = value
        first = pltpu.roll(value, HALO * v, 2)
        last = pltpu.roll(value, lax.rem(HALO * v + HALO, XC), 2)
        left[zs, y0 : y0 + 8, :] = jnp.where(mine, first, left[zs, y0 : y0 + 8, :])
        right[zs, y0 : y0 + 8, :] = jnp.where(mine, last, right[zs, y0 : y0 + 8, :])

    z_sum(win, taps, v, store)


def forward(tz, window, data, wy, wxa, wxb):
    one = pl.Buffered(1)
    view = pl.BlockSpec((1, ZC, YC, XC), lambda v: (v, 0, 0, 0))
    pack = pl.BlockSpec((ZC, YC, XC), lambda v: (0, 0, 0))
    shape = jax.ShapeDtypeStruct((ZC, YC, XC), F32)
    return pl.pallas_call(
        forward_kernel,
        name="forward",
        grid=(VIEWS,),
        out_shape=(jax.ShapeDtypeStruct((VIEWS, ZC, YC, XC), F32), shape, shape),
        in_specs=[
            pl.BlockSpec(memory_space=pltpu.SMEM),
            pl.BlockSpec((ZW, YW, 2 * XC), lambda v: (0, 0, 0), pipeline_mode=one),
            view,
            pl.BlockSpec((VIEWS * YC, 3 * YW), lambda v: (0, 0), pipeline_mode=one),
            pl.BlockSpec((1, 2 * XC, 2 * XC), lambda v: (v, 0, 0)),
            pl.BlockSpec((1, 2 * XC, XC), lambda v: (v, 0, 0)),
        ],
        out_specs=(view, pack, pack),
        scratch_shapes=[
            pltpu.VMEM((VIEWS, ZW * YC, 2 * XC), BF16),
            pltpu.VMEM((VIEWS, ZW * YC, 2 * XC), BF16),
            pltpu.VMEM((ZW, YC, XC), F32),
        ],
        compiler_params=pltpu.CompilerParams(vmem_limit_bytes=LIMIT),
    )(tz, window, data, wy, wxa, wxb)


def adjoint_x_kernel(ratio, before, after, wown, wha, whb, out, top, bottom):
    planes = 16

    @pl.loop(0, ZC // planes)
    def _(b):
        zs = pl.ds(pl.multiple_of(b * planes, planes), planes)
        rows = planes * YC
        hi, lo = split(ratio[0, zs].reshape(rows, XC))
        sides = jnp.concatenate([before[zs].reshape(rows, XC), after[zs].reshape(rows, XC)], axis=1)
        shi, slo = split(sides)
        two = dot(jnp.concatenate([hi, lo], axis=1), wown[0]) + dot(shi, wha[0])
        value = two[:, :XC] + two[:, XC:] + dot(slo, whb[0])
        value = value.reshape(planes, YC, XC)
        out[0, zs] = value
        top[0, zs] = value[:, :HALO]
        bottom[0, zs] = value[:, YC - HALO :]


def adjoint_x(ratio, before, after, wown, wha, whb):
    views = ratio.shape[0]
    view = pl.BlockSpec((1, ZC, YC, XC), lambda v: (v, 0, 0, 0))
    pack = pl.BlockSpec((ZC, YC, XC), lambda v: (0, 0, 0))
    edge = pl.BlockSpec((1, ZC, HALO, XC), lambda v: (v, 0, 0, 0))
    edge_shape = jax.ShapeDtypeStruct((views, ZC, HALO, XC), F32)
    return pl.pallas_call(
        adjoint_x_kernel,
        name="adjoint_x",
        grid=(views,),
        out_shape=(jax.ShapeDtypeStruct((views, ZC, YC, XC), F32), edge_shape, edge_shape),
        in_specs=[
            view,
            pack,
            pack,
            pl.BlockSpec((1, 2 * XC, 2 * XC), lambda v: (v, 0, 0)),
            pl.BlockSpec((1, 2 * XC, 2 * XC), lambda v: (v, 0, 0)),
            pl.BlockSpec((1, 2 * XC, XC), lambda v: (v, 0, 0)),
        ],
        out_specs=(view, edge, edge),
        compiler_params=pltpu.CompilerParams(vmem_limit_bytes=LIMIT),
    )(ratio, before, after, wown, wha, whb)


def adjoint_y_kernel(value, before, after, wy, out, low, high):
    empty = jnp.zeros((YW - YC - 2 * HALO, 2 * XC), F32)

    def pair(ref, z):
        return jnp.concatenate([ref[0, z], ref[0, z + 1]], axis=1)

    @pl.loop(0, ZC // 2, unroll=4)
    def _(b):
        z = 2 * b
        rows = jnp.concatenate([pair(before, z), pair(value, z), pair(after, z), empty], axis=0)
        hi, lo = split(rows)
        got = dot(wy[0], jnp.concatenate([hi, lo, hi], axis=0))
        out[0, z] = got[:YC, :XC]
        out[0, z + 1] = got[:YC, XC:]

    low[0] = out[0, :HALO]
    high[0] = out[0, ZC - HALO :]


def adjoint_y(value, before, after, wy):
    views = value.shape[0]
    view = pl.BlockSpec((1, ZC, YC, XC), lambda v: (v, 0, 0, 0))
    edge = pl.BlockSpec((1, ZC, HALO, XC), lambda v: (v, 0, 0, 0))
    face = pl.BlockSpec((1, HALO, YC, XC), lambda v: (v, 0, 0, 0))
    face_shape = jax.ShapeDtypeStruct((views, HALO, YC, XC), F32)
    return pl.pallas_call(
        adjoint_y_kernel,
        name="adjoint_y",
        grid=(views,),
        out_shape=(jax.ShapeDtypeStruct((views, ZC, YC, XC), F32), face_shape, face_shape),
        in_specs=[view, edge, edge, pl.BlockSpec((1, 32, 3 * YW), lambda v: (v, 0, 0))],
        out_specs=(view, face, face),
        compiler_params=pltpu.CompilerParams(vmem_limit_bytes=LIMIT),
    )(value, before, after, wy)


def adjoint_z_kernel(taps, value, before, after, estimate, out, win, total):
    v = pl.program_id(0)
    win[:HALO] = before[0]
    win[HALO : HALO + ZC] = value[0]
    win[HALO + ZC :] = after[0]

    @pl.when(v == 0)
    def _():
        total[...] = jnp.zeros_like(total)

    def store(z0, y0, back):
        total[pl.ds(z0, 16), y0 : y0 + 8, :] += jnp.log(back)

    z_sum(win, taps, v, store)

    @pl.when(v == VIEWS - 1)
    def _():
        out[...] = estimate[...] * jnp.exp(total[...] / VIEWS)


def adjoint_z(tz, value, before, after, estimate):
    view = pl.BlockSpec((1, ZC, YC, XC), lambda v: (v, 0, 0, 0))
    face = pl.BlockSpec((1, HALO, YC, XC), lambda v: (v, 0, 0, 0))
    chunk = pl.BlockSpec((ZC, YC, XC), lambda v: (0, 0, 0))
    return pl.pallas_call(
        adjoint_z_kernel,
        name="adjoint_z",
        grid=(VIEWS,),
        out_shape=jax.ShapeDtypeStruct((ZC, YC, XC), F32),
        in_specs=[pl.BlockSpec(memory_space=pltpu.SMEM), view, face, face, chunk],
        out_specs=chunk,
        scratch_shapes=[pltpu.VMEM((ZW, YC, XC), F32), pltpu.VMEM((ZC, YC, XC), F32)],
        compiler_params=pltpu.CompilerParams(vmem_limit_bytes=LIMIT),
    )(tz, value, before, after, estimate)


def side_columns(right, left):
    lane = lax.broadcasted_iota(jnp.int32, right.shape, right.ndim - 1)
    return jnp.where(lane < XC // 2, right, left)


def add_z(middle):
    before, after = exchange(middle[:HALO], middle[-HALO:], "z", 4)
    return jnp.concatenate([before, middle, after], axis=0)


def first_window(slab):
    padded = jnp.pad(slab, ((0, 0), (HALO, YW - HALO - YC), (XC, XC)))
    c = lax.axis_index(V)
    own, right, left = (lax.dynamic_slice_in_dim(padded, XC * (c + k), XC, axis=2) for k in (1, 2, 0))
    wide = jnp.concatenate([own, side_columns(right, left)], axis=2)
    blocks = jnp.stack([wide[:, YC * k : YC * k + YW] for k in range(SLABS)])
    planes = lax.all_to_all(blocks, S, 0, 0, tiled=True).reshape(ZC, YW, 2 * XC)
    return add_z(planes)


def next_window(chunk):
    left, right = exchange(chunk, chunk, V, VIEWS)
    wide = add_z(jnp.concatenate([chunk, side_columns(right, left)], axis=2))
    before, after = exchange(wide[:, :HALO], wide[:, YC - HALO :], S, SLABS)
    empty = jnp.zeros((ZW, YW - YC - 2 * HALO, 2 * XC), F32)
    return jnp.concatenate([before, wide, after, empty], axis=1)


def matrices(taps):
    def rows(n):
        return jnp.arange(n)[:, None]

    def columns(n):
        return jnp.arange(n)[None, :]

    k = rows(2 * XC)
    x_of = jnp.where(k < XC + XC // 2, k, k - 2 * XC)
    fx_hi, fx_lo = split_constant(banded(taps[:, 0], x_of - columns(XC) + RADIUS))
    fxa = jnp.concatenate([fx_hi, fx_lo], axis=2)
    r = columns(YW) - HALO
    fy_hi, fy_lo = split_constant(banded(taps[:, 1], r - rows(YC) + RADIUS))
    fy = jnp.concatenate([fy_hi, fy_hi, fy_lo], axis=2).reshape(VIEWS * YC, 3 * YW)
    ax_hi, ax_lo = split_constant(banded(taps[:, 0], columns(XC) - rows(XC) + RADIUS))
    own = jnp.concatenate(
        [jnp.concatenate([ax_hi, ax_lo], axis=2), jnp.concatenate([ax_hi, jnp.zeros_like(ax_lo)], axis=2)], axis=1
    )
    lane = rows(XC)
    mine = (lane // HALO)[None] == jnp.arange(VIEWS)[:, None, None]
    sides = [
        jnp.where(mine, banded(taps[:, 0], columns(XC) - at + RADIUS), 0.0)
        for at in (lane % HALO - HALO, lane % HALO + XC)
    ]
    sh_hi, sh_lo = split_constant(jnp.concatenate(sides, axis=1))
    sha = jnp.concatenate([sh_hi, sh_lo], axis=2)
    ay = jnp.pad(banded(taps[:, 1], rows(YC) - r + RADIUS), ((0, 0), (0, 32 - YC), (0, 0)))
    ay_hi, ay_lo = split_constant(ay)
    ay = jnp.concatenate([ay_hi, ay_hi, ay_lo], axis=2)
    return dict(fxa=fxa, fxb=fx_hi, fy=fy, own=own, sha=sha, shb=sh_hi, ay=ay)


def per_device(views_data, estimate, kernels):
    everyone = lax.all_gather(kernels[0], V, axis=0)
    taps = everyone / jnp.sum(everyone, axis=-1, keepdims=True)
    m = matrices(taps)
    tz, tz_flipped = taps[:, 2], taps[:, 2, ::-1]

    window = first_window(estimate)
    depth = views_data.shape[1]
    blocks = views_data[0].reshape(depth, SLABS, YC, VIEWS, XC).transpose(3, 1, 0, 2, 4)
    blocks = blocks.reshape(VIEWS * SLABS, depth, YC, XC)
    data = lax.all_to_all(blocks, V + S, 0, 0, tiled=True).reshape(VIEWS, ZC, YC, XC)
    chunk = window[HALO : HALO + ZC, HALO : HALO + YC, :XC]
    for number in range(ITERS):
        if number:
            window = next_window(chunk)
        ratio, left, right = forward(tz, window, data, m["fy"], m["fxa"], m["fxb"])
        before, after = exchange(left, right, V, VIEWS)
        value, top, bottom = adjoint_x(ratio, before, after, m["own"], m["sha"], m["shb"])
        before, after = exchange(top, bottom, S, SLABS)
        value, low, high = adjoint_y(value, before, after, m["ay"])
        before, after = exchange(low, high, "z", 4)
        chunk = adjoint_z(tz_flipped, value, before, after, chunk)

    parts = chunk.reshape(1, SLABS, depth, YC, XC)
    parts = jnp.broadcast_to(parts, (VIEWS, SLABS, depth, YC, XC)).reshape(VIEWS * SLABS, depth, YC, XC)
    got = lax.all_to_all(parts, V + S, 0, 0, tiled=True).reshape(VIEWS, SLABS, depth, YC, XC)
    return got.transpose(2, 1, 3, 0, 4).reshape(depth, SLABS * YC, VIEWS * XC)


def solution(mesh):
    fine = Mesh(mesh.devices.reshape(2, 4, 4, 2, 2), V + ("z",) + S)
    gz = ("z",) + S
    return jax.shard_map(
        per_device,
        mesh=fine,
        in_specs=(P(V, gz, None, None), P(gz, None, None), P(V, None, None)),
        out_specs=P(gz, None, None),
        check_vma=False,
    )
```

time: 1540 us -> 711 us (0.46)
  waiting for transfers between devices: 795 us -> 256 us
  matrix products: 526 us -> 0 us
  Pallas kernels: 0 us -> 192 us
  blocking collectives: 0 us -> 111 us
  other arithmetic: 140 us -> 34 us
  starting transfers between devices: 25.4 us -> 75 us
    dot_general x8 -> x0, matrix products: 526 us -> none  [the longest x4 419 us: xy_pass(): passed = jnp.dot(volume, mat_x, precision=lax.Precision.HIGHEST)]
    psum x2 -> x0, waiting for transfers between devices: 299 us -> none  [per_device(): logsum = lax.psum(logs, 'view')]
    ppermute x8 -> x20, waiting for transfers between devices: 496 us -> 217 us  [exchange(): return (lax.ppermute(high, axis, up), lax.ppermute(low, axis, down))]
    pallas_call x0 -> x8, Pallas kernels: none -> 192 us  [the longest x2 93.5 us: forward(): pl.pallas_call(forward_kernel, name='forward', grid=(VIEWS,), out_shape=(...]
    log x2 -> x0, other arithmetic: 128 us -> none  [per_device(): logs = jnp.log(back)]
    all_to_all x0 -> x1, blocking collectives: none -> 85 us  [per_device(): lax.all_to_all(parts, V + S, 0, 0, tiled=True)]
    all_to_all x0 -> x2, waiting for transfers between devices: none -> 39.8 us  [the longest x1 28.5 us: per_device(): lax.all_to_all(blocks, V + S, 0, 0, tiled=True).reshape(VIEWS, ZC, YC, XC)]
    ppermute x8 -> x20, starting transfers between devices: 25.4 us -> 60.5 us  [exchange(): return (lax.ppermute(high, axis, up), lax.ppermute(low, axis, down))]
  transfers between devices with their start and end apart: 10 -> 22, of which waited for: 8 -> 22; matrix products, arithmetic and copies ran while one was open for 0% -> 6% of each run, Pallas kernels for 0% -> 0%
where the time goes in v1:
time: 711 us; the launch traced here: 709 us
  waiting for transfers between devices  256 us (36%)
  Pallas kernels  192 us (27%)
  blocking collectives  111 us (16%)
  starting transfers between devices  75 us (11%)
  local copies, waits for them, and re-layouts  39.4 us (6%)
  other arithmetic  34 us (5%)
    ppermute x20, waiting for transfers between devices, exchange(): return (lax.ppermute(high, axis, up), lax.ppermute(low, axis, down))  217 us
    pallas_call x2, Pallas kernels, forward(): pl.pallas_call(forward_kernel, name='forward', grid=(VIEWS,), out_shape=(...  93.5 us
    all_to_all x1, blocking collectives, per_device(): lax.all_to_all(parts, V + S, 0, 0, tiled=True)  85 us
    ppermute x20, starting transfers between devices, exchange(): return (lax.ppermute(high, axis, up), lax.ppermute(low, axis, down))  60.5 us
    pallas_call x2, Pallas kernels, adjoint_z(): pl.pallas_call(adjoint_z_kernel, name='adjoint_z', grid=(VIEWS,), out_sha...  36.2 us
    pallas_call x2, Pallas kernels, adjoint_y(): pl.pallas_call(adjoint_y_kernel, name='adjoint_y', grid=(views,), out_sha...  31.8 us
    pallas_call x2, Pallas kernels, adjoint_x(): pl.pallas_call(adjoint_x_kernel, name='adjoint_x', grid=(views,), out_sha...  30.7 us
    all_to_all x1, waiting for transfers between devices, per_device(): lax.all_to_all(blocks, V + S, 0, 0, tiled=True).reshape(VIEWS, ZC, YC, XC)  28.5 us
  transfers between devices with their start and end apart: 22, of which 22 were waited for; matrix products, arithmetic and copies ran while one was open for 6% of the time, Pallas kernels for 0%

profile of v1, /device:TPU:1, one launch (start us, length us, event | category | flops | bytes accessed | tf_op | source)
XLA Modules:
  0.0 708.6 jit_solution(5972206417907995448)
XLA Ops:
  10.7 26.0 %all_gather.3 = f32[8,3,31]{2,1,0:T(4,128)S(1)} all-gather(f32[1,3,31]{2,1,0:T(4,128)S(1)} %copy.12), channel_id=1, replica_groups=mesh['yh'=2,'x'=4,'z'=4,'yl'=2,'co'=2] {'yh','x'}, dimensions={0}, use_global_device_ids=true | all-gather | bytes 3348 | tf_op jit(solution)/shard_map/all_gather | solution.py:314
  47.1 11.3 %all-to-all-done = f32[4,16,64,256]{3,2,1,0:T(8,128)} async-done(((f32[4,16,64,256]{3,2,1,0:T(8,128)}), f32[4,16,64,256]{3,2,1,0:T(8,128)}, u32[]{:S(2)}, u32[]{:S(2)}) %all-to-all-start) | async-done | bytes 4194336 | tf_op jit(solution)/shard_map/all_to_all | solution.py:269
  58.4 8.0 %all-to-all-start.1 = ((f32[32,16,24,128]{3,2,1,0:T(8,128)}), f32[32,16,24,128]{3,2,1,0:T(8,128)}, u32[]{:S(2)}, u32[]{:S(2)}) async-start(f32[32,16,24,128]{3,2,1,0:T(8,128)} %bitcast.129), calls=%async_computation.1 | async-start | bytes 12582912 | tf_op jit(solution)/shard_map/all_to_all | solution.py:323
  92.5 15.7 %collective-permute-done = f32[16,64,256]{2,1,0:T(8,128)S(1)} collective-permute-done((f32[16,64,256]{2,1,0:T(8,128)S(1)}, f32[16,64,256]{2,1,0:T(8,128)S(1)}, u32[]{:S(2)}, u32[]{:S(2)}) %collective-permute-start) | collective-permute-done | bytes 1048608 | tf_op jit(solution)/shard_map/ppermute | solution.py:55
  118.3 28.5 %all-to-all-done.1 = f32[32,16,24,128]{3,2,1,0:T(8,128)} async-done(((f32[32,16,24,128]{3,2,1,0:T(8,128)}), f32[32,16,24,128]{3,2,1,0:T(8,128)}, u32[]{:S(2)}, u32[]{:S(2)}) %all-to-all-start.1) | async-done | bytes 6291488 | tf_op jit(solution)/shard_map/all_to_all | solution.py:323
  146.8 46.7 %forward.2 = (f32[8,64,24,128]{3,2,1,0:T(8,128)}, f32[64,24,128]{2,1,0:T(8,128)}, f32[64,24,128]{2,1,0:T(8,128)}) custom-call(f32[8,31]{1,0:T(8,128)} %get-tuple-element.126.taps, f32[96,64,256]{2,1,0:T(8,128)} %pad_maximum_fusion.est, f32[8,64,24,128]{3,2,1,0:T(8,128)} %bitcast.11.data, bf16[192,192]{1,0:T(8,128)(2,1)} %pad_maximum_fusion.10.wy, ...), custom_call_target="tpu_custom_call" | custom-call | tf_op jit(solution)/shard_map/forward/pallas_call | solution.py:116
  193.5 14.7 %collective-permute-start.2 = (f32[64,24,128]{2,1,0:T(8,128)}, f32[64,24,128]{2,1,0:T(8,128)S(1)}, u32[]{:S(2)}, u32[]{:S(2)}) collective-permute-start(f32[64,24,128]{2,1,0:T(8,128)} %get-tuple-element.24), channel_id=1, source_target_pairs={{0,16},{16,32},{32,48},{48,64},{64,80},{80,96},{96,112},{1,17},{17... | collective-permute-start | bytes 2359304 | tf_op jit(solution)/shard_map/ppermute | solution.py:55
  213.0 11.3 %collective-permute-done.2.before = f32[64,24,128]{2,1,0:T(8,128)S(1)} collective-permute-done((f32[64,24,128]{2,1,0:T(8,128)}, f32[64,24,128]{2,1,0:T(8,128)S(1)}, u32[]{:S(2)}, u32[]{:S(2)}) %collective-permute-start.2) | collective-permute-done | bytes 786464 | tf_op jit(solution)/shard_map/ppermute | solution.py:55
  229.0 15.4 %adjoint_x.2 = (f32[8,64,24,128]{3,2,1,0:T(8,128)}, f32[8,64,16,128]{3,2,1,0:T(8,128)}, f32[8,64,16,128]{3,2,1,0:T(8,128)}) custom-call(f32[8,64,24,128]{3,2,1,0:T(8,128)} %get-tuple-element.23.ratio, f32[64,24,128]{2,1,0:T(8,128)} %copy-done.9, f32[64,24,128]{2,1,0:T(8,128)} %copy-done.10, bf16[8,256,256]{2,1,0:T(8,128)(2,1)} %fusion.4.wown, ...), custom_call_target="tpu_custom_call" | custom-call | tf_op jit(solution)/shard_map/adjoint_x/pallas_call | solution.py:163
  251.2 40.8 %collective-permute-done.4.before = f32[8,64,16,128]{3,2,1,0:T(8,128)S(1)} collective-permute-done((f32[8,64,16,128]{3,2,1,0:T(8,128)}, f32[8,64,16,128]{3,2,1,0:T(8,128)S(1)}, u32[]{:S(2)}, u32[]{:S(2)}) %collective-permute-start.4) | collective-permute-done | bytes 4194336 | tf_op jit(solution)/shard_map/ppermute | solution.py:55
  296.6 15.9 %adjoint_y.2 = (f32[8,64,24,128]{3,2,1,0:T(8,128)}, f32[8,16,24,128]{3,2,1,0:T(8,128)}, f32[8,16,24,128]{3,2,1,0:T(8,128)}) custom-call(f32[8,64,24,128]{3,2,1,0:T(8,128)} %get-tuple-element.26.value, f32[8,64,16,128]{3,2,1,0:T(8,128)} %copy-done.3, f32[8,64,16,128]{3,2,1,0:T(8,128)} %collective-permute-done.5.after, bf16[8,32,192]{2,1,0:T(8,128)(2,1)} %pad_maximum_fusion.9.wy), custom_call_target="tpu_custom_call" | custom-call | tf_op jit(solution)/shard_map/adjoint_y/pallas_call | solution.py:206
  320.1 13.5 %collective-permute-done.6.before = f32[8,16,24,128]{3,2,1,0:T(8,128)S(1)} collective-permute-done((f32[8,16,24,128]{3,2,1,0:T(8,128)}, f32[8,16,24,128]{3,2,1,0:T(8,128)S(1)}, u32[]{:S(2)}, u32[]{:S(2)}) %collective-permute-start.6) | collective-permute-done | bytes 1572896 | tf_op jit(solution)/shard_map/ppermute | solution.py:55
  338.7 18.1 %adjoint_z.2.estimate = f32[64,24,128]{2,1,0:T(8,128)} custom-call(f32[8,31]{1,0:T(8,128)} %bitcast.135, f32[8,64,24,128]{3,2,1,0:T(8,128)} %get-tuple-element.29.value, f32[8,16,24,128]{3,2,1,0:T(8,128)} %copy-done.5, f32[8,16,24,128]{3,2,1,0:T(8,128)} %copy-done.6, f32[64,24,128]{2,1,0:T(8,128)} %slice.452.estimate), custom_call_target="tpu_custom_call" | custom-call | tf_op jit(solution)/shard_map/adjoint_z/pallas_call | solution.py:241
  360.5 7.9 %collective-permute-done.9 = f32[64,24,128]{2,1,0:T(8,128)S(1)} collective-permute-done((f32[64,24,128]{2,1,0:T(8,128)}, f32[64,24,128]{2,1,0:T(8,128)S(1)}, u32[]{:S(2)}, u32[]{:S(2)}) %collective-permute-start.9) | collective-permute-done | bytes 786464 | tf_op jit(solution)/shard_map/ppermute | solution.py:55
  394.1 15.1 %collective-permute-done.12 = f32[96,16,256]{2,1,0:T(8,128)S(1)} collective-permute-done((f32[96,16,256]{2,1,0:T(8,128)S(1)}, f32[96,16,256]{2,1,0:T(8,128)S(1)}, u32[]{:S(2)}, u32[]{:S(2)}) %collective-permute-start.12) | collective-permute-done | bytes 1572896 | tf_op jit(solution)/shard_map/ppermute | solution.py:55
  417.5 46.8 %forward.3 = (f32[8,64,24,128]{3,2,1,0:T(8,128)}, f32[64,24,128]{2,1,0:T(8,128)}, f32[64,24,128]{2,1,0:T(8,128)}) custom-call(f32[8,31]{1,0:T(8,128)} %get-tuple-element.126.taps, f32[96,64,256]{2,1,0:T(8,128)} %maximum_maximum_fusion.est, f32[8,64,24,128]{3,2,1,0:T(8,128)} %bitcast.11.data, bf16[192,192]{1,0:T(8,128)(2,1)} %pad_maximum_fusion.10.wy, ...), custom_call_target="tpu_custom_call" | custom-call | tf_op jit(solution)/shard_map/forward/pallas_call | solution.py:116
  466.9 7.9 %collective-permute-done.14.before = f32[64,24,128]{2,1,0:T(8,128)S(1)} collective-permute-done((f32[64,24,128]{2,1,0:T(8,128)}, f32[64,24,128]{2,1,0:T(8,128)S(1)}, u32[]{:S(2)}, u32[]{:S(2)}) %collective-permute-start.14) | collective-permute-done | bytes 786464 | tf_op jit(solution)/shard_map/ppermute | solution.py:55
  479.7 15.3 %adjoint_x.3 = (f32[8,64,24,128]{3,2,1,0:T(8,128)}, f32[8,64,16,128]{3,2,1,0:T(8,128)}, f32[8,64,16,128]{3,2,1,0:T(8,128)}) custom-call(f32[8,64,24,128]{3,2,1,0:T(8,128)} %get-tuple-element.32.ratio, f32[64,24,128]{2,1,0:T(8,128)} %copy-done.11, f32[64,24,128]{2,1,0:T(8,128)} %copy-done.12, bf16[8,256,256]{2,1,0:T(8,128)(2,1)} %fusion.4.wown, ...), custom_call_target="tpu_custom_call" | custom-call | tf_op jit(solution)/shard_map/adjoint_x/pallas_call | solution.py:163
  499.9 43.8 %collective-permute-done.16.before = f32[8,64,16,128]{3,2,1,0:T(8,128)S(1)} collective-permute-done((f32[8,64,16,128]{3,2,1,0:T(8,128)}, f32[8,64,16,128]{3,2,1,0:T(8,128)S(1)}, u32[]{:S(2)}, u32[]{:S(2)}) %collective-permute-start.16) | collective-permute-done | bytes 4194336 | tf_op jit(solution)/shard_map/ppermute | solution.py:55
  548.3 15.9 %adjoint_y.3 = (f32[8,64,24,128]{3,2,1,0:T(8,128)}, f32[8,16,24,128]{3,2,1,0:T(8,128)}, f32[8,16,24,128]{3,2,1,0:T(8,128)}) custom-call(f32[8,64,24,128]{3,2,1,0:T(8,128)} %get-tuple-element.35.value, f32[8,64,16,128]{3,2,1,0:T(8,128)} %copy-done.4, f32[8,64,16,128]{3,2,1,0:T(8,128)} %collective-permute-done.17.after, bf16[8,32,192]{2,1,0:T(8,128)(2,1)} %pad_maximum_fusion.9.wy), custom_call_target="tpu_custom_call" | custom-call | tf_op jit(solution)/shard_map/adjoint_y/pallas_call | solution.py:206
  569.0 16.3 %collective-permute-done.18.before = f32[8,16,24,128]{3,2,1,0:T(8,128)S(1)} collective-permute-done((f32[8,16,24,128]{3,2,1,0:T(8,128)}, f32[8,16,24,128]{3,2,1,0:T(8,128)S(1)}, u32[]{:S(2)}, u32[]{:S(2)}) %collective-permute-start.18) | collective-permute-done | bytes 1572896 | tf_op jit(solution)/shard_map/ppermute | solution.py:55
  590.2 18.1 %adjoint_z.3 = f32[64,24,128]{2,1,0:T(8,128)} custom-call(f32[8,31]{1,0:T(8,128)} %bitcast.136, f32[8,64,24,128]{3,2,1,0:T(8,128)} %get-tuple-element.38.value, f32[8,16,24,128]{3,2,1,0:T(8,128)} %copy-done.7, f32[8,16,24,128]{3,2,1,0:T(8,128)} %copy-done.8, f32[64,24,128]{2,1,0:T(8,128)} %adjoint_z.2.estimate), custom_call_target="tpu_custom_call" | custom-call | tf_op jit(solution)/shard_map/adjoint_z/pallas_call | solution.py:241
  610.2 85.0 %all_to_all.15 = f32[32,16,24,128]{3,2,1,0:T(8,128)S(1)} all-to-all(f32[32,16,24,128]{3,2,1,0:T(8,128)S(1)} %bitcast.130), channel_id=1, replica_groups=mesh['yh'=2,'x'=4,'z'=4,'yl'=2,'co'=2] {'yh','x','yl','co'}, dimensions={0} | all-to-all | bytes 12582912 | tf_op jit(solution)/shard_map/all_to_all | solution.py:338
  701.5 7.1 reshape.379
  (190 shorter events, 163.1 us)
Async XLA Ops:
  4.2 54.1 %all-to-all-start = ((f32[4,16,64,256]{3,2,1,0:T(8,128)}), f32[4,16,64,256]{3,2,1,0:T(8,128)}, u32[]{:S(2)}, u32[]{:S(2)}) async-start(f32[4,16,64,256]{3,2,1,0:T(8,128)} %pad_maximum_fusion.1), calls=%async_computation | async-start | bytes 8388608 | tf_op jit(solution)/shard_map/all_to_all | solution.py:269
  58.4 88.4 %all-to-all-start.1 = ((f32[32,16,24,128]{3,2,1,0:T(8,128)}), f32[32,16,24,128]{3,2,1,0:T(8,128)}, u32[]{:S(2)}, u32[]{:S(2)}) async-start(f32[32,16,24,128]{3,2,1,0:T(8,128)} %bitcast.129), calls=%async_computation.1 | async-start | bytes 12582912 | tf_op jit(solution)/shard_map/all_to_all | solution.py:323
  82.7 25.6 %collective-permute-start = (f32[16,64,256]{2,1,0:T(8,128)S(1)}, f32[16,64,256]{2,1,0:T(8,128)S(1)}, u32[]{:S(2)}, u32[]{:S(2)}) collective-permute-start(f32[16,64,256]{2,1,0:T(8,128)S(1)} %get-tuple-element.111), channel_id=1, source_target_pairs={{0,4},{4,8},{8,12},{1,5},{5,9},{9,13},{2,6},{6,10},{10,14},{3,7},{... | collective-permute-start | bytes 3145736 | tf_op jit(solution)/shard_map/ppermute | solution.py:55
  86.3 26.2 %collective-permute-start.1 = (f32[16,64,256]{2,1,0:T(8,128)S(1)}, f32[16,64,256]{2,1,0:T(8,128)S(1)}, u32[]{:S(2)}, u32[]{:S(2)}) collective-permute-start(f32[16,64,256]{2,1,0:T(8,128)S(1)} %get-tuple-element.112), channel_id=1, source_target_pairs={{4,0},{8,4},{12,8},{5,1},{9,5},{13,9},{6,2},{10,6},{14,10},{7,3},{... | collective-permute-start | bytes 3145736 | tf_op jit(solution)/shard_map/ppermute | solution.py:55
  91.3 27.0 %copy-start.2 = (bf16[8,256,128]{2,1,0:T(8,128)(2,1)}, bf16[8,256,128]{2,1,0:T(8,128)(2,1)S(1)}, u32[]{:S(2)}) copy-start(bf16[8,256,128]{2,1,0:T(8,128)(2,1)S(1)} %get-tuple-element.105.wxb) | copy-start | bytes 1572868
  193.5 30.9 %collective-permute-start.2 = (f32[64,24,128]{2,1,0:T(8,128)}, f32[64,24,128]{2,1,0:T(8,128)S(1)}, u32[]{:S(2)}, u32[]{:S(2)}) collective-permute-start(f32[64,24,128]{2,1,0:T(8,128)} %get-tuple-element.24), channel_id=1, source_target_pairs={{0,16},{16,32},{32,48},{48,64},{64,80},{80,96},{96,112},{1,17},{17... | collective-permute-start | bytes 2359304 | tf_op jit(solution)/shard_map/ppermute | solution.py:55
  208.1 19.9 %collective-permute-start.3 = (f32[64,24,128]{2,1,0:T(8,128)}, f32[64,24,128]{2,1,0:T(8,128)S(1)}, u32[]{:S(2)}, u32[]{:S(2)}) collective-permute-start(f32[64,24,128]{2,1,0:T(8,128)} %get-tuple-element.25), channel_id=1, source_target_pairs={{16,0},{32,16},{48,32},{64,48},{80,64},{96,80},{112,96},{17,1},{33... | collective-permute-start | bytes 2359304 | tf_op jit(solution)/shard_map/ppermute | solution.py:55
  244.3 47.7 %collective-permute-start.4 = (f32[8,64,16,128]{3,2,1,0:T(8,128)}, f32[8,64,16,128]{3,2,1,0:T(8,128)S(1)}, u32[]{:S(2)}, u32[]{:S(2)}) collective-permute-start(f32[8,64,16,128]{3,2,1,0:T(8,128)} %get-tuple-element.27), channel_id=1, source_target_pairs={{0,1},{1,2},{2,3},{4,5},{5,6},{6,7},{8,9},{9,10},{10,11},{12,13},{... | collective-permute-start | bytes 12582920 | tf_op jit(solution)/shard_map/ppermute | solution.py:55
  246.2 50.3 %collective-permute-start.5 = (f32[8,64,16,128]{3,2,1,0:T(8,128)}, f32[8,64,16,128]{3,2,1,0:T(8,128)}, u32[]{:S(2)}, u32[]{:S(2)}) collective-permute-start(f32[8,64,16,128]{3,2,1,0:T(8,128)} %get-tuple-element.28), channel_id=1, source_target_pairs={{1,0},{2,1},{3,2},{5,4},{6,5},{7,6},{9,8},{10,9},{11,10},{13,12},{... | collective-permute-start | bytes 12582920 | tf_op jit(solution)/shard_map/ppermute | solution.py:55
  312.4 21.2 %collective-permute-start.6 = (f32[8,16,24,128]{3,2,1,0:T(8,128)}, f32[8,16,24,128]{3,2,1,0:T(8,128)S(1)}, u32[]{:S(2)}, u32[]{:S(2)}) collective-permute-start(f32[8,16,24,128]{3,2,1,0:T(8,128)} %get-tuple-element.30), channel_id=1, source_target_pairs={{0,4},{4,8},{8,12},{1,5},{5,9},{9,13},{2,6},{6,10},{10,14},{3,7},{... | collective-permute-start | bytes 4718600 | tf_op jit(solution)/shard_map/ppermute | solution.py:55
  316.1 21.4 %collective-permute-start.7 = (f32[8,16,24,128]{3,2,1,0:T(8,128)}, f32[8,16,24,128]{3,2,1,0:T(8,128)S(1)}, u32[]{:S(2)}, u32[]{:S(2)}) collective-permute-start(f32[8,16,24,128]{3,2,1,0:T(8,128)} %get-tuple-element.31), channel_id=1, source_target_pairs={{4,0},{8,4},{12,8},{5,1},{9,5},{13,9},{6,2},{10,6},{14,10},{7,3},{... | collective-permute-start | bytes 4718600 | tf_op jit(solution)/shard_map/ppermute | solution.py:55
  356.8 28.4 %copy-start = (f32[64,24,128]{2,1,0:T(8,128)S(1)}, f32[64,24,128]{2,1,0:T(8,128)}, u32[]{:S(2)}) copy-start(f32[64,24,128]{2,1,0:T(8,128)} %adjoint_z.2.estimate) | copy-start | bytes 2359300
  356.8 11.5 %collective-permute-start.9 = (f32[64,24,128]{2,1,0:T(8,128)}, f32[64,24,128]{2,1,0:T(8,128)S(1)}, u32[]{:S(2)}, u32[]{:S(2)}) collective-permute-start(f32[64,24,128]{2,1,0:T(8,128)} %adjoint_z.2.estimate), channel_id=1, source_target_pairs={{0,16},{16,32},{32,48},{48,64},{64,80},{80,96},{96,112},{1,17},{17... | collective-permute-start | bytes 2359304 | tf_op jit(solution)/shard_map/ppermute | solution.py:55
  359.2 12.9 %collective-permute-start.8 = (f32[64,24,128]{2,1,0:T(8,128)}, f32[64,24,128]{2,1,0:T(8,128)S(1)}, u32[]{:S(2)}, u32[]{:S(2)}) collective-permute-start(f32[64,24,128]{2,1,0:T(8,128)} %adjoint_z.2.estimate), channel_id=1, source_target_pairs={{16,0},{32,16},{48,32},{64,48},{80,64},{96,80},{112,96},{17,1},{33... | collective-permute-start | bytes 2359304 | tf_op jit(solution)/shard_map/ppermute | solution.py:55
  373.3 8.1 %collective-permute-start.10 = (f32[16,24,256]{2,1,0:T(8,128)S(1)}, f32[16,24,256]{2,1,0:T(8,128)S(1)}, u32[]{:S(2)}, u32[]{:S(2)}) collective-permute-start(f32[16,24,256]{2,1,0:T(8,128)S(1)} %get-tuple-element.119), channel_id=1, source_target_pairs={{0,4},{4,8},{8,12},{1,5},{5,9},{9,13},{2,6},{6,10},{10,14},{3,7},{... | collective-permute-start | bytes 1179656 | tf_op jit(solution)/shard_map/ppermute | solution.py:55
  376.7 8.5 %collective-permute-start.11 = (f32[16,24,256]{2,1,0:T(8,128)S(1)}, f32[16,24,256]{2,1,0:T(8,128)S(1)}, u32[]{:S(2)}, u32[]{:S(2)}) collective-permute-start(f32[16,24,256]{2,1,0:T(8,128)S(1)} %get-tuple-element.120), channel_id=1, source_target_pairs={{4,0},{8,4},{12,8},{5,1},{9,5},{13,9},{6,2},{10,6},{14,10},{7,3},{... | collective-permute-start | bytes 1179656 | tf_op jit(solution)/shard_map/ppermute | solution.py:55
  385.6 23.5 %collective-permute-start.12 = (f32[96,16,256]{2,1,0:T(8,128)S(1)}, f32[96,16,256]{2,1,0:T(8,128)S(1)}, u32[]{:S(2)}, u32[]{:S(2)}) collective-permute-start(f32[96,16,256]{2,1,0:T(8,128)S(1)} %get-tuple-element.113), channel_id=1, source_target_pairs={{0,1},{1,2},{2,3},{4,5},{5,6},{6,7},{8,9},{9,10},{10,11},{12,13},{... | collective-permute-start | bytes 4718600 | tf_op jit(solution)/shard_map/ppermute | solution.py:55
  392.0 21.7 %collective-permute-start.13 = (f32[96,16,256]{2,1,0:T(8,128)S(1)}, f32[96,16,256]{2,1,0:T(8,128)S(1)}, u32[]{:S(2)}, u32[]{:S(2)}) collective-permute-start(f32[96,16,256]{2,1,0:T(8,128)S(1)} %get-tuple-element.114), channel_id=1, source_target_pairs={{1,0},{2,1},{3,2},{5,4},{6,5},{7,6},{9,8},{10,9},{11,10},{13,12},{... | collective-permute-start | bytes 4718600 | tf_op jit(solution)/shard_map/ppermute | solution.py:55
  464.2 10.6 %collective-permute-start.14 = (f32[64,24,128]{2,1,0:T(8,128)}, f32[64,24,128]{2,1,0:T(8,128)S(1)}, u32[]{:S(2)}, u32[]{:S(2)}) collective-permute-start(f32[64,24,128]{2,1,0:T(8,128)} %get-tuple-element.33), channel_id=1, source_target_pairs={{0,16},{16,32},{32,48},{48,64},{64,80},{80,96},{96,112},{1,17},{17... | collective-permute-start | bytes 2359304 | tf_op jit(solution)/shard_map/ppermute | solution.py:55
  465.6 13.2 %collective-permute-start.15 = (f32[64,24,128]{2,1,0:T(8,128)}, f32[64,24,128]{2,1,0:T(8,128)S(1)}, u32[]{:S(2)}, u32[]{:S(2)}) collective-permute-start(f32[64,24,128]{2,1,0:T(8,128)} %get-tuple-element.34), channel_id=1, source_target_pairs={{16,0},{32,16},{48,32},{64,48},{80,64},{96,80},{112,96},{17,1},{33... | collective-permute-start | bytes 2359304 | tf_op jit(solution)/shard_map/ppermute | solution.py:55
  495.0 48.7 %collective-permute-start.16 = (f32[8,64,16,128]{3,2,1,0:T(8,128)}, f32[8,64,16,128]{3,2,1,0:T(8,128)S(1)}, u32[]{:S(2)}, u32[]{:S(2)}) collective-permute-start(f32[8,64,16,128]{3,2,1,0:T(8,128)} %get-tuple-element.36), channel_id=1, source_target_pairs={{0,1},{1,2},{2,3},{4,5},{5,6},{6,7},{8,9},{9,10},{10,11},{12,13},{... | collective-permute-start | bytes 12582920 | tf_op jit(solution)/shard_map/ppermute | solution.py:55
  498.0 50.3 %collective-permute-start.17 = (f32[8,64,16,128]{3,2,1,0:T(8,128)}, f32[8,64,16,128]{3,2,1,0:T(8,128)}, u32[]{:S(2)}, u32[]{:S(2)}) collective-permute-start(f32[8,64,16,128]{3,2,1,0:T(8,128)} %get-tuple-element.37), channel_id=1, source_target_pairs={{1,0},{2,1},{3,2},{5,4},{6,5},{7,6},{9,8},{10,9},{11,10},{13,12},{... | collective-permute-start | bytes 12582920 | tf_op jit(solution)/shard_map/ppermute | solution.py:55
  564.2 21.0 %collective-permute-start.18 = (f32[8,16,24,128]{3,2,1,0:T(8,128)}, f32[8,16,24,128]{3,2,1,0:T(8,128)S(1)}, u32[]{:S(2)}, u32[]{:S(2)}) collective-permute-start(f32[8,16,24,128]{3,2,1,0:T(8,128)} %get-tuple-element.39), channel_id=1, source_target_pairs={{0,4},{4,8},{8,12},{1,5},{5,9},{9,13},{2,6},{6,10},{10,14},{3,7},{... | collective-permute-start | bytes 4718600 | tf_op jit(solution)/shard_map/ppermute | solution.py:55
  567.7 21.4 %collective-permute-start.19 = (f32[8,16,24,128]{3,2,1,0:T(8,128)}, f32[8,16,24,128]{3,2,1,0:T(8,128)S(1)}, u32[]{:S(2)}, u32[]{:S(2)}) collective-permute-start(f32[8,16,24,128]{3,2,1,0:T(8,128)} %get-tuple-element.40), channel_id=1, source_target_pairs={{4,0},{8,4},{12,8},{5,1},{9,5},{13,9},{6,2},{10,6},{14,10},{7,3},{... | collective-permute-start | bytes 4718600 | tf_op jit(solution)/shard_map/ppermute | solution.py:55
  (12 other events, 47.6 us)

commit v2 on v1

v2 whole, which is shorter than its diff:
```python
import jax
import jax.numpy as jnp
from jax import lax
from jax.experimental import pallas as pl
from jax.experimental.pallas import tpu as pltpu
from jax.sharding import Mesh
from jax.sharding import PartitionSpec as P

TAPS = 31
ITERS = 2
RADIUS = 15
HALO = 16
VIEWS = 8
GROUP = 4
ZC = 64
YC = 24
XC = 128
YW = YC + 2 * HALO
YK = 64
ZW = ZC + 2 * HALO
SLABS = 4
DEPTH = ZC // SLABS
PACKED = DEPTH // 4
V = ("yh", "x")
S = ("yl", "co")
F32 = jnp.float32
BF16 = jnp.bfloat16
LIMIT = 56 * 1024 * 1024


def params(us):
    cost = pl.CostEstimate(flops=int(us * 1e9), bytes_accessed=int(us * 2e6), transcendentals=0)
    return dict(compiler_params=pltpu.CompilerParams(vmem_limit_bytes=LIMIT), cost_estimate=cost)


def split(value):
    hi = value.astype(BF16)
    return hi, (value - hi.astype(F32)).astype(BF16)


def split_constant(value):
    hi = lax.reduce_precision(value, 8, 7)
    return hi.astype(BF16), (value - hi).astype(BF16)


def dot(a, b):
    return jnp.dot(a, b, preferred_element_type=F32)


def banded(taps, offsets):
    result = jnp.zeros((taps.shape[0],) + offsets.shape, F32)
    for t in range(TAPS):
        result = result + jnp.where(offsets == t, taps[:, t, None, None], 0.0)
    return result


def exchange(low, high, axis, size):
    up = [(i, i + 1) for i in range(size - 1)]
    down = [(j, i) for i, j in up]
    return lax.ppermute(high, axis, up), lax.ppermute(low, axis, down)


def z_sum(win, taps, v, store):
    @pl.loop(0, ZC // 16)
    def _(b):
        z0 = pl.multiple_of(b * 16, 16)
        for y0 in range(0, YC, 8):
            acc = jnp.zeros((16, 8, XC), F32)
            for t in range(TAPS):
                acc = acc + taps[v, t] * win[pl.ds(z0 + t + 1, 16), y0 : y0 + 8, :]
            store(z0, y0, acc)


def forward_kernel(taps, est, data, wy, wown, wpack, ratio, left, right, yown, ypack, win):
    v = pl.program_id(0)

    @pl.when(v == 0)
    def _():
        empty = jnp.zeros((YK - YW, 2 * XC), F32)

        @pl.loop(0, SLABS + 2)
        def _(b):
            for i in range((DEPTH + PACKED) // 2):
                planes = jnp.concatenate([est[b, 2 * i], est[b, 2 * i + 1]], axis=1)
                hi, lo = split(jnp.concatenate([planes, empty], axis=0))
                got = dot(wy[...], jnp.concatenate([hi, lo, hi], axis=0))
                if i < DEPTH // 2:
                    dest, first = yown, b * DEPTH * YC + 2 * i * YC
                else:
                    dest, first = ypack, b * PACKED * YC + 2 * (i - DEPTH // 2) * YC
                rows = pl.ds(pl.multiple_of(first, 16), 2 * YC)
                for u in range(GROUP):
                    one = got[u * YC : (u + 1) * YC]
                    hi, lo = split(jnp.concatenate([one[:, :XC], one[:, XC:]], axis=0))
                    dest[u, rows, :] = jnp.concatenate([hi, lo], axis=1)

    step = 4

    @pl.loop(0, ZW // 4 // step)
    def _(b):
        rows = pl.ds(pl.multiple_of(b * step * 4 * YC, 16), step * 4 * YC)
        two = dot(yown[v, rows, :], wown[0])
        own = (two[:, :XC] + two[:, XC:]).reshape(step, 4, YC, XC)
        packed = ypack[v, pl.ds(pl.multiple_of(b * step * YC, 16), step * YC), :]
        for j in range(4):
            two = dot(packed, wpack[0, j])
            out = own[:, j] + (two[:, :XC] + two[:, XC:]).reshape(step, YC, XC)
            for q in range(step):
                win[b * step * 4 + q * 4 + j] = out[q]

    group = lax.broadcasted_iota(jnp.int32, (16, 8, XC), 2) // HALO

    def store(z0, y0, blurred):
        zs = pl.ds(z0, 16)
        value = data[0, zs, y0 : y0 + 8, :] / blurred
        ratio[0, zs, y0 : y0 + 8, :] = value
        half = z0 // (ZC // 2)
        at = GROUP * half + v
        zs = pl.ds(z0 - half * (ZC // 2), 16)
        first = pltpu.roll(value, HALO * at, 2)
        last = pltpu.roll(value, lax.rem(HALO * at + HALO, XC), 2)
        left[zs, y0 : y0 + 8, :] = jnp.where(group == at, first, left[zs, y0 : y0 + 8, :])
        right[zs, y0 : y0 + 8, :] = jnp.where(group == at, last, right[zs, y0 : y0 + 8, :])

    z_sum(win, taps, v, store)


def forward(g, tz, window, data, wy, wown, wpack):
    view = pl.BlockSpec((1, ZC, YC, XC), lambda v: (v + g * GROUP, 0, 0, 0))
    out = pl.BlockSpec((1, ZC, YC, XC), lambda v: (v, 0, 0, 0))
    pack = pl.BlockSpec((ZC // 2, YC, XC), lambda v: (0, 0, 0))
    shape = jax.ShapeDtypeStruct((ZC // 2, YC, XC), F32)
    return pl.pallas_call(
        forward_kernel,
        name="forward",
        grid=(GROUP,),
        out_shape=(jax.ShapeDtypeStruct((GROUP, ZC, YC, XC), F32), shape, shape),
        in_specs=[
            pl.BlockSpec(memory_space=pltpu.SMEM),
            pl.BlockSpec(window.shape, lambda v: (0, 0, 0, 0), pipeline_mode=pl.Buffered(1)),
            view,
            pl.BlockSpec((GROUP * YC, 3 * YK), lambda v: (g, 0), pipeline_mode=pl.Buffered(1)),
            pl.BlockSpec((1, 2 * XC, 2 * XC), lambda v: (v + g * GROUP, 0, 0)),
            pl.BlockSpec((1, 4, 2 * XC, 2 * XC), lambda v: (v + g * GROUP, 0, 0, 0)),
        ],
        out_specs=(out, pack, pack),
        scratch_shapes=[
            pltpu.VMEM((GROUP, ZW * YC, 2 * XC), BF16),
            pltpu.VMEM((GROUP, ZW // 4 * YC, 2 * XC), BF16),
            pltpu.VMEM((ZW, YC, XC), F32),
        ],
        **params(24),
    )(tz[g * GROUP : (g + 1) * GROUP], window, data, wy, wown, wpack)


def adjoint_x_kernel(ratio, before, after, wown, wha, whb, out, top, bottom):
    planes = 16

    @pl.loop(0, ZC // planes)
    def _(b):
        rows = planes * YC
        half = b // 2
        zs = pl.ds(pl.multiple_of(b * planes, planes), planes)
        hs = pl.ds(pl.multiple_of((b - 2 * half) * planes, planes), planes)
        hi, lo = split(ratio[0, zs].reshape(rows, XC))
        sides = jnp.concatenate([before[hs].reshape(rows, XC), after[hs].reshape(rows, XC)], axis=1)
        shi, slo = split(sides)
        two = dot(jnp.concatenate([hi, lo], axis=1), wown[0]) + dot(shi, wha[0, half])
        value = two[:, :XC] + two[:, XC:] + dot(slo, whb[0, half])
        value = value.reshape(planes, YC, XC)
        out[0, zs] = value
        top[0, zs] = value[:, :HALO]
        bottom[0, zs] = value[:, YC - HALO :]


def adjoint_x(g, ratio, before, after, wown, wha, whb):
    view = pl.BlockSpec((1, ZC, YC, XC), lambda v: (v, 0, 0, 0))
    pack = pl.BlockSpec((ZC // 2, YC, XC), lambda v: (0, 0, 0))
    edge = pl.BlockSpec((1, ZC, HALO, XC), lambda v: (v, 0, 0, 0))
    edge_shape = jax.ShapeDtypeStruct((GROUP, ZC, HALO, XC), F32)
    return pl.pallas_call(
        adjoint_x_kernel,
        name="adjoint_x",
        grid=(GROUP,),
        out_shape=(jax.ShapeDtypeStruct((GROUP, ZC, YC, XC), F32), edge_shape, edge_shape),
        in_specs=[
            view,
            pack,
            pack,
            pl.BlockSpec((1, 2 * XC, 2 * XC), lambda v: (v + g * GROUP, 0, 0)),
            pl.BlockSpec((1, 2, 2 * XC, 2 * XC), lambda v: (v + g * GROUP, 0, 0, 0)),
            pl.BlockSpec((1, 2, 2 * XC, XC), lambda v: (v + g * GROUP, 0, 0, 0)),
        ],
        out_specs=(view, edge, edge),
        **params(8),
    )(ratio, before, after, wown, wha, whb)


def adjoint_y_kernel(value, before, after, wy, out, low, high):
    empty = jnp.zeros((YK - YW, 2 * XC), F32)

    def pair(ref, z):
        return jnp.concatenate([ref[0, z], ref[0, z + 1]], axis=1)

    @pl.loop(0, ZC // 2, unroll=4)
    def _(b):
        z = 2 * b
        rows = jnp.concatenate([pair(before, z), pair(value, z), pair(after, z), empty], axis=0)
        hi, lo = split(rows)
        got = dot(wy[0], jnp.concatenate([hi, lo, hi], axis=0))
        out[0, z] = got[:YC, :XC]
        out[0, z + 1] = got[:YC, XC:]

    low[0] = out[0, :HALO]
    high[0] = out[0, ZC - HALO :]


def adjoint_y(g, value, before, after, wy):
    view = pl.BlockSpec((1, ZC, YC, XC), lambda v: (v, 0, 0, 0))
    edge = pl.BlockSpec((1, ZC, HALO, XC), lambda v: (v, 0, 0, 0))
    face = pl.BlockSpec((1, HALO, YC, XC), lambda v: (v, 0, 0, 0))
    face_shape = jax.ShapeDtypeStruct((GROUP, HALO, YC, XC), F32)
    return pl.pallas_call(
        adjoint_y_kernel,
        name="adjoint_y",
        grid=(GROUP,),
        out_shape=(jax.ShapeDtypeStruct((GROUP, ZC, YC, XC), F32), face_shape, face_shape),
        in_specs=[view, edge, edge, pl.BlockSpec((1, 32, 3 * YK), lambda v: (v + g * GROUP, 0, 0))],
        out_specs=(view, face, face),
        **params(8),
    )(value, before, after, wy)


def pack_sides(first, last, q):
    group = lax.broadcasted_iota(jnp.int32, first.shape[1:], 1) // HALO
    acc = jnp.zeros(first.shape[1:], F32)
    for j in range(4):
        acc = jnp.where(group == j, pltpu.roll(first[4 * q + j], HALO * j + HALO, 1), acc)
        acc = jnp.where(group == 4 + j, pltpu.roll(last[4 * q + j], XC // 2 + HALO * j, 1), acc)
    return acc


def sides_kernel(first, last, out):
    for q in range(out.shape[0]):
        out[q] = pack_sides(first, last, q)


def pack(first, last):
    return pl.pallas_call(
        sides_kernel,
        name="sides",
        out_shape=jax.ShapeDtypeStruct((first.shape[0] // 4,) + first.shape[1:], F32),
        **params(2),
    )(first, last)


def add_logs(taps, value, before, after, win, total):
    win[:HALO] = before[0]
    win[HALO : HALO + ZC] = value[0]
    win[HALO + ZC :] = after[0]

    def store(z0, y0, back):
        total[pl.ds(z0, 16), y0 : y0 + 8, :] += jnp.log(back)

    z_sum(win, taps, pl.program_id(0), store)


def first_logs_kernel(taps, value, before, after, total, win):
    @pl.when(pl.program_id(0) == 0)
    def _():
        total[...] = jnp.zeros_like(total)

    add_logs(taps, value, before, after, win, total)


def last_logs_kernel(taps, value, before, after, logs, estimate, out, sides, win, total):
    @pl.when(pl.program_id(0) == 0)
    def _():
        total[...] = logs[...]

    add_logs(taps, value, before, after, win, total)

    @pl.when(pl.program_id(0) == GROUP - 1)
    def _():
        out[...] = estimate[...] * jnp.exp(total[...] / VIEWS)

        @pl.loop(0, ZC // 4)
        def _(q):
            sides[q] = pack_sides(out, out, q)


def adjoint_z(g, tz, value, before, after, logs, estimate):
    view = pl.BlockSpec((1, ZC, YC, XC), lambda v: (v, 0, 0, 0))
    face = pl.BlockSpec((1, HALO, YC, XC), lambda v: (v, 0, 0, 0))
    chunk = pl.BlockSpec((ZC, YC, XC), lambda v: (0, 0, 0))
    packed = pl.BlockSpec((ZC // 4, YC, XC), lambda v: (0, 0, 0))
    chunk_shape = jax.ShapeDtypeStruct((ZC, YC, XC), F32)
    ins = [pl.BlockSpec(memory_space=pltpu.SMEM), view, face, face]
    win = pltpu.VMEM((ZW, YC, XC), F32)
    args = (tz[g * GROUP : (g + 1) * GROUP], value, before, after)
    if logs is None:
        return pl.pallas_call(
            first_logs_kernel,
            name="first_logs",
            grid=(GROUP,),
            out_shape=chunk_shape,
            in_specs=ins,
            out_specs=chunk,
            scratch_shapes=[win],
            **params(9),
        )(*args)
    return pl.pallas_call(
        last_logs_kernel,
        name="last_logs",
        grid=(GROUP,),
        out_shape=(chunk_shape, jax.ShapeDtypeStruct((ZC // 4, YC, XC), F32)),
        in_specs=ins + [chunk, chunk],
        out_specs=(chunk, packed),
        scratch_shapes=[win, pltpu.VMEM((ZC, YC, XC), F32)],
        **params(10),
    )(*args, logs, estimate)


def add_z(blocks):
    before, after = exchange(blocks[0], blocks[SLABS - 1], "z", 4)
    return jnp.concatenate([before[None], blocks, after[None]], axis=0)


def first_window(slab):
    padded = jnp.pad(slab, ((0, 0), (HALO, HALO), (XC, XC)))
    c = lax.axis_index(V)
    before, own, after = (lax.dynamic_slice_in_dim(padded, XC * (c + k), XC, axis=2) for k in range(3))
    planes = jnp.concatenate([own, pack(before, after)], axis=0)
    me = lax.axis_index(S)

    def rows(k):
        return lax.dynamic_slice_in_dim(planes, YC * k, YW, axis=1)

    got = [rows(me)]
    for k in range(1, SLABS):
        got.append(lax.ppermute(rows(me ^ k), S, [(i, i ^ k) for i in range(SLABS)]))
    got = jnp.stack(got)
    blocks = jnp.stack([lax.dynamic_index_in_dim(got, me ^ k, 0, keepdims=False) for k in range(SLABS)])
    return add_z(blocks), own


def next_window(chunk, sides):
    before, after = exchange(sides, sides, V, VIEWS)
    lane = lax.broadcasted_iota(jnp.int32, sides.shape, 2)
    packed = jnp.where(lane < XC // 2, before, after)
    blocks = [chunk.reshape(SLABS, DEPTH, YC, XC), packed.reshape(SLABS, PACKED, YC, XC)]
    blocks = add_z(jnp.concatenate(blocks, axis=1))
    before, after = exchange(blocks[:, :, :HALO], blocks[:, :, YC - HALO :], S, SLABS)
    return jnp.concatenate([before, blocks, after], axis=2)


def matrices(taps):
    def rows(n):
        return jnp.arange(n)[:, None]

    def columns(n):
        return jnp.arange(n)[None, :]

    def stacked(value):
        hi, lo = split_constant(value)
        top = jnp.concatenate([hi, lo], axis=-1)
        return jnp.concatenate([top, jnp.concatenate([hi, jnp.zeros_like(lo)], axis=-1)], axis=-2)

    lane = rows(XC)
    fx = stacked(banded(taps[:, 0], lane - columns(XC) + RADIUS))
    x_of = jnp.where(lane < XC // 2, lane % HALO - HALO, lane % HALO + XC)
    mine = (lane // HALO % 4)[None] == jnp.arange(4)[:, None, None]
    fp = stacked(jnp.where(mine[None], banded(taps[:, 0], x_of - columns(XC) + RADIUS)[:, None], 0.0))
    r = columns(YK) - HALO
    fy_hi, fy_lo = split_constant(banded(taps[:, 1], r - rows(YC) + RADIUS))
    fy = jnp.concatenate([fy_hi, fy_hi, fy_lo], axis=2).reshape(VIEWS * YC, 3 * YK)
    ax = stacked(banded(taps[:, 0], columns(XC) - lane + RADIUS))
    slot = GROUP * jnp.arange(2)[None, :] + (jnp.arange(VIEWS) % GROUP)[:, None]
    mine = (lane // HALO)[None, None] == slot[:, :, None, None]
    sides = [
        jnp.where(mine, banded(taps[:, 0], columns(XC) - at + RADIUS)[:, None], 0.0)
        for at in (lane % HALO - HALO, lane % HALO + XC)
    ]
    sh_hi, sh_lo = split_constant(jnp.concatenate(sides, axis=2))
    sha = jnp.concatenate([sh_hi, sh_lo], axis=3)
    ay = jnp.pad(banded(taps[:, 1], rows(YC) - r + RADIUS), ((0, 0), (0, 32 - YC), (0, 0)))
    ay_hi, ay_lo = split_constant(ay)
    ay = jnp.concatenate([ay_hi, ay_hi, ay_lo], axis=2)
    return (fy, fx, fp), (ax, sha, sh_hi), ay


def per_device(views_data, estimate, kernels):
    everyone = lax.all_gather(kernels[0], V, axis=0)
    taps = everyone / jnp.sum(everyone, axis=-1, keepdims=True)
    w_forward, w_x, w_y = matrices(taps)
    tz, tz_flipped = taps[:, 2], taps[:, 2, ::-1]

    blocks = views_data[0].reshape(DEPTH, SLABS, YC, VIEWS, XC).transpose(3, 1, 0, 2, 4)
    blocks = blocks.reshape(VIEWS * SLABS, DEPTH, YC, XC)
    data = lax.all_to_all(blocks, V + S, 0, 0, tiled=True).reshape(VIEWS, ZC, YC, XC)
    window, own = first_window(estimate)
    chunk = window[1 : 1 + SLABS, :DEPTH, HALO : HALO + YC].reshape(ZC, YC, XC)
    groups = range(VIEWS // GROUP)
    for number in range(ITERS):
        if number:
            window = next_window(chunk, sides)
        faces = []
        for g in groups:
            ratio, left, right = forward(g, tz, window, data, *w_forward)
            faces.append((ratio,) + exchange(left, right, V, VIEWS))
        edges = []
        for g in groups:
            value, top, bottom = adjoint_x(g, *faces[g], *w_x)
            edges.append((value,) + exchange(top, bottom, S, SLABS))
        ends = []
        for g in groups:
            value, low, high = adjoint_y(g, *edges[g], w_y)
            ends.append((value,) + exchange(low, high, "z", 4))
        logs = adjoint_z(0, tz_flipped, *ends[0], None, None)
        chunk, sides = adjoint_z(1, tz_flipped, *ends[1], logs, chunk)

    parts = chunk.reshape(1, SLABS, DEPTH, YC, XC)
    parts = jnp.broadcast_to(parts, (VIEWS, SLABS, DEPTH, YC, XC)).reshape(VIEWS * SLABS, DEPTH, YC, XC)
    got = lax.all_to_all(parts, V + S, 0, 0, tiled=True).reshape(VIEWS, SLABS, DEPTH, YC, XC)
    return got.transpose(2, 1, 3, 0, 4).reshape(DEPTH, SLABS * YC, VIEWS * XC)


def solution(mesh):
    fine = Mesh(mesh.devices.reshape(2, 4, 4, 2, 2), V + ("z",) + S)
    gz = ("z",) + S
    return jax.shard_map(
        per_device,
        mesh=fine,
        in_specs=(P(V, gz, None, None), P(gz, None, None), P(V, None, None)),
        out_specs=P(gz, None, None),
        check_vma=False,
    )
```

time: 711 us -> 686 us (0.965)
  waiting for transfers between devices: 256 us -> 65.2 us
  blocking collectives: 111 us -> 198 us
  starting transfers between devices: 75 us -> 102 us
  local copies, waits for them, and re-layouts: 39.4 us -> 63.5 us
  Pallas kernels: 192 us -> 208 us
  other arithmetic: 34 us -> 42.8 us
    ppermute x20 -> x32, waiting for transfers between devices: 217 us -> 65.2 us  [exchange(): return (lax.ppermute(high, axis, up), lax.ppermute(low, axis, down))]
    all_gather x1, blocking collectives: 26 us -> 105 us  [per_device(): everyone = lax.all_gather(kernels[0], V, axis=0)]
    ppermute x20 -> x32, starting transfers between devices: 60.5 us -> 90.7 us  [exchange(): return (lax.ppermute(high, axis, up), lax.ppermute(low, axis, down))]
    all_to_all x1, waiting for transfers between devices: 28.5 us -> 0.01 us  [per_device(): lax.all_to_all(blocks, V + S, 0, 0, tiled=True).reshape(VIEWS, ZC, YC, XC)]
    pallas_call x8 -> x17, Pallas kernels: 192 us -> 208 us  [the longest x4 88.7 us: forward(): pl.pallas_call(forward_kernel, name='forward', grid=(GROUP,), out_shape=(...]
    broadcast_in_dim x62, local copies, waits for them, and re-layouts: 4.68 us -> 16.7 us  [banded(): result = result + jnp.where(offsets == t, taps[:, t, None, None], 0.0)]
    all_to_all x1 -> x0, waiting for transfers between devices: 11.3 us -> none  [first_window(): planes = lax.all_to_all(blocks, S, 0, 0, tiled=True).reshape(ZC, YW, 2 * XC)]
    unnamed x30 -> x93, local copies, waits for them, and re-layouts: 8.49 us -> 17 us
  transfers between devices with their start and end apart: 22 -> 36, of which waited for: 22 -> 18; matrix products, arithmetic and copies ran while one was open for 6% -> 11% of each run, Pallas kernels for 0% -> 20%
where the time goes in v2:
time: 686 us; the launch traced here: 680 us
  Pallas kernels  208 us (30%)
  blocking collectives  198 us (29%)
  starting transfers between devices  102 us (15%)
  waiting for transfers between devices  65.2 us (10%)
  local copies, waits for them, and re-layouts  63.5 us (9%)
  other arithmetic  42.8 us (6%)
    all_gather x1, blocking collectives, per_device(): everyone = lax.all_gather(kernels[0], V, axis=0)  105 us
    all_to_all x1, blocking collectives, per_device(): lax.all_to_all(parts, V + S, 0, 0, tiled=True)  92.8 us
    ppermute x32, starting transfers between devices, exchange(): return (lax.ppermute(high, axis, up), lax.ppermute(low, axis, down))  90.7 us
    pallas_call x4, Pallas kernels, forward(): pl.pallas_call(forward_kernel, name='forward', grid=(GROUP,), out_shape=(...  88.7 us
    ppermute x32, waiting for transfers between devices, exchange(): return (lax.ppermute(high, axis, up), lax.ppermute(low, axis, down))  65.2 us
    pallas_call x4, Pallas kernels, adjoint_x(): pl.pallas_call(adjoint_x_kernel, name='adjoint_x', grid=(GROUP,), out_sha...  35.9 us
    pallas_call x4, Pallas kernels, adjoint_y(): pl.pallas_call(adjoint_y_kernel, name='adjoint_y', grid=(GROUP,), out_sha...  35.8 us
    pallas_call x2, Pallas kernels, adjoint_z(): pl.pallas_call(last_logs_kernel, name='last_logs', grid=(GROUP,), out_sha...  24.4 us
  transfers between devices with their start and end apart: 36, of which 18 were waited for; matrix products, arithmetic and copies ran while one was open for 11% of the time, Pallas kernels for 20%

profile of v2, /device:TPU:1, one launch (start us, length us, event | category | flops | bytes accessed | tf_op | source)
XLA Modules:
  0.0 679.8 jit_solution(13948612297832676424)
XLA Ops:
  17.4 7.9 %all-to-all-start = ((f32[32,16,24,128]{3,2,1,0:T(8,128)}), f32[32,16,24,128]{3,2,1,0:T(8,128)}, u32[]{:S(2)}, u32[]{:S(2)}) async-start(f32[32,16,24,128]{3,2,1,0:T(8,128)} %bitcast.136), calls=%async_computation | async-start | bytes 12582912 | tf_op jit(solution)/shard_map/all_to_all | solution.py:400
  25.8 104.9 %all_gather.3 = f32[8,3,31]{2,1,0:T(4,128)S(1)} all-gather(f32[1,3,31]{2,1,0:T(4,128)S(1)} %copy.8), channel_id=1, replica_groups=mesh['yh'=2,'x'=4,'z'=4,'yl'=2,'co'=2] {'yh','x'}, dimensions={0}, use_global_device_ids=true | all-gather | bytes 3348 | tf_op jit(solution)/shard_map/all_gather | solution.py:393
  206.4 22.1 %forward.5 = (f32[4,64,24,128]{3,2,1,0:T(8,128)}, f32[32,24,128]{2,1,0:T(8,128)}, f32[32,24,128]{2,1,0:T(8,128)}) custom-call(f32[4,31]{1,0:T(4,128)} %bitcast.163, f32[6,20,56,128]{3,2,1,0:T(8,128)} %bitcast_dynamic-update-slice_fusion.est, f32[8,64,24,128]{3,2,1,0:T(8,128)} %bitcast.12.data, bf16[192,192]{1,0:T(8,128)(2,1)} %pad_maximum_fusion.10.wy, ...), custom_call_target="tpu_custom_call" | custom-call | flops 24000000000 | bytes 48000000 | tf_op jit(solution)/shard_map/forward/pallas_call | solution.py:133
  231.1 22.2 %forward.4 = (f32[4,64,24,128]{3,2,1,0:T(8,128)}, f32[32,24,128]{2,1,0:T(8,128)}, f32[32,24,128]{2,1,0:T(8,128)}) custom-call(f32[4,31]{1,0:T(4,128)} %bitcast.161, f32[6,20,56,128]{3,2,1,0:T(8,128)} %bitcast_dynamic-update-slice_fusion.est, f32[8,64,24,128]{3,2,1,0:T(8,128)} %bitcast.12.data, bf16[192,192]{1,0:T(8,128)(2,1)} %pad_maximum_fusion.10.wy, ...), custom_call_target="tpu_custom_call" | custom-call | flops 24000000000 | bytes 48000000 | tf_op jit(solution)/shard_map/forward/pallas_call | solution.py:133
  259.5 9.0 %adjoint_x.5 = (f32[4,64,24,128]{3,2,1,0:T(8,128)}, f32[4,64,16,128]{3,2,1,0:T(8,128)}, f32[4,64,16,128]{3,2,1,0:T(8,128)}) custom-call(f32[4,64,24,128]{3,2,1,0:T(8,128)} %get-tuple-element.53.ratio, f32[32,24,128]{2,1,0:T(8,128)} %copy-done.38, f32[32,24,128]{2,1,0:T(8,128)} %copy-done.39, bf16[8,256,256]{2,1,0:T(8,128)(2,1)} %fusion.7.wown, ...), custom_call_target="tpu_custom_call" | custom-call | flops 8000000000 | bytes 16000000 | tf_op jit(solution)/shard_map/adjoint_x/pallas_call | solution.py:181
  268.4 9.7 %collective-permute-start.13 = (f32[4,64,16,128]{3,2,1,0:T(8,128)}, f32[4,64,16,128]{3,2,1,0:T(8,128)}, u32[]{:S(2)}, u32[]{:S(2)}) collective-permute-start(f32[4,64,16,128]{3,2,1,0:T(8,128)} %get-tuple-element.57), channel_id=1, source_target_pairs={{0,1},{1,2},{2,3},{4,5},{5,6},{6,7},{8,9},{9,10},{10,11},{12,13},{... | collective-permute-start | bytes 6291464 | tf_op jit(solution)/shard_map/ppermute | solution.py:60
  281.4 9.0 %adjoint_x.4 = (f32[4,64,24,128]{3,2,1,0:T(8,128)}, f32[4,64,16,128]{3,2,1,0:T(8,128)}, f32[4,64,16,128]{3,2,1,0:T(8,128)}) custom-call(f32[4,64,24,128]{3,2,1,0:T(8,128)} %get-tuple-element.44.ratio, f32[32,24,128]{2,1,0:T(8,128)} %copy-done.33, f32[32,24,128]{2,1,0:T(8,128)} %copy-done.35, bf16[8,256,256]{2,1,0:T(8,128)(2,1)} %fusion.7.wown, ...), custom_call_target="tpu_custom_call" | custom-call | flops 8000000000 | bytes 16000000 | tf_op jit(solution)/shard_map/adjoint_x/pallas_call | solution.py:181
  305.8 9.1 %adjoint_y.5 = (f32[4,64,24,128]{3,2,1,0:T(8,128)}, f32[4,16,24,128]{3,2,1,0:T(8,128)}, f32[4,16,24,128]{3,2,1,0:T(8,128)}) custom-call(f32[4,64,24,128]{3,2,1,0:T(8,128)} %get-tuple-element.56.value, f32[4,64,16,128]{3,2,1,0:T(8,128)} %collective-permute-done.13.before, f32[4,64,16,128]{3,2,1,0:T(8,128)} %collective-permute-done.14.after, ...), custom_call_target="tpu_custom_call" | custom-call | flops 8000000000 | bytes 16000000 | tf_op jit(solution)/shard_map/adjoint_y/pallas_call | solution.py:223
  328.5 8.9 %adjoint_y.4 = (f32[4,64,24,128]{3,2,1,0:T(8,128)}, f32[4,16,24,128]{3,2,1,0:T(8,128)}, f32[4,16,24,128]{3,2,1,0:T(8,128)}) custom-call(f32[4,64,24,128]{3,2,1,0:T(8,128)} %get-tuple-element.47.value, f32[4,64,16,128]{3,2,1,0:T(8,128)} %collective-permute-done.7.before, f32[4,64,16,128]{3,2,1,0:T(8,128)} %collective-permute-done.8.after, ...), custom_call_target="tpu_custom_call" | custom-call | flops 8000000000 | bytes 16000000 | tf_op jit(solution)/shard_map/adjoint_y/pallas_call | solution.py:223
  343.4 10.0 %first_logs.2.logs = f32[64,24,128]{2,1,0:T(8,128)} custom-call(f32[4,31]{1,0:T(4,128)} %bitcast.167, f32[4,64,24,128]{3,2,1,0:T(8,128)} %get-tuple-element.59.value, f32[4,16,24,128]{3,2,1,0:T(8,128)} %copy-done.24, f32[4,16,24,128]{3,2,1,0:T(8,128)} %copy-done.25), custom_call_target="tpu_custom_call" | custom-call | flops 8999999488 | bytes 18000000 | tf_op jit(solution)/shard_map/first_logs/pallas_call | solution.py:302
  354.8 12.2 %last_logs.2 = (f32[64,24,128]{2,1,0:T(8,128)}, f32[16,24,128]{2,1,0:T(8,128)}) custom-call(f32[4,31]{1,0:T(4,128)} %bitcast.165, f32[4,64,24,128]{3,2,1,0:T(8,128)} %get-tuple-element.50.value, f32[4,16,24,128]{3,2,1,0:T(8,128)} %copy-done.29, f32[4,16,24,128]{3,2,1,0:T(8,128)} %copy-done.31, f32[64,24,128]{2,1,0:T(8,128)} %first_logs.2.logs, ...), custom_call_target="tpu_custom_call" | custom-call | flops 10000000000 | bytes 20000000 | tf_op jit(solution)/shard_map/last_logs/pallas_call | solution.py:312
  395.8 9.1 %collective-permute-done.21 = f32[6,20,16,128]{3,2,1,0:T(8,128)S(1)} collective-permute-done((f32[6,20,16,128]{3,2,1,0:T(8,128)S(1)}, f32[6,20,16,128]{3,2,1,0:T(8,128)S(1)}, u32[]{:S(2)}, u32[]{:S(2)}) %collective-permute-start.21) | collective-permute-done | bytes 983072 | tf_op jit(solution)/shard_map/ppermute | solution.py:60
  411.3 22.1 %forward.7 = (f32[4,64,24,128]{3,2,1,0:T(8,128)}, f32[32,24,128]{2,1,0:T(8,128)}, f32[32,24,128]{2,1,0:T(8,128)}) custom-call(f32[4,31]{1,0:T(4,128)} %bitcast.164, f32[6,20,56,128]{3,2,1,0:T(8,128)} %pad_maximum_fusion.est, f32[8,64,24,128]{3,2,1,0:T(8,128)} %bitcast.12.data, bf16[192,192]{1,0:T(8,128)(2,1)} %pad_maximum_fusion.10.wy, ...), custom_call_target="tpu_custom_call" | custom-call | flops 24000000000 | bytes 48000000 | tf_op jit(solution)/shard_map/forward/pallas_call | solution.py:133
  438.8 22.3 %forward.6 = (f32[4,64,24,128]{3,2,1,0:T(8,128)}, f32[32,24,128]{2,1,0:T(8,128)}, f32[32,24,128]{2,1,0:T(8,128)}) custom-call(f32[4,31]{1,0:T(4,128)} %bitcast.162, f32[6,20,56,128]{3,2,1,0:T(8,128)} %pad_maximum_fusion.est, f32[8,64,24,128]{3,2,1,0:T(8,128)} %bitcast.12.data, bf16[192,192]{1,0:T(8,128)(2,1)} %pad_maximum_fusion.10.wy, ...), custom_call_target="tpu_custom_call" | custom-call | flops 24000000000 | bytes 48000000 | tf_op jit(solution)/shard_map/forward/pallas_call | solution.py:133
  469.4 9.0 %adjoint_x.7 = (f32[4,64,24,128]{3,2,1,0:T(8,128)}, f32[4,64,16,128]{3,2,1,0:T(8,128)}, f32[4,64,16,128]{3,2,1,0:T(8,128)}) custom-call(f32[4,64,24,128]{3,2,1,0:T(8,128)} %get-tuple-element.73.ratio, f32[32,24,128]{2,1,0:T(8,128)} %copy-done.36, f32[32,24,128]{2,1,0:T(8,128)} %copy-done.37, bf16[8,256,256]{2,1,0:T(8,128)(2,1)} %fusion.7.wown, ...), custom_call_target="tpu_custom_call" | custom-call | flops 8000000000 | bytes 16000000 | tf_op jit(solution)/shard_map/adjoint_x/pallas_call | solution.py:181
  483.7 8.9 %adjoint_x.6 = (f32[4,64,24,128]{3,2,1,0:T(8,128)}, f32[4,64,16,128]{3,2,1,0:T(8,128)}, f32[4,64,16,128]{3,2,1,0:T(8,128)}) custom-call(f32[4,64,24,128]{3,2,1,0:T(8,128)} %get-tuple-element.64.ratio, f32[32,24,128]{2,1,0:T(8,128)} %copy-done.32, f32[32,24,128]{2,1,0:T(8,128)} %copy-done.34, bf16[8,256,256]{2,1,0:T(8,128)(2,1)} %fusion.7.wown, ...), custom_call_target="tpu_custom_call" | custom-call | flops 8000000000 | bytes 16000000 | tf_op jit(solution)/shard_map/adjoint_x/pallas_call | solution.py:181
  498.0 10.1 %collective-permute-done.31.before = f32[4,64,16,128]{3,2,1,0:T(8,128)S(1)} collective-permute-done((f32[4,64,16,128]{3,2,1,0:T(8,128)}, f32[4,64,16,128]{3,2,1,0:T(8,128)S(1)}, u32[]{:S(2)}, u32[]{:S(2)}) %collective-permute-start.31) | collective-permute-done | bytes 2097184 | tf_op jit(solution)/shard_map/ppermute | solution.py:60
  512.2 8.9 %adjoint_y.7 = (f32[4,64,24,128]{3,2,1,0:T(8,128)}, f32[4,16,24,128]{3,2,1,0:T(8,128)}, f32[4,16,24,128]{3,2,1,0:T(8,128)}) custom-call(f32[4,64,24,128]{3,2,1,0:T(8,128)} %get-tuple-element.76.value, f32[4,64,16,128]{3,2,1,0:T(8,128)} %copy-done.21, f32[4,64,16,128]{3,2,1,0:T(8,128)} %copy-done.23, bf16[8,32,192]{2,1,0:T(8,128)(2,1)} %pad_maximum_fusion.9.wy), custom_call_target="tpu_custom_call" | custom-call | flops 8000000000 | bytes 16000000 | tf_op jit(solution)/shard_map/adjoint_y/pallas_call | solution.py:223
  533.7 8.9 %adjoint_y.6 = (f32[4,64,24,128]{3,2,1,0:T(8,128)}, f32[4,16,24,128]{3,2,1,0:T(8,128)}, f32[4,16,24,128]{3,2,1,0:T(8,128)}) custom-call(f32[4,64,24,128]{3,2,1,0:T(8,128)} %get-tuple-element.67.value, f32[4,64,16,128]{3,2,1,0:T(8,128)} %copy-done.22, f32[4,64,16,128]{3,2,1,0:T(8,128)} %collective-permute-done.26.after, bf16[8,32,192]{2,1,0:T(8,128)(2,1)} %pad_maximum_fusion.9.wy), custom_call_target="tpu_custom_call" | custom-call | flops 8000000000 | bytes 16000000 | tf_op jit(solution)/shard_map/adjoint_y/pallas_call | solution.py:223
  548.0 9.9 %first_logs.3.logs = f32[64,24,128]{2,1,0:T(8,128)} custom-call(f32[4,31]{1,0:T(4,128)} %bitcast.168, f32[4,64,24,128]{3,2,1,0:T(8,128)} %get-tuple-element.79.value, f32[4,16,24,128]{3,2,1,0:T(8,128)} %copy-done.26, f32[4,16,24,128]{3,2,1,0:T(8,128)} %copy-done.27), custom_call_target="tpu_custom_call" | custom-call | flops 8999999488 | bytes 18000000 | tf_op jit(solution)/shard_map/first_logs/pallas_call | solution.py:302
  559.3 12.2 %last_logs.3 = (f32[64,24,128]{2,1,0:T(8,128)}, f32[16,24,128]{2,1,0:T(8,128)}) custom-call(f32[4,31]{1,0:T(4,128)} %bitcast.166, f32[4,64,24,128]{3,2,1,0:T(8,128)} %get-tuple-element.70.value, f32[4,16,24,128]{3,2,1,0:T(8,128)} %copy-done.28, f32[4,16,24,128]{3,2,1,0:T(8,128)} %copy-done.30, f32[64,24,128]{2,1,0:T(8,128)} %first_logs.3.logs, ...), custom_call_target="tpu_custom_call" | custom-call | flops 10000000000 | bytes 20000000 | tf_op jit(solution)/shard_map/last_logs/pallas_call | solution.py:312
  573.4 92.8 %all_to_all.10 = f32[32,16,24,128]{3,2,1,0:T(8,128)S(1)} all-to-all(f32[32,16,24,128]{3,2,1,0:T(8,128)S(1)} %bitcast.137), channel_id=1, replica_groups=mesh['yh'=2,'x'=4,'z'=4,'yl'=2,'co'=2] {'yh','x','yl','co'}, dimensions={0} | all-to-all | bytes 12582912 | tf_op jit(solution)/shard_map/all_to_all | solution.py:424
  666.2 6.3 copy.10
  672.5 7.1 %reshape.649 = f32[16,96,1024]{2,1,0:T(8,128)} reshape(f32[16,4,24,8,128]{4,3,2,1,0:T(8,128)} %copy.10) | data formatting | bytes 12582912 | tf_op jit(solution)/shard_map/reshape | solution.py:425
  (315 shorter events, 226.0 us)
Async XLA Ops:
  8.9 166.7 %collective-permute-start = (f32[20,56,128]{2,1,0:T(8,128)}, f32[20,56,128]{2,1,0:T(8,128)S(1)}, u32[]{:S(2)}, u32[]{:S(2)}) collective-permute-start(f32[20,56,128]{2,1,0:T(8,128)} %get-tuple-element.165), channel_id=1, source_target_pairs={{0,1},{1,0},{2,3},{3,2},{4,5},{5,4},{6,7},{7,6},{8,9},{9,8},{10,11... | collective-permute-start | bytes 1720328 | tf_op jit(solution)/shard_map/ppermute | solution.py:341
  10.3 165.3 %collective-permute-start.1 = (f32[20,56,128]{2,1,0:T(8,128)}, f32[20,56,128]{2,1,0:T(8,128)}, u32[]{:S(2)}, u32[]{:S(2)}) collective-permute-start(f32[20,56,128]{2,1,0:T(8,128)} %get-tuple-element.166), channel_id=1, source_target_pairs={{0,2},{1,3},{2,0},{3,1},{4,6},{5,7},{6,4},{7,5},{8,10},{9,11},{10,... | collective-permute-start | bytes 1720328 | tf_op jit(solution)/shard_map/ppermute | solution.py:341
  11.7 163.9 %collective-permute-start.2 = (f32[20,56,128]{2,1,0:T(8,128)}, f32[20,56,128]{2,1,0:T(8,128)}, u32[]{:S(2)}, u32[]{:S(2)}) collective-permute-start(f32[20,56,128]{2,1,0:T(8,128)} %get-tuple-element.167), channel_id=1, source_target_pairs={{0,3},{1,2},{2,1},{3,0},{4,7},{5,6},{6,5},{7,4},{8,11},{9,10},{10,... | collective-permute-start | bytes 1720328 | tf_op jit(solution)/shard_map/ppermute | solution.py:341
  17.4 189.0 %all-to-all-start = ((f32[32,16,24,128]{3,2,1,0:T(8,128)}), f32[32,16,24,128]{3,2,1,0:T(8,128)}, u32[]{:S(2)}, u32[]{:S(2)}) async-start(f32[32,16,24,128]{3,2,1,0:T(8,128)} %bitcast.136), calls=%async_computation | async-start | bytes 12582912 | tf_op jit(solution)/shard_map/all_to_all | solution.py:400
  228.5 30.1 %collective-permute-start.11 = (f32[32,24,128]{2,1,0:T(8,128)}, f32[32,24,128]{2,1,0:T(8,128)S(1)}, u32[]{:S(2)}, u32[]{:S(2)}) collective-permute-start(f32[32,24,128]{2,1,0:T(8,128)} %get-tuple-element.54), channel_id=1, source_target_pairs={{0,16},{16,32},{32,48},{48,64},{64,80},{80,96},{96,112},{1,17},{17... | collective-permute-start | bytes 1179656 | tf_op jit(solution)/shard_map/ppermute | solution.py:60
  229.8 28.8 %collective-permute-start.12 = (f32[32,24,128]{2,1,0:T(8,128)}, f32[32,24,128]{2,1,0:T(8,128)S(1)}, u32[]{:S(2)}, u32[]{:S(2)}) collective-permute-start(f32[32,24,128]{2,1,0:T(8,128)} %get-tuple-element.55), channel_id=1, source_target_pairs={{16,0},{32,16},{48,32},{64,48},{80,64},{96,80},{112,96},{17,1},{33... | collective-permute-start | bytes 1179656 | tf_op jit(solution)/shard_map/ppermute | solution.py:60
  253.3 27.2 %collective-permute-start.5 = (f32[32,24,128]{2,1,0:T(8,128)}, f32[32,24,128]{2,1,0:T(8,128)S(1)}, u32[]{:S(2)}, u32[]{:S(2)}) collective-permute-start(f32[32,24,128]{2,1,0:T(8,128)} %get-tuple-element.45), channel_id=1, source_target_pairs={{0,16},{16,32},{32,48},{48,64},{64,80},{80,96},{96,112},{1,17},{17... | collective-permute-start | bytes 1179656 | tf_op jit(solution)/shard_map/ppermute | solution.py:60
  257.3 23.2 %collective-permute-start.6 = (f32[32,24,128]{2,1,0:T(8,128)}, f32[32,24,128]{2,1,0:T(8,128)S(1)}, u32[]{:S(2)}, u32[]{:S(2)}) collective-permute-start(f32[32,24,128]{2,1,0:T(8,128)} %get-tuple-element.46), channel_id=1, source_target_pairs={{16,0},{32,16},{48,32},{64,48},{80,64},{96,80},{112,96},{17,1},{33... | collective-permute-start | bytes 1179656 | tf_op jit(solution)/shard_map/ppermute | solution.py:60
  268.4 33.0 %collective-permute-start.13 = (f32[4,64,16,128]{3,2,1,0:T(8,128)}, f32[4,64,16,128]{3,2,1,0:T(8,128)}, u32[]{:S(2)}, u32[]{:S(2)}) collective-permute-start(f32[4,64,16,128]{3,2,1,0:T(8,128)} %get-tuple-element.57), channel_id=1, source_target_pairs={{0,1},{1,2},{2,3},{4,5},{5,6},{6,7},{8,9},{9,10},{10,11},{12,13},{... | collective-permute-start | bytes 6291464 | tf_op jit(solution)/shard_map/ppermute | solution.py:60
  278.2 27.7 %collective-permute-start.14 = (f32[4,64,16,128]{3,2,1,0:T(8,128)}, f32[4,64,16,128]{3,2,1,0:T(8,128)}, u32[]{:S(2)}, u32[]{:S(2)}) collective-permute-start(f32[4,64,16,128]{3,2,1,0:T(8,128)} %get-tuple-element.58), channel_id=1, source_target_pairs={{1,0},{2,1},{3,2},{5,4},{6,5},{7,6},{9,8},{10,9},{11,10},{13,12},{... | collective-permute-start | bytes 6291464 | tf_op jit(solution)/shard_map/ppermute | solution.py:60
  290.4 33.5 %collective-permute-start.7 = (f32[4,64,16,128]{3,2,1,0:T(8,128)}, f32[4,64,16,128]{3,2,1,0:T(8,128)}, u32[]{:S(2)}, u32[]{:S(2)}) collective-permute-start(f32[4,64,16,128]{3,2,1,0:T(8,128)} %get-tuple-element.48), channel_id=1, source_target_pairs={{0,1},{1,2},{2,3},{4,5},{5,6},{6,7},{8,9},{9,10},{10,11},{12,13},{... | collective-permute-start | bytes 6291464 | tf_op jit(solution)/shard_map/ppermute | solution.py:60
  294.1 34.4 %collective-permute-start.8 = (f32[4,64,16,128]{3,2,1,0:T(8,128)}, f32[4,64,16,128]{3,2,1,0:T(8,128)}, u32[]{:S(2)}, u32[]{:S(2)}) collective-permute-start(f32[4,64,16,128]{3,2,1,0:T(8,128)} %get-tuple-element.49), channel_id=1, source_target_pairs={{1,0},{2,1},{3,2},{5,4},{6,5},{7,6},{9,8},{10,9},{11,10},{13,12},{... | collective-permute-start | bytes 6291464 | tf_op jit(solution)/shard_map/ppermute | solution.py:60
  314.9 27.4 %collective-permute-start.15 = (f32[4,16,24,128]{3,2,1,0:T(8,128)}, f32[4,16,24,128]{3,2,1,0:T(8,128)S(1)}, u32[]{:S(2)}, u32[]{:S(2)}) collective-permute-start(f32[4,16,24,128]{3,2,1,0:T(8,128)} %get-tuple-element.60), channel_id=1, source_target_pairs={{0,4},{4,8},{8,12},{1,5},{5,9},{9,13},{2,6},{6,10},{10,14},{3,7},{... | collective-permute-start | bytes 2359304 | tf_op jit(solution)/shard_map/ppermute | solution.py:60
  318.5 23.8 %collective-permute-start.16 = (f32[4,16,24,128]{3,2,1,0:T(8,128)}, f32[4,16,24,128]{3,2,1,0:T(8,128)S(1)}, u32[]{:S(2)}, u32[]{:S(2)}) collective-permute-start(f32[4,16,24,128]{3,2,1,0:T(8,128)} %get-tuple-element.61), channel_id=1, source_target_pairs={{4,0},{8,4},{12,8},{5,1},{9,5},{13,9},{6,2},{10,6},{14,10},{7,3},{... | collective-permute-start | bytes 2359304 | tf_op jit(solution)/shard_map/ppermute | solution.py:60
  337.4 16.0 %collective-permute-start.9 = (f32[4,16,24,128]{3,2,1,0:T(8,128)}, f32[4,16,24,128]{3,2,1,0:T(8,128)S(1)}, u32[]{:S(2)}, u32[]{:S(2)}) collective-permute-start(f32[4,16,24,128]{3,2,1,0:T(8,128)} %get-tuple-element.51), channel_id=1, source_target_pairs={{0,4},{4,8},{8,12},{1,5},{5,9},{9,13},{2,6},{6,10},{10,14},{3,7},{... | collective-permute-start | bytes 2359304 | tf_op jit(solution)/shard_map/ppermute | solution.py:60
  433.4 35.0 %collective-permute-start.29 = (f32[32,24,128]{2,1,0:T(8,128)}, f32[32,24,128]{2,1,0:T(8,128)S(1)}, u32[]{:S(2)}, u32[]{:S(2)}) collective-permute-start(f32[32,24,128]{2,1,0:T(8,128)} %get-tuple-element.74), channel_id=1, source_target_pairs={{0,16},{16,32},{32,48},{48,64},{64,80},{80,96},{96,112},{1,17},{17... | collective-permute-start | bytes 1179656 | tf_op jit(solution)/shard_map/ppermute | solution.py:60
  437.5 31.0 %collective-permute-start.30 = (f32[32,24,128]{2,1,0:T(8,128)}, f32[32,24,128]{2,1,0:T(8,128)S(1)}, u32[]{:S(2)}, u32[]{:S(2)}) collective-permute-start(f32[32,24,128]{2,1,0:T(8,128)} %get-tuple-element.75), channel_id=1, source_target_pairs={{16,0},{32,16},{48,32},{64,48},{80,64},{96,80},{112,96},{17,1},{33... | collective-permute-start | bytes 1179656 | tf_op jit(solution)/shard_map/ppermute | solution.py:60
  461.0 21.8 %collective-permute-start.23 = (f32[32,24,128]{2,1,0:T(8,128)}, f32[32,24,128]{2,1,0:T(8,128)S(1)}, u32[]{:S(2)}, u32[]{:S(2)}) collective-permute-start(f32[32,24,128]{2,1,0:T(8,128)} %get-tuple-element.65), channel_id=1, source_target_pairs={{0,16},{16,32},{32,48},{48,64},{64,80},{80,96},{96,112},{1,17},{17... | collective-permute-start | bytes 1179656 | tf_op jit(solution)/shard_map/ppermute | solution.py:60
  478.3 29.8 %collective-permute-start.31 = (f32[4,64,16,128]{3,2,1,0:T(8,128)}, f32[4,64,16,128]{3,2,1,0:T(8,128)S(1)}, u32[]{:S(2)}, u32[]{:S(2)}) collective-permute-start(f32[4,64,16,128]{3,2,1,0:T(8,128)} %get-tuple-element.77), channel_id=1, source_target_pairs={{0,1},{1,2},{2,3},{4,5},{5,6},{6,7},{8,9},{9,10},{10,11},{12,13},{... | collective-permute-start | bytes 6291464 | tf_op jit(solution)/shard_map/ppermute | solution.py:60
  480.6 30.3 %collective-permute-start.32 = (f32[4,64,16,128]{3,2,1,0:T(8,128)}, f32[4,64,16,128]{3,2,1,0:T(8,128)S(1)}, u32[]{:S(2)}, u32[]{:S(2)}) collective-permute-start(f32[4,64,16,128]{3,2,1,0:T(8,128)} %get-tuple-element.78), channel_id=1, source_target_pairs={{1,0},{2,1},{3,2},{5,4},{6,5},{7,6},{9,8},{10,9},{11,10},{13,12},{... | collective-permute-start | bytes 6291464 | tf_op jit(solution)/shard_map/ppermute | solution.py:60
  492.6 37.9 %collective-permute-start.25 = (f32[4,64,16,128]{3,2,1,0:T(8,128)}, f32[4,64,16,128]{3,2,1,0:T(8,128)S(1)}, u32[]{:S(2)}, u32[]{:S(2)}) collective-permute-start(f32[4,64,16,128]{3,2,1,0:T(8,128)} %get-tuple-element.68), channel_id=1, source_target_pairs={{0,1},{1,2},{2,3},{4,5},{5,6},{6,7},{8,9},{9,10},{10,11},{12,13},{... | collective-permute-start | bytes 6291464 | tf_op jit(solution)/shard_map/ppermute | solution.py:60
  496.1 37.6 %collective-permute-start.26 = (f32[4,64,16,128]{3,2,1,0:T(8,128)}, f32[4,64,16,128]{3,2,1,0:T(8,128)}, u32[]{:S(2)}, u32[]{:S(2)}) collective-permute-start(f32[4,64,16,128]{3,2,1,0:T(8,128)} %get-tuple-element.69), channel_id=1, source_target_pairs={{1,0},{2,1},{3,2},{5,4},{6,5},{7,6},{9,8},{10,9},{11,10},{13,12},{... | collective-permute-start | bytes 6291464 | tf_op jit(solution)/shard_map/ppermute | solution.py:60
  521.2 25.6 %collective-permute-start.33 = (f32[4,16,24,128]{3,2,1,0:T(8,128)}, f32[4,16,24,128]{3,2,1,0:T(8,128)S(1)}, u32[]{:S(2)}, u32[]{:S(2)}) collective-permute-start(f32[4,16,24,128]{3,2,1,0:T(8,128)} %get-tuple-element.80), channel_id=1, source_target_pairs={{0,4},{4,8},{8,12},{1,5},{5,9},{9,13},{2,6},{6,10},{10,14},{3,7},{... | collective-permute-start | bytes 2359304 | tf_op jit(solution)/shard_map/ppermute | solution.py:60
  524.1 22.7 %collective-permute-start.34 = (f32[4,16,24,128]{3,2,1,0:T(8,128)}, f32[4,16,24,128]{3,2,1,0:T(8,128)S(1)}, u32[]{:S(2)}, u32[]{:S(2)}) collective-permute-start(f32[4,16,24,128]{3,2,1,0:T(8,128)} %get-tuple-element.81), channel_id=1, source_target_pairs={{4,0},{8,4},{12,8},{5,1},{9,5},{13,9},{6,2},{10,6},{14,10},{7,3},{... | collective-permute-start | bytes 2359304 | tf_op jit(solution)/shard_map/ppermute | solution.py:60
  (55 other events, 386.2 us)

commit v3 on v2

--- a/solution.py
+++ b/solution.py
@@ -1,3 +1,5 @@
+import functools
+
 import jax
 import jax.numpy as jnp
 from jax import lax
@@ -38,19 +40,14 @@
     return hi, (value - hi.astype(F32)).astype(BF16)
 
 
-def split_constant(value):
-    hi = lax.reduce_precision(value, 8, 7)
-    return hi.astype(BF16), (value - hi).astype(BF16)
-
-
 def dot(a, b):
     return jnp.dot(a, b, preferred_element_type=F32)
 
 
-def banded(taps, offsets):
-    result = jnp.zeros((taps.shape[0],) + offsets.shape, F32)
+def banded(taps, v, axis, offsets):
+    result = jnp.zeros(offsets.shape, F32)
     for t in range(TAPS):
-        result = result + jnp.where(offsets == t, taps[:, t, None, None], 0.0)
+        result = jnp.where(offsets == t, taps[v, axis * TAPS + t], result)
     return result
 
 
@@ -60,30 +57,32 @@
     return lax.ppermute(high, axis, up), lax.ppermute(low, axis, down)
 
 
-def z_sum(win, taps, v, store):
+def z_sum(win, taps, v, flipped, store):
     @pl.loop(0, ZC // 16)
     def _(b):
         z0 = pl.multiple_of(b * 16, 16)
         for y0 in range(0, YC, 8):
             acc = jnp.zeros((16, 8, XC), F32)
             for t in range(TAPS):
-                acc = acc + taps[v, t] * win[pl.ds(z0 + t + 1, 16), y0 : y0 + 8, :]
+                tap = taps[v, 2 * TAPS + (TAPS - 1 - t if flipped else t)]
+                acc = acc + tap * win[pl.ds(z0 + t + 1, 16), y0 : y0 + 8, :]
             store(z0, y0, acc)
 
 
-def forward_kernel(taps, est, data, wy, wown, wpack, ratio, left, right, yown, ypack, win):
+def blur_planes(g, taps, est, wy, wown, wpack, yown, ypack, win):
     v = pl.program_id(0)
 
     @pl.when(v == 0)
     def _():
         empty = jnp.zeros((YK - YW, 2 * XC), F32)
+        matrix = wy[...].astype(BF16)
 
         @pl.loop(0, SLABS + 2)
         def _(b):
             for i in range((DEPTH + PACKED) // 2):
                 planes = jnp.concatenate([est[b, 2 * i], est[b, 2 * i + 1]], axis=1)
                 hi, lo = split(jnp.concatenate([planes, empty], axis=0))
-                got = dot(wy[...], jnp.concatenate([hi, lo, hi], axis=0))
+                got = dot(matrix, jnp.concatenate([hi, lo, hi], axis=0))
                 if i < DEPTH // 2:
                     dest, first = yown, b * DEPTH * YC + 2 * i * YC
                 else:
@@ -108,49 +107,104 @@
             for q in range(step):
                 win[b * step * 4 + q * 4 + j] = out[q]
 
-    group = lax.broadcasted_iota(jnp.int32, (16, 8, XC), 2) // HALO
-
-    def store(z0, y0, blurred):
-        zs = pl.ds(z0, 16)
-        value = data[0, zs, y0 : y0 + 8, :] / blurred
-        ratio[0, zs, y0 : y0 + 8, :] = value
-        half = z0 // (ZC // 2)
-        at = GROUP * half + v
-        zs = pl.ds(z0 - half * (ZC // 2), 16)
-        first = pltpu.roll(value, HALO * at, 2)
-        last = pltpu.roll(value, lax.rem(HALO * at + HALO, XC), 2)
-        left[zs, y0 : y0 + 8, :] = jnp.where(group == at, first, left[zs, y0 : y0 + 8, :])
-        right[zs, y0 : y0 + 8, :] = jnp.where(group == at, last, right[zs, y0 : y0 + 8, :])
-
-    z_sum(win, taps, v, store)
-
-
-def forward(g, tz, window, data, wy, wown, wpack):
-    view = pl.BlockSpec((1, ZC, YC, XC), lambda v: (v + g * GROUP, 0, 0, 0))
-    out = pl.BlockSpec((1, ZC, YC, XC), lambda v: (v, 0, 0, 0))
-    pack = pl.BlockSpec((ZC // 2, YC, XC), lambda v: (0, 0, 0))
-    shape = jax.ShapeDtypeStruct((ZC // 2, YC, XC), F32)
-    return pl.pallas_call(
-        forward_kernel,
-        name="forward",
+
+def divide(z0, y0, recorded, blurred, ratio, left, right):
+    v = pl.program_id(0)
+    zs, ys = pl.ds(z0, 16), pl.ds(y0, 8)
+    value = recorded[0, zs, ys, :] / blurred
+    ratio[0, zs, ys, :] = value
+    half = z0 // (ZC // 2)
+    at = GROUP * half + v
+    mine = lax.broadcasted_iota(jnp.int32, value.shape, 2) // HALO == at
+    zs = pl.ds(z0 - half * (ZC // 2), 16)
+    first = pltpu.roll(value, HALO * at, 2)
+    last = pltpu.roll(value, lax.rem(HALO * at + HALO, XC), 2)
+    left[zs, ys, :] = jnp.where(mine, first, left[zs, ys, :])
+    right[zs, ys, :] = jnp.where(mine, last, right[zs, ys, :])
+
+
+def blur_kernel(g, taps, est, wy, wown, wpack, blurred, yown, ypack, win):
+    blur_planes(g, taps, est, wy, wown, wpack, yown, ypack, win)
+
+    def store(z0, y0, value):
+        blurred[0, pl.ds(z0, 16), y0 : y0 + 8, :] = value
+
+    z_sum(win, taps, g * GROUP + pl.program_id(0), False, store)
+
+
+def blur_and_divide_kernel(g, taps, est, wy, wown, wpack, data, ratio, left, right, yown, ypack, win):
+    blur_planes(g, taps, est, wy, wown, wpack, yown, ypack, win)
+
+    def store(z0, y0, value):
+        divide(z0, y0, data, value, ratio, left, right)
+
+    z_sum(win, taps, g * GROUP + pl.program_id(0), False, store)
+
+
+def divide_kernel(data, blurred, ratio, left, right):
+    @pl.loop(0, ZC // 16)
+    def _(b):
+        z0 = pl.multiple_of(b * 16, 16)
+        for y0 in range(0, YC, 8):
+            divide(z0, y0, data, blurred[0, pl.ds(z0, 16), y0 : y0 + 8, :], ratio, left, right)
+
+
+def of_view(g, *shape):
+    return pl.BlockSpec((1,) + shape, lambda v: (v + g * GROUP,) + (0,) * len(shape))
+
+
+OUT_VIEW = pl.BlockSpec((1, ZC, YC, XC), lambda v: (v, 0, 0, 0))
+OUT_SIDES = pl.BlockSpec((ZC // 2, YC, XC), lambda v: (0, 0, 0))
+VIEW_SHAPE = jax.ShapeDtypeStruct((GROUP, ZC, YC, XC), F32)
+SIDES_SHAPE = jax.ShapeDtypeStruct((ZC // 2, YC, XC), F32)
+
+
+def forward(g, taps, window, data, wy, wown, wpack):
+    ins = [
+        pl.BlockSpec(memory_space=pltpu.SMEM),
+        pl.BlockSpec(window.shape, lambda v: (0, 0, 0, 0), pipeline_mode=pl.Buffered(1)),
+        pl.BlockSpec((GROUP * YC, 3 * YK), lambda v: (g, 0), pipeline_mode=pl.Buffered(1)),
+        of_view(g, 2 * XC, 2 * XC),
+        of_view(g, 4, 2 * XC, 2 * XC),
+    ]
+    scratch = [
+        pltpu.VMEM((GROUP, ZW * YC, 2 * XC), BF16),
+        pltpu.VMEM((GROUP, ZW // 4 * YC, 2 * XC), BF16),
+        pltpu.VMEM((ZW, YC, XC), F32),
+    ]
+    if data is None:
+        return pl.pallas_call(
+            functools.partial(blur_kernel, g),
+            name="blur",
+            grid=(GROUP,),
+            out_shape=VIEW_SHAPE,
+            in_specs=ins,
+            out_specs=OUT_VIEW,
+            scratch_shapes=scratch,
+            **params(18),
+        )(taps, window, wy, wown, wpack)
+    return pl.pallas_call(
+        functools.partial(blur_and_divide_kernel, g),
+        name="blur_and_divide",
         grid=(GROUP,),
-        out_shape=(jax.ShapeDtypeStruct((GROUP, ZC, YC, XC), F32), shape, shape),
-        in_specs=[
-            pl.BlockSpec(memory_space=pltpu.SMEM),
-            pl.BlockSpec(window.shape, lambda v: (0, 0, 0, 0), pipeline_mode=pl.Buffered(1)),
-            view,
-            pl.BlockSpec((GROUP * YC, 3 * YK), lambda v: (g, 0), pipeline_mode=pl.Buffered(1)),
-            pl.BlockSpec((1, 2 * XC, 2 * XC), lambda v: (v + g * GROUP, 0, 0)),
-            pl.BlockSpec((1, 4, 2 * XC, 2 * XC), lambda v: (v + g * GROUP, 0, 0, 0)),
-        ],
-        out_specs=(out, pack, pack),
-        scratch_shapes=[
-            pltpu.VMEM((GROUP, ZW * YC, 2 * XC), BF16),
-            pltpu.VMEM((GROUP, ZW // 4 * YC, 2 * XC), BF16),
-            pltpu.VMEM((ZW, YC, XC), F32),
-        ],
+        out_shape=(VIEW_SHAPE, SIDES_SHAPE, SIDES_SHAPE),
+        in_specs=ins + [of_view(g, ZC, YC, XC)],
+        out_specs=(OUT_VIEW, OUT_SIDES, OUT_SIDES),
+        scratch_shapes=scratch,
         **params(24),
-    )(tz[g * GROUP : (g + 1) * GROUP], window, data, wy, wown, wpack)
+    )(taps, window, wy, wown, wpack, data)
+
+
+def divide_by(g, data, blurred):
+    return pl.pallas_call(
+        divide_kernel,
+        name="divide",
+        grid=(GROUP,),
+        out_shape=(VIEW_SHAPE, SIDES_SHAPE, SIDES_SHAPE),
+        in_specs=[of_view(g, ZC, YC, XC), OUT_VIEW],
+        out_specs=(OUT_VIEW, OUT_SIDES, OUT_SIDES),
+        **params(5),
+    )(data, blurred)
 
 
 def adjoint_x_kernel(ratio, before, after, wown, wha, whb, out, top, bottom):
@@ -250,11 +304,11 @@
         sides_kernel,
         name="sides",
         out_shape=jax.ShapeDtypeStruct((first.shape[0] // 4,) + first.shape[1:], F32),
-        **params(2),
+        **params(1),
     )(first, last)
 
 
-def add_logs(taps, value, before, after, win, total):
+def add_logs(g, taps, value, before, after, win, total):
     win[:HALO] = before[0]
     win[HALO : HALO + ZC] = value[0]
     win[HALO + ZC :] = after[0]
@@ -262,23 +316,23 @@
     def store(z0, y0, back):
         total[pl.ds(z0, 16), y0 : y0 + 8, :] += jnp.log(back)
 
-    z_sum(win, taps, pl.program_id(0), store)
-
-
-def first_logs_kernel(taps, value, before, after, total, win):
+    z_sum(win, taps, g * GROUP + pl.program_id(0), True, store)
+
+
+def first_logs_kernel(g, taps, value, before, after, total, win):
     @pl.when(pl.program_id(0) == 0)
     def _():
         total[...] = jnp.zeros_like(total)
 
-    add_logs(taps, value, before, after, win, total)
-
-
-def last_logs_kernel(taps, value, before, after, logs, estimate, out, sides, win, total):
+    add_logs(g, taps, value, before, after, win, total)
+
+
+def last_logs_kernel(g, taps, value, before, after, logs, estimate, out, sides, win, total):
     @pl.when(pl.program_id(0) == 0)
     def _():
         total[...] = logs[...]
 
-    add_logs(taps, value, before, after, win, total)
+    add_logs(g, taps, value, before, after, win, total)
 
     @pl.when(pl.program_id(0) == GROUP - 1)
     def _():
@@ -289,7 +343,7 @@
             sides[q] = pack_sides(out, out, q)
 
 
-def adjoint_z(g, tz, value, before, after, logs, estimate):
+def adjoint_z(g, taps, value, before, after, logs, estimate):
     view = pl.BlockSpec((1, ZC, YC, XC), lambda v: (v, 0, 0, 0))
     face = pl.BlockSpec((1, HALO, YC, XC), lambda v: (v, 0, 0, 0))
     chunk = pl.BlockSpec((ZC, YC, XC), lambda v: (0, 0, 0))
@@ -297,10 +351,10 @@
     chunk_shape = jax.ShapeDtypeStruct((ZC, YC, XC), F32)
     ins = [pl.BlockSpec(memory_space=pltpu.SMEM), view, face, face]
     win = pltpu.VMEM((ZW, YC, XC), F32)
-    args = (tz[g * GROUP : (g + 1) * GROUP], value, before, after)
+    args = (taps, value, before, after)
     if logs is None:
         return pl.pallas_call(
-            first_logs_kernel,
+            functools.partial(first_logs_kernel, g),
             name="first_logs",
             grid=(GROUP,),
             out_shape=chunk_shape,
@@ -310,7 +364,7 @@
             **params(9),
         )(*args)
     return pl.pallas_call(
-        last_logs_kernel,
+        functools.partial(last_logs_kernel, g),
         name="last_logs",
         grid=(GROUP,),
         out_shape=(chunk_shape, jax.ShapeDtypeStruct((ZC // 4, YC, XC), F32)),
@@ -341,7 +395,7 @@
         got.append(lax.ppermute(rows(me ^ k), S, [(i, i ^ k) for i in range(SLABS)]))
     got = jnp.stack(got)
     blocks = jnp.stack([lax.dynamic_index_in_dim(got, me ^ k, 0, keepdims=False) for k in range(SLABS)])
-    return add_z(blocks), own
+    return add_z(blocks)
 
 
 def next_window(chunk, sides):
@@ -354,59 +408,110 @@
     return jnp.concatenate([before, blocks, after], axis=2)
 
 
+def matrices_kernel(taps, fy, fx, fp, ax, sha, shb, ay):
+    v = pl.program_id(0)
+
+    def row_column(rows, columns):
+        return tuple(lax.broadcasted_iota(jnp.int32, (rows, columns), d) for d in range(2))
+
+    def stacked(ref, at, value):
+        hi, lo = split(value)
+        ref[at + (slice(0, XC), slice(0, XC))] = hi
+        ref[at + (slice(0, XC), slice(XC, 2 * XC))] = lo
+        ref[at + (slice(XC, 2 * XC), slice(0, XC))] = hi
+        ref[at + (slice(XC, 2 * XC), slice(XC, 2 * XC))] = jnp.zeros_like(lo)
+
+    def along_y(value):
+        hi, lo = split(value)
+        column = row_column(*value.shape)[1]
+        return jnp.where(column < 2 * YK, hi.astype(F32), lo.astype(F32))
+
+    r, c = row_column(XC, XC)
+    stacked(fx, (0,), banded(taps, v, 0, r - c + RADIUS))
+    stacked(ax, (0,), banded(taps, v, 0, c - r + RADIUS))
+    x_of = jnp.where(r < XC // 2, r % HALO - HALO, r % HALO + XC)
+    packed = banded(taps, v, 0, x_of - c + RADIUS)
+    for j in range(4):
+        stacked(fp, (0, j), jnp.where(r // HALO % 4 == j, packed, 0.0))
+    for side, x_of in enumerate((r % HALO - HALO, r % HALO + XC)):
+        values = banded(taps, v, 0, c - x_of + RADIUS)
+        rows = slice(side * XC, (side + 1) * XC)
+        for half in range(2):
+            hi, lo = split(jnp.where(r // HALO == GROUP * half + v % GROUP, values, 0.0))
+            sha[0, half, rows, :XC] = hi
+            sha[0, half, rows, XC:] = lo
+            shb[0, half, rows, :] = hi
+    r, c = row_column(YC, 3 * YK)
+    fy[...] = along_y(banded(taps, v, 1, c % YK - HALO - r + RADIUS))
+    r, c = row_column(32, 3 * YK)
+    values = banded(taps, v, 1, r - (c % YK - HALO) + RADIUS)
+    ay[0] = along_y(jnp.where(r < YC, values, 0.0)).astype(BF16)
+
+
 def matrices(taps):
-    def rows(n):
-        return jnp.arange(n)[:, None]
-
-    def columns(n):
-        return jnp.arange(n)[None, :]
-
-    def stacked(value):
-        hi, lo = split_constant(value)
-        top = jnp.concatenate([hi, lo], axis=-1)
-        return jnp.concatenate([top, jnp.concatenate([hi, jnp.zeros_like(lo)], axis=-1)], axis=-2)
-
-    lane = rows(XC)
-    fx = stacked(banded(taps[:, 0], lane - columns(XC) + RADIUS))
-    x_of = jnp.where(lane < XC // 2, lane % HALO - HALO, lane % HALO + XC)
-    mine = (lane // HALO % 4)[None] == jnp.arange(4)[:, None, None]
-    fp = stacked(jnp.where(mine[None], banded(taps[:, 0], x_of - columns(XC) + RADIUS)[:, None], 0.0))
-    r = columns(YK) - HALO
-    fy_hi, fy_lo = split_constant(banded(taps[:, 1], r - rows(YC) + RADIUS))
-    fy = jnp.concatenate([fy_hi, fy_hi, fy_lo], axis=2).reshape(VIEWS * YC, 3 * YK)
-    ax = stacked(banded(taps[:, 0], columns(XC) - lane + RADIUS))
-    slot = GROUP * jnp.arange(2)[None, :] + (jnp.arange(VIEWS) % GROUP)[:, None]
-    mine = (lane // HALO)[None, None] == slot[:, :, None, None]
-    sides = [
-        jnp.where(mine, banded(taps[:, 0], columns(XC) - at + RADIUS)[:, None], 0.0)
-        for at in (lane % HALO - HALO, lane % HALO + XC)
+    shapes = [
+        (2 * XC, 2 * XC),
+        (4, 2 * XC, 2 * XC),
+        (2 * XC, 2 * XC),
+        (2, 2 * XC, 2 * XC),
+        (2, 2 * XC, XC),
+        (32, 3 * YK),
     ]
-    sh_hi, sh_lo = split_constant(jnp.concatenate(sides, axis=2))
-    sha = jnp.concatenate([sh_hi, sh_lo], axis=3)
-    ay = jnp.pad(banded(taps[:, 1], rows(YC) - r + RADIUS), ((0, 0), (0, 32 - YC), (0, 0)))
-    ay_hi, ay_lo = split_constant(ay)
-    ay = jnp.concatenate([ay_hi, ay_hi, ay_lo], axis=2)
-    return (fy, fx, fp), (ax, sha, sh_hi), ay
+    fy, fx, fp, ax, sha, shb, ay = pl.pallas_call(
+        matrices_kernel,
+        name="matrices",
+        grid=(VIEWS,),
+        out_shape=[jax.ShapeDtypeStruct((VIEWS * YC, 3 * YK), F32)]
+        + [jax.ShapeDtypeStruct((VIEWS,) + shape, BF16) for shape in shapes],
+        in_specs=[pl.BlockSpec(memory_space=pltpu.SMEM)],
+        out_specs=[pl.BlockSpec((YC, 3 * YK), lambda v: (v, 0))] + [of_view(0, *shape) for shape in shapes],
+        **params(1),
+    )(taps)
+    return (fy, fx, fp), (ax, sha, shb), ay
+
+
+def spread_kernel(got, out):
+    for c in range(VIEWS):
+        for y in range(SLABS):
+            out[:, y * YC : (y + 1) * YC, c * XC : (c + 1) * XC] = got[c, y]
+
+
+def spread(got):
+    planes = 2
+    return pl.pallas_call(
+        spread_kernel,
+        name="spread",
+        grid=(DEPTH // planes,),
+        out_shape=jax.ShapeDtypeStruct((DEPTH, SLABS * YC, VIEWS * XC), F32),
+        in_specs=[pl.BlockSpec((VIEWS, SLABS, planes, YC, XC), lambda b: (0, 0, b, 0, 0))],
+        out_specs=pl.BlockSpec((planes, SLABS * YC, VIEWS * XC), lambda b: (b, 0, 0)),
+        **params(5),
+    )(got)
 
 
 def per_device(views_data, estimate, kernels):
     everyone = lax.all_gather(kernels[0], V, axis=0)
-    taps = everyone / jnp.sum(everyone, axis=-1, keepdims=True)
+    views_data, estimate, everyone = lax.optimization_barrier((views_data, estimate, everyone))
+    taps = (everyone / jnp.sum(everyone, axis=-1, keepdims=True)).reshape(VIEWS, 3 * TAPS)
     w_forward, w_x, w_y = matrices(taps)
-    tz, tz_flipped = taps[:, 2], taps[:, 2, ::-1]
 
     blocks = views_data[0].reshape(DEPTH, SLABS, YC, VIEWS, XC).transpose(3, 1, 0, 2, 4)
     blocks = blocks.reshape(VIEWS * SLABS, DEPTH, YC, XC)
     data = lax.all_to_all(blocks, V + S, 0, 0, tiled=True).reshape(VIEWS, ZC, YC, XC)
-    window, own = first_window(estimate)
+    window = first_window(estimate)
     chunk = window[1 : 1 + SLABS, :DEPTH, HALO : HALO + YC].reshape(ZC, YC, XC)
     groups = range(VIEWS // GROUP)
     for number in range(ITERS):
         if number:
             window = next_window(chunk, sides)
+        if not number:
+            blurred = [forward(g, taps, window, None, *w_forward) for g in groups]
         faces = []
         for g in groups:
-            ratio, left, right = forward(g, tz, window, data, *w_forward)
+            if number:
+                ratio, left, right = forward(g, taps, window, data, *w_forward)
+            else:
+                ratio, left, right = divide_by(g, data, blurred[g])
             faces.append((ratio,) + exchange(left, right, V, VIEWS))
         edges = []
         for g in groups:
@@ -416,13 +521,13 @@
         for g in groups:
             value, low, high = adjoint_y(g, *edges[g], w_y)
             ends.append((value,) + exchange(low, high, "z", 4))
-        logs = adjoint_z(0, tz_flipped, *ends[0], None, None)
-        chunk, sides = adjoint_z(1, tz_flipped, *ends[1], logs, chunk)
+        logs = adjoint_z(0, taps, *ends[0], None, None)
+        chunk, sides = adjoint_z(1, taps, *ends[1], logs, chunk)
 
     parts = chunk.reshape(1, SLABS, DEPTH, YC, XC)
     parts = jnp.broadcast_to(parts, (VIEWS, SLABS, DEPTH, YC, XC)).reshape(VIEWS * SLABS, DEPTH, YC, XC)
     got = lax.all_to_all(parts, V + S, 0, 0, tiled=True).reshape(VIEWS, SLABS, DEPTH, YC, XC)
-    return got.transpose(2, 1, 3, 0, 4).reshape(DEPTH, SLABS * YC, VIEWS * XC)
+    return spread(got)
 
 
 def solution(mesh):

time: 686 us -> 603 us (0.88)
  blocking collectives: 198 us -> 116 us
  other arithmetic: 42.8 us -> 8.93 us
  local copies, waits for them, and re-layouts: 63.5 us -> 32.7 us
  Pallas kernels: 208 us -> 233 us
  waiting for transfers between devices: 65.2 us -> 89.4 us
  starting transfers between devices: 102 us -> 120 us
    all_gather x1, blocking collectives: 105 us -> 26.5 us  [per_device(): everyone = lax.all_gather(kernels[0], V, axis=0)]
    pallas_call x8 -> x12, Pallas kernels: 133 us -> 158 us  [the longest x2 44.6 us: forward(): pl.pallas_call(functools.partial(blur_and_divide_kernel, g), name='blur_a...]
    ppermute x32, starting transfers between devices: 90.7 us -> 108 us  [exchange(): return (lax.ppermute(high, axis, up), lax.ppermute(low, axis, down))]
    broadcast_in_dim x62 -> x0, local copies, waits for them, and re-layouts: 16.7 us -> none  [banded(): result = result + jnp.where(offsets == t, taps[:, t, None, None], 0.0)]
    ppermute x3, waiting for transfers between devices: 0.01 us -> 16.4 us  [first_window(): lax.ppermute(rows(me ^ k), S, [(i, i ^ k) for i in range(SLABS)])]
    convert_element_type x9 -> x0, other arithmetic: 11.2 us -> none  [split_constant(): return (hi.astype(BF16), (value - hi).astype(BF16))]
    concatenate x6 -> x0, other arithmetic: 8.82 us -> none  [the longest x3 5.65 us: stacked(): jnp.concatenate([top, jnp.concatenate([hi, jnp.zeros_like(lo)], axis=-1)]...]
    add x6 -> x0, other arithmetic: 8.34 us -> none  [the longest x4 8.26 us: banded(): result = result + jnp.where(offsets == t, taps[:, t, None, None], 0.0)]
  transfers between devices with their start and end apart: 36 -> 36, of which waited for: 18 -> 18; matrix products, arithmetic and copies ran while one was open for 11% -> 3% of each run, Pallas kernels for 20% -> 28%
where the time goes in v3:
time: 603 us; the launch traced here: 601 us
  Pallas kernels  233 us (39%)
  starting transfers between devices  120 us (20%)
  blocking collectives  116 us (19%)
  waiting for transfers between devices  89.4 us (15%)
  local copies, waits for them, and re-layouts  32.7 us (5%)
  other arithmetic  8.93 us (1%)
    ppermute x32, starting transfers between devices, exchange(): return (lax.ppermute(high, axis, up), lax.ppermute(low, axis, down))  108 us
    all_to_all x1, blocking collectives, per_device(): lax.all_to_all(parts, V + S, 0, 0, tiled=True)  89.7 us
    ppermute x32, waiting for transfers between devices, exchange(): return (lax.ppermute(high, axis, up), lax.ppermute(low, axis, down))  73.1 us
    pallas_call x2, Pallas kernels, forward(): pl.pallas_call(functools.partial(blur_and_divide_kernel, g), name='blur_a...  44.6 us
    pallas_call x2, Pallas kernels, forward(): pl.pallas_call(functools.partial(blur_kernel, g), name='blur', grid=(GROU...  38.2 us
    pallas_call x4, Pallas kernels, adjoint_x(): pl.pallas_call(adjoint_x_kernel, name='adjoint_x', grid=(GROUP,), out_sha...  35.8 us
    pallas_call x4, Pallas kernels, adjoint_y(): pl.pallas_call(adjoint_y_kernel, name='adjoint_y', grid=(GROUP,), out_sha...  35.7 us
    all_gather x1, blocking collectives, per_device(): everyone = lax.all_gather(kernels[0], V, axis=0)  26.5 us
  transfers between devices with their start and end apart: 36, of which 18 were waited for; matrix products, arithmetic and copies ran while one was open for 3% of the time, Pallas kernels for 28%

profile of v3, /device:TPU:1, one launch (start us, length us, event | category | flops | bytes accessed | tf_op | source)
XLA Modules:
  0.0 601.0 jit_solution(2385783985878206879)
XLA Ops:
  0.7 26.5 %all_gather.3 = f32[8,3,31]{2,1,0:T(4,128)S(1)} all-gather(f32[1,3,31]{2,1,0:T(4,128)S(1)} %copy.8), channel_id=1, replica_groups=mesh['yh'=2,'x'=4,'z'=4,'yl'=2,'co'=2] {'yh','x'}, dimensions={0}, use_global_device_ids=true | all-gather | bytes 3348 | tf_op jit(solution)/shard_map/all_gather | solution.py:493
  55.4 16.4 %collective-permute-done.2 = f32[20,56,128]{2,1,0:T(8,128)S(1)} collective-permute-done((f32[20,56,128]{2,1,0:T(8,128)S(1)}, f32[20,56,128]{2,1,0:T(8,128)S(1)}, u32[]{:S(2)}, u32[]{:S(2)}) %collective-permute-start.2) | collective-permute-done | bytes 573472 | tf_op jit(solution)/shard_map/ppermute | solution.py:395
  77.6 11.4 %collective-permute-done.3 = f32[20,56,128]{2,1,0:T(8,128)S(1)} collective-permute-done((f32[20,56,128]{2,1,0:T(8,128)S(1)}, f32[20,56,128]{2,1,0:T(8,128)S(1)}, u32[]{:S(2)}, u32[]{:S(2)}) %collective-permute-start.3) | collective-permute-done | bytes 573472 | tf_op jit(solution)/shard_map/ppermute | solution.py:57
  92.9 10.7 %matrices.1 = (f32[192,192]{1,0:T(8,128)}, bf16[8,256,256]{2,1,0:T(8,128)(2,1)}, bf16[8,4,256,256]{3,2,1,0:T(8,128)(2,1)}, bf16[8,256,256]{2,1,0:T(8,128)(2,1)},...) custom-call(f32[8,93]{1,0:T(8,128)} %reshape.27.taps), custom_call_target="tpu_custom_call" | custom-call | flops 1000000000 | bytes 2000000 | tf_op jit(solution)/shard_map/matrices/pallas_call | solution.py:460
  108.7 19.1 %blur.3.blurred = f32[4,64,24,128]{3,2,1,0:T(8,128)} custom-call(f32[8,93]{1,0:T(8,128)} %reshape.27.taps, f32[6,20,56,128]{3,2,1,0:T(8,128)} %bitcast_dynamic-update-slice_fusion.est, f32[192,192]{1,0:T(8,128)} %get-tuple-element.57.wy, bf16[8,256,256]{2,1,0:T(8,128)(2,1)} %get-tuple-element.58.wown, bf16[8,4,256,256]{3,2,1,0:T(8,128)(2,1)} %get-tuple-element.59.wpack), custom_call_target="tpu_custom_call" | custom-call | flops 17999998976 | bytes 36000000 | tf_op jit(solution)/shard_map/blur/pallas_call | solution.py:176
  127.8 19.1 %blur.2.blurred = f32[4,64,24,128]{3,2,1,0:T(8,128)} custom-call(f32[8,93]{1,0:T(8,128)} %reshape.27.taps, f32[6,20,56,128]{3,2,1,0:T(8,128)} %bitcast_dynamic-update-slice_fusion.est, f32[192,192]{1,0:T(8,128)} %get-tuple-element.57.wy, bf16[8,256,256]{2,1,0:T(8,128)(2,1)} %get-tuple-element.58.wown, bf16[8,4,256,256]{3,2,1,0:T(8,128)(2,1)} %get-tuple-element.59.wpack), custom_call_target="tpu_custom_call" | custom-call | flops 17999998976 | bytes 36000000 | tf_op jit(solution)/shard_map/blur/pallas_call | solution.py:176
  168.4 14.5 %collective-permute-start.5 = (f32[32,24,128]{2,1,0:T(8,128)}, f32[32,24,128]{2,1,0:T(8,128)S(1)}, u32[]{:S(2)}, u32[]{:S(2)}) collective-permute-start(f32[32,24,128]{2,1,0:T(8,128)} %get-tuple-element.61), channel_id=1, source_target_pairs={{0,16},{16,32},{32,48},{48,64},{64,80},{80,96},{96,112},{1,17},{17... | collective-permute-start | bytes 1179656 | tf_op jit(solution)/shard_map/ppermute | solution.py:57
  185.1 8.9 %adjoint_x.5 = (f32[4,64,24,128]{3,2,1,0:T(8,128)}, f32[4,64,16,128]{3,2,1,0:T(8,128)}, f32[4,64,16,128]{3,2,1,0:T(8,128)}) custom-call(f32[4,64,24,128]{3,2,1,0:T(8,128)} %get-tuple-element.73.ratio, f32[32,24,128]{2,1,0:T(8,128)} %copy-done.24, f32[32,24,128]{2,1,0:T(8,128)} %copy-done.25, bf16[8,256,256]{2,1,0:T(8,128)(2,1)} %get-tuple-element.63.wown, ...), custom_call_target="tpu_custom_call" | custom-call | flops 8000000000 | bytes 16000000 | tf_op jit(solution)/shard_map/adjoint_x/pallas_call | solution.py:235
  201.4 9.0 %adjoint_x.4 = (f32[4,64,24,128]{3,2,1,0:T(8,128)}, f32[4,64,16,128]{3,2,1,0:T(8,128)}, f32[4,64,16,128]{3,2,1,0:T(8,128)}) custom-call(f32[4,64,24,128]{3,2,1,0:T(8,128)} %get-tuple-element.60.ratio, f32[32,24,128]{2,1,0:T(8,128)} %copy-done.19, f32[32,24,128]{2,1,0:T(8,128)} %copy-done.21, bf16[8,256,256]{2,1,0:T(8,128)(2,1)} %get-tuple-element.63.wown, ...), custom_call_target="tpu_custom_call" | custom-call | flops 8000000000 | bytes 16000000 | tf_op jit(solution)/shard_map/adjoint_x/pallas_call | solution.py:235
  227.3 9.0 %adjoint_y.5 = (f32[4,64,24,128]{3,2,1,0:T(8,128)}, f32[4,16,24,128]{3,2,1,0:T(8,128)}, f32[4,16,24,128]{3,2,1,0:T(8,128)}) custom-call(f32[4,64,24,128]{3,2,1,0:T(8,128)} %get-tuple-element.76.value, f32[4,64,16,128]{3,2,1,0:T(8,128)} %collective-permute-done.13.before, f32[4,64,16,128]{3,2,1,0:T(8,128)} %collective-permute-done.14.after, ...), custom_call_target="tpu_custom_call" | custom-call | flops 8000000000 | bytes 16000000 | tf_op jit(solution)/shard_map/adjoint_y/pallas_call | solution.py:277
  251.3 8.9 %adjoint_y.4 = (f32[4,64,24,128]{3,2,1,0:T(8,128)}, f32[4,16,24,128]{3,2,1,0:T(8,128)}, f32[4,16,24,128]{3,2,1,0:T(8,128)}) custom-call(f32[4,64,24,128]{3,2,1,0:T(8,128)} %get-tuple-element.66.value, f32[4,64,16,128]{3,2,1,0:T(8,128)} %copy-done.5, f32[4,64,16,128]{3,2,1,0:T(8,128)} %copy-done.6, bf16[8,32,192]{2,1,0:T(8,128)(2,1)} %get-tuple-element.69.wy), custom_call_target="tpu_custom_call" | custom-call | flops 8000000000 | bytes 16000000 | tf_op jit(solution)/shard_map/adjoint_y/pallas_call | solution.py:277
  266.9 9.8 %first_logs.2.logs = f32[64,24,128]{2,1,0:T(8,128)} custom-call(f32[8,93]{1,0:T(8,128)} %reshape.27.taps, f32[4,64,24,128]{3,2,1,0:T(8,128)} %get-tuple-element.79.value, f32[4,16,24,128]{3,2,1,0:T(8,128)} %copy-done.10, f32[4,16,24,128]{3,2,1,0:T(8,128)} %copy-done.11), custom_call_target="tpu_custom_call" | custom-call | flops 8999999488 | bytes 18000000 | tf_op jit(solution)/shard_map/first_logs/pallas_call | solution.py:356
  277.8 12.2 %last_logs.2 = (f32[64,24,128]{2,1,0:T(8,128)}, f32[16,24,128]{2,1,0:T(8,128)}) custom-call(f32[8,93]{1,0:T(8,128)} %reshape.27.taps, f32[4,64,24,128]{3,2,1,0:T(8,128)} %get-tuple-element.70.value, f32[4,16,24,128]{3,2,1,0:T(8,128)} %copy-done.17, f32[4,16,24,128]{3,2,1,0:T(8,128)} %copy-done.15, f32[64,24,128]{2,1,0:T(8,128)} %first_logs.2.logs, ...), custom_call_target="tpu_custom_call" | custom-call | flops 10000000000 | bytes 20000000 | tf_op jit(solution)/shard_map/last_logs/pallas_call | solution.py:366
  290.0 8.3 %collective-permute-start.17 = (f32[16,24,128]{2,1,0:T(8,128)}, f32[16,24,128]{2,1,0:T(8,128)S(1)}, u32[]{:S(2)}, u32[]{:S(2)}) collective-permute-start(f32[16,24,128]{2,1,0:T(8,128)} %get-tuple-element.83), channel_id=1, source_target_pairs={{0,16},{16,32},{32,48},{48,64},{64,80},{80,96},{96,112},{1,17},{17... | collective-permute-start | bytes 589832 | tf_op jit(solution)/shard_map/ppermute | solution.py:57
  324.7 9.1 %collective-permute-done.21 = f32[6,20,16,128]{3,2,1,0:T(8,128)S(1)} collective-permute-done((f32[6,20,16,128]{3,2,1,0:T(8,128)S(1)}, f32[6,20,16,128]{3,2,1,0:T(8,128)S(1)}, u32[]{:S(2)}, u32[]{:S(2)}) %collective-permute-start.21) | collective-permute-done | bytes 983072 | tf_op jit(solution)/shard_map/ppermute | solution.py:57
  340.2 22.3 %blur_and_divide.3 = (f32[4,64,24,128]{3,2,1,0:T(8,128)}, f32[32,24,128]{2,1,0:T(8,128)}, f32[32,24,128]{2,1,0:T(8,128)}) custom-call(f32[8,93]{1,0:T(8,128)} %reshape.27.taps, f32[6,20,56,128]{3,2,1,0:T(8,128)} %pad_maximum_fusion.est, f32[192,192]{1,0:T(8,128)} %get-tuple-element.57.wy, bf16[8,256,256]{2,1,0:T(8,128)(2,1)} %get-tuple-element.58.wown, ...), custom_call_target="tpu_custom_call" | custom-call | flops 24000000000 | bytes 48000000 | tf_op jit(solution)/shard_map/blur_and_divide/pallas_call | solution.py:186
  369.0 22.3 %blur_and_divide.2 = (f32[4,64,24,128]{3,2,1,0:T(8,128)}, f32[32,24,128]{2,1,0:T(8,128)}, f32[32,24,128]{2,1,0:T(8,128)}) custom-call(f32[8,93]{1,0:T(8,128)} %reshape.27.taps, f32[6,20,56,128]{3,2,1,0:T(8,128)} %pad_maximum_fusion.est, f32[192,192]{1,0:T(8,128)} %get-tuple-element.57.wy, bf16[8,256,256]{2,1,0:T(8,128)(2,1)} %get-tuple-element.58.wown, ...), custom_call_target="tpu_custom_call" | custom-call | flops 24000000000 | bytes 48000000 | tf_op jit(solution)/shard_map/blur_and_divide/pallas_call | solution.py:186
  401.5 9.0 %adjoint_x.7 = (f32[4,64,24,128]{3,2,1,0:T(8,128)}, f32[4,64,16,128]{3,2,1,0:T(8,128)}, f32[4,64,16,128]{3,2,1,0:T(8,128)}) custom-call(f32[4,64,24,128]{3,2,1,0:T(8,128)} %get-tuple-element.93.ratio, f32[32,24,128]{2,1,0:T(8,128)} %copy-done.22, f32[32,24,128]{2,1,0:T(8,128)} %copy-done.23, bf16[8,256,256]{2,1,0:T(8,128)(2,1)} %get-tuple-element.63.wown, ...), custom_call_target="tpu_custom_call" | custom-call | flops 8000000000 | bytes 16000000 | tf_op jit(solution)/shard_map/adjoint_x/pallas_call | solution.py:235
  415.8 8.9 %adjoint_x.6 = (f32[4,64,24,128]{3,2,1,0:T(8,128)}, f32[4,64,16,128]{3,2,1,0:T(8,128)}, f32[4,64,16,128]{3,2,1,0:T(8,128)}) custom-call(f32[4,64,24,128]{3,2,1,0:T(8,128)} %get-tuple-element.84.ratio, f32[32,24,128]{2,1,0:T(8,128)} %copy-done.18, f32[32,24,128]{2,1,0:T(8,128)} %copy-done.20, bf16[8,256,256]{2,1,0:T(8,128)(2,1)} %get-tuple-element.63.wown, ...), custom_call_target="tpu_custom_call" | custom-call | flops 8000000000 | bytes 16000000 | tf_op jit(solution)/shard_map/adjoint_x/pallas_call | solution.py:235
  441.7 8.9 %adjoint_y.7 = (f32[4,64,24,128]{3,2,1,0:T(8,128)}, f32[4,16,24,128]{3,2,1,0:T(8,128)}, f32[4,16,24,128]{3,2,1,0:T(8,128)}) custom-call(f32[4,64,24,128]{3,2,1,0:T(8,128)} %get-tuple-element.96.value, f32[4,64,16,128]{3,2,1,0:T(8,128)} %copy-done.7, f32[4,64,16,128]{3,2,1,0:T(8,128)} %copy-done.9, bf16[8,32,192]{2,1,0:T(8,128)(2,1)} %get-tuple-element.69.wy), custom_call_target="tpu_custom_call" | custom-call | flops 8000000000 | bytes 16000000 | tf_op jit(solution)/shard_map/adjoint_y/pallas_call | solution.py:277
  463.0 8.9 %adjoint_y.6 = (f32[4,64,24,128]{3,2,1,0:T(8,128)}, f32[4,16,24,128]{3,2,1,0:T(8,128)}, f32[4,16,24,128]{3,2,1,0:T(8,128)}) custom-call(f32[4,64,24,128]{3,2,1,0:T(8,128)} %get-tuple-element.87.value, f32[4,64,16,128]{3,2,1,0:T(8,128)} %copy-done.8, f32[4,64,16,128]{3,2,1,0:T(8,128)} %collective-permute-done.26.after, bf16[8,32,192]{2,1,0:T(8,128)(2,1)} %get-tuple-element.69.wy), custom_call_target="tpu_custom_call" | custom-call | flops 8000000000 | bytes 16000000 | tf_op jit(solution)/shard_map/adjoint_y/pallas_call | solution.py:277
  477.9 9.9 %first_logs.3.logs = f32[64,24,128]{2,1,0:T(8,128)} custom-call(f32[8,93]{1,0:T(8,128)} %reshape.27.taps, f32[4,64,24,128]{3,2,1,0:T(8,128)} %get-tuple-element.99.value, f32[4,16,24,128]{3,2,1,0:T(8,128)} %copy-done.12, f32[4,16,24,128]{3,2,1,0:T(8,128)} %copy-done.13), custom_call_target="tpu_custom_call" | custom-call | flops 8999999488 | bytes 18000000 | tf_op jit(solution)/shard_map/first_logs/pallas_call | solution.py:356
  489.3 12.2 %last_logs.3 = (f32[64,24,128]{2,1,0:T(8,128)}, f32[16,24,128]{2,1,0:T(8,128)}) custom-call(f32[8,93]{1,0:T(8,128)} %reshape.27.taps, f32[4,64,24,128]{3,2,1,0:T(8,128)} %get-tuple-element.90.value, f32[4,16,24,128]{3,2,1,0:T(8,128)} %copy-done.14, f32[4,16,24,128]{3,2,1,0:T(8,128)} %copy-done.16, f32[64,24,128]{2,1,0:T(8,128)} %first_logs.3.logs, ...), custom_call_target="tpu_custom_call" | custom-call | flops 10000000000 | bytes 20000000 | tf_op jit(solution)/shard_map/last_logs/pallas_call | solution.py:366
  503.4 89.7 %all_to_all.10 = f32[32,16,24,128]{3,2,1,0:T(8,128)} all-to-all(f32[32,16,24,128]{3,2,1,0:T(8,128)S(1)} %bitcast.35), channel_id=1, replica_groups=mesh['yh'=2,'x'=4,'z'=4,'yl'=2,'co'=2] {'yh','x','yl','co'}, dimensions={0} | all-to-all | bytes 12582912 | tf_op jit(solution)/shard_map/all_to_all | solution.py:529
  (147 shorter events, 215.5 us)
Async XLA Ops:
  35.2 20.2 %collective-permute-start = (f32[20,56,128]{2,1,0:T(8,128)}, f32[20,56,128]{2,1,0:T(8,128)S(1)}, u32[]{:S(2)}, u32[]{:S(2)}) collective-permute-start(f32[20,56,128]{2,1,0:T(8,128)} %get-tuple-element.115), channel_id=1, source_target_pairs={{0,1},{1,0},{2,3},{3,2},{4,5},{5,4},{6,7},{7,6},{8,9},{9,8},{10,11... | collective-permute-start | bytes 1720328 | tf_op jit(solution)/shard_map/ppermute | solution.py:395
  41.2 30.5 %collective-permute-start.2 = (f32[20,56,128]{2,1,0:T(8,128)S(1)}, f32[20,56,128]{2,1,0:T(8,128)S(1)}, u32[]{:S(2)}, u32[]{:S(2)}) collective-permute-start(f32[20,56,128]{2,1,0:T(8,128)S(1)} %get-tuple-element.117), channel_id=1, source_target_pairs={{0,3},{1,2},{2,1},{3,0},{4,7},{5,6},{6,5},{7,4},{8,11},{9,10},{10,... | collective-permute-start | bytes 1720328 | tf_op jit(solution)/shard_map/ppermute | solution.py:395
  50.3 96.6 %all-to-all-start = ((f32[32,16,24,128]{3,2,1,0:T(8,128)}), f32[32,16,24,128]{3,2,1,0:T(8,128)}, u32[]{:S(2)}, u32[]{:S(2)}) async-start(f32[32,16,24,128]{3,2,1,0:T(8,128)} %bitcast.34), calls=%async_computation | async-start | bytes 12582912 | tf_op jit(solution)/shard_map/all_to_all | solution.py:500
  90.9 15.9 %collective-permute-start.4 = (f32[20,56,128]{2,1,0:T(8,128)S(1)}, f32[20,56,128]{2,1,0:T(8,128)}, u32[]{:S(2)}, u32[]{:S(2)}) collective-permute-start(f32[20,56,128]{2,1,0:T(8,128)S(1)} %bitcast.45), channel_id=1, source_target_pairs={{4,0},{8,4},{12,8},{5,1},{9,5},{13,9},{6,2},{10,6},{14,10},{7,3},{... | collective-permute-start | bytes 1720328 | tf_op jit(solution)/shard_map/ppermute | solution.py:57
  153.4 30.8 %collective-permute-start.11 = (f32[32,24,128]{2,1,0:T(8,128)}, f32[32,24,128]{2,1,0:T(8,128)S(1)}, u32[]{:S(2)}, u32[]{:S(2)}) collective-permute-start(f32[32,24,128]{2,1,0:T(8,128)} %get-tuple-element.74), channel_id=1, source_target_pairs={{0,16},{16,32},{32,48},{48,64},{64,80},{80,96},{96,112},{1,17},{17... | collective-permute-start | bytes 1179656 | tf_op jit(solution)/shard_map/ppermute | solution.py:57
  160.6 23.6 %collective-permute-start.12 = (f32[32,24,128]{2,1,0:T(8,128)}, f32[32,24,128]{2,1,0:T(8,128)S(1)}, u32[]{:S(2)}, u32[]{:S(2)}) collective-permute-start(f32[32,24,128]{2,1,0:T(8,128)} %get-tuple-element.75), channel_id=1, source_target_pairs={{16,0},{32,16},{48,32},{64,48},{80,64},{96,80},{112,96},{17,1},{33... | collective-permute-start | bytes 1179656 | tf_op jit(solution)/shard_map/ppermute | solution.py:57
  168.4 32.1 %collective-permute-start.5 = (f32[32,24,128]{2,1,0:T(8,128)}, f32[32,24,128]{2,1,0:T(8,128)S(1)}, u32[]{:S(2)}, u32[]{:S(2)}) collective-permute-start(f32[32,24,128]{2,1,0:T(8,128)} %get-tuple-element.61), channel_id=1, source_target_pairs={{0,16},{16,32},{32,48},{48,64},{64,80},{80,96},{96,112},{1,17},{17... | collective-permute-start | bytes 1179656 | tf_op jit(solution)/shard_map/ppermute | solution.py:57
  182.9 17.7 %collective-permute-start.6 = (f32[32,24,128]{2,1,0:T(8,128)}, f32[32,24,128]{2,1,0:T(8,128)S(1)}, u32[]{:S(2)}, u32[]{:S(2)}) collective-permute-start(f32[32,24,128]{2,1,0:T(8,128)} %get-tuple-element.62), channel_id=1, source_target_pairs={{16,0},{32,16},{48,32},{64,48},{80,64},{96,80},{112,96},{17,1},{33... | collective-permute-start | bytes 1179656 | tf_op jit(solution)/shard_map/ppermute | solution.py:57
  194.0 27.8 %collective-permute-start.13 = (f32[4,64,16,128]{3,2,1,0:T(8,128)}, f32[4,64,16,128]{3,2,1,0:T(8,128)}, u32[]{:S(2)}, u32[]{:S(2)}) collective-permute-start(f32[4,64,16,128]{3,2,1,0:T(8,128)} %get-tuple-element.77), channel_id=1, source_target_pairs={{0,1},{1,2},{2,3},{4,5},{5,6},{6,7},{8,9},{9,10},{10,11},{12,13},{... | collective-permute-start | bytes 6291464 | tf_op jit(solution)/shard_map/ppermute | solution.py:57
  198.6 28.7 %collective-permute-start.14 = (f32[4,64,16,128]{3,2,1,0:T(8,128)}, f32[4,64,16,128]{3,2,1,0:T(8,128)}, u32[]{:S(2)}, u32[]{:S(2)}) collective-permute-start(f32[4,64,16,128]{3,2,1,0:T(8,128)} %get-tuple-element.78), channel_id=1, source_target_pairs={{1,0},{2,1},{3,2},{5,4},{6,5},{7,6},{9,8},{10,9},{11,10},{13,12},{... | collective-permute-start | bytes 6291464 | tf_op jit(solution)/shard_map/ppermute | solution.py:57
  210.4 33.9 %collective-permute-start.7 = (f32[4,64,16,128]{3,2,1,0:T(8,128)}, f32[4,64,16,128]{3,2,1,0:T(8,128)S(1)}, u32[]{:S(2)}, u32[]{:S(2)}) collective-permute-start(f32[4,64,16,128]{3,2,1,0:T(8,128)} %get-tuple-element.67), channel_id=1, source_target_pairs={{0,1},{1,2},{2,3},{4,5},{5,6},{6,7},{8,9},{9,10},{10,11},{12,13},{... | collective-permute-start | bytes 6291464 | tf_op jit(solution)/shard_map/ppermute | solution.py:57
  214.9 35.0 %collective-permute-start.8 = (f32[4,64,16,128]{3,2,1,0:T(8,128)}, f32[4,64,16,128]{3,2,1,0:T(8,128)S(1)}, u32[]{:S(2)}, u32[]{:S(2)}) collective-permute-start(f32[4,64,16,128]{3,2,1,0:T(8,128)} %get-tuple-element.68), channel_id=1, source_target_pairs={{1,0},{2,1},{3,2},{5,4},{6,5},{7,6},{9,8},{10,9},{11,10},{13,12},{... | collective-permute-start | bytes 6291464 | tf_op jit(solution)/shard_map/ppermute | solution.py:57
  236.3 29.3 %collective-permute-start.15 = (f32[4,16,24,128]{3,2,1,0:T(8,128)}, f32[4,16,24,128]{3,2,1,0:T(8,128)S(1)}, u32[]{:S(2)}, u32[]{:S(2)}) collective-permute-start(f32[4,16,24,128]{3,2,1,0:T(8,128)} %get-tuple-element.80), channel_id=1, source_target_pairs={{0,4},{4,8},{8,12},{1,5},{5,9},{9,13},{2,6},{6,10},{10,14},{3,7},{... | collective-permute-start | bytes 2359304 | tf_op jit(solution)/shard_map/ppermute | solution.py:57
  239.8 25.8 %collective-permute-start.16 = (f32[4,16,24,128]{3,2,1,0:T(8,128)}, f32[4,16,24,128]{3,2,1,0:T(8,128)S(1)}, u32[]{:S(2)}, u32[]{:S(2)}) collective-permute-start(f32[4,16,24,128]{3,2,1,0:T(8,128)} %get-tuple-element.81), channel_id=1, source_target_pairs={{4,0},{8,4},{12,8},{5,1},{9,5},{13,9},{6,2},{10,6},{14,10},{7,3},{... | collective-permute-start | bytes 2359304 | tf_op jit(solution)/shard_map/ppermute | solution.py:57
  260.2 16.5 %collective-permute-start.10 = (f32[4,16,24,128]{3,2,1,0:T(8,128)}, f32[4,16,24,128]{3,2,1,0:T(8,128)S(1)}, u32[]{:S(2)}, u32[]{:S(2)}) collective-permute-start(f32[4,16,24,128]{3,2,1,0:T(8,128)} %get-tuple-element.72), channel_id=1, source_target_pairs={{4,0},{8,4},{12,8},{5,1},{9,5},{13,9},{6,2},{10,6},{14,10},{7,3},{... | collective-permute-start | bytes 2359304 | tf_op jit(solution)/shard_map/ppermute | solution.py:57
  362.5 38.1 %collective-permute-start.29 = (f32[32,24,128]{2,1,0:T(8,128)}, f32[32,24,128]{2,1,0:T(8,128)S(1)}, u32[]{:S(2)}, u32[]{:S(2)}) collective-permute-start(f32[32,24,128]{2,1,0:T(8,128)} %get-tuple-element.94), channel_id=1, source_target_pairs={{0,16},{16,32},{32,48},{48,64},{64,80},{80,96},{96,112},{1,17},{17... | collective-permute-start | bytes 1179656 | tf_op jit(solution)/shard_map/ppermute | solution.py:57
  367.7 32.9 %collective-permute-start.30 = (f32[32,24,128]{2,1,0:T(8,128)}, f32[32,24,128]{2,1,0:T(8,128)S(1)}, u32[]{:S(2)}, u32[]{:S(2)}) collective-permute-start(f32[32,24,128]{2,1,0:T(8,128)} %get-tuple-element.95), channel_id=1, source_target_pairs={{16,0},{32,16},{48,32},{64,48},{80,64},{96,80},{112,96},{17,1},{33... | collective-permute-start | bytes 1179656 | tf_op jit(solution)/shard_map/ppermute | solution.py:57
  391.3 23.6 %collective-permute-start.23 = (f32[32,24,128]{2,1,0:T(8,128)}, f32[32,24,128]{2,1,0:T(8,128)S(1)}, u32[]{:S(2)}, u32[]{:S(2)}) collective-permute-start(f32[32,24,128]{2,1,0:T(8,128)} %get-tuple-element.85), channel_id=1, source_target_pairs={{0,16},{16,32},{32,48},{48,64},{64,80},{80,96},{96,112},{1,17},{17... | collective-permute-start | bytes 1179656 | tf_op jit(solution)/shard_map/ppermute | solution.py:57
  410.4 25.7 %collective-permute-start.31 = (f32[4,64,16,128]{3,2,1,0:T(8,128)}, f32[4,64,16,128]{3,2,1,0:T(8,128)S(1)}, u32[]{:S(2)}, u32[]{:S(2)}) collective-permute-start(f32[4,64,16,128]{3,2,1,0:T(8,128)} %get-tuple-element.97), channel_id=1, source_target_pairs={{0,1},{1,2},{2,3},{4,5},{5,6},{6,7},{8,9},{9,10},{10,11},{12,13},{... | collective-permute-start | bytes 6291464 | tf_op jit(solution)/shard_map/ppermute | solution.py:57
  412.8 27.6 %collective-permute-start.32 = (f32[4,64,16,128]{3,2,1,0:T(8,128)}, f32[4,64,16,128]{3,2,1,0:T(8,128)S(1)}, u32[]{:S(2)}, u32[]{:S(2)}) collective-permute-start(f32[4,64,16,128]{3,2,1,0:T(8,128)} %get-tuple-element.98), channel_id=1, source_target_pairs={{1,0},{2,1},{3,2},{5,4},{6,5},{7,6},{9,8},{10,9},{11,10},{13,12},{... | collective-permute-start | bytes 6291464 | tf_op jit(solution)/shard_map/ppermute | solution.py:57
  424.7 33.8 %collective-permute-start.25 = (f32[4,64,16,128]{3,2,1,0:T(8,128)}, f32[4,64,16,128]{3,2,1,0:T(8,128)S(1)}, u32[]{:S(2)}, u32[]{:S(2)}) collective-permute-start(f32[4,64,16,128]{3,2,1,0:T(8,128)} %get-tuple-element.88), channel_id=1, source_target_pairs={{0,1},{1,2},{2,3},{4,5},{5,6},{6,7},{8,9},{9,10},{10,11},{12,13},{... | collective-permute-start | bytes 6291464 | tf_op jit(solution)/shard_map/ppermute | solution.py:57
  428.2 34.7 %collective-permute-start.26 = (f32[4,64,16,128]{3,2,1,0:T(8,128)}, f32[4,64,16,128]{3,2,1,0:T(8,128)}, u32[]{:S(2)}, u32[]{:S(2)}) collective-permute-start(f32[4,64,16,128]{3,2,1,0:T(8,128)} %get-tuple-element.89), channel_id=1, source_target_pairs={{1,0},{2,1},{3,2},{5,4},{6,5},{7,6},{9,8},{10,9},{11,10},{13,12},{... | collective-permute-start | bytes 6291464 | tf_op jit(solution)/shard_map/ppermute | solution.py:57
  450.7 26.1 %collective-permute-start.33 = (f32[4,16,24,128]{3,2,1,0:T(8,128)}, f32[4,16,24,128]{3,2,1,0:T(8,128)S(1)}, u32[]{:S(2)}, u32[]{:S(2)}) collective-permute-start(f32[4,16,24,128]{3,2,1,0:T(8,128)} %get-tuple-element.100), channel_id=1, source_target_pairs={{0,4},{4,8},{8,12},{1,5},{5,9},{9,13},{2,6},{6,10},{10,14},{3,7},{... | collective-permute-start | bytes 2359304 | tf_op jit(solution)/shard_map/ppermute | solution.py:57
  454.0 22.7 %collective-permute-start.34 = (f32[4,16,24,128]{3,2,1,0:T(8,128)}, f32[4,16,24,128]{3,2,1,0:T(8,128)S(1)}, u32[]{:S(2)}, u32[]{:S(2)}) collective-permute-start(f32[4,16,24,128]{3,2,1,0:T(8,128)} %get-tuple-element.101), channel_id=1, source_target_pairs={{4,0},{8,4},{12,8},{5,1},{9,5},{13,9},{6,2},{10,6},{14,10},{7,3},{... | collective-permute-start | bytes 2359304 | tf_op jit(solution)/shard_map/ppermute | solution.py:57
  (38 other events, 238.2 us)

commit v4 on v3

--- a/solution.py
+++ b/solution.py
@@ -114,13 +114,14 @@
     value = recorded[0, zs, ys, :] / blurred
     ratio[0, zs, ys, :] = value
     half = z0 // (ZC // 2)
+    slot = lax.broadcasted_iota(jnp.int32, value.shape, 2) // HALO
+    zs = pl.ds(z0 - half * (ZC // 2), 16)
+    at = GROUP * (1 - half) + v
+    first = pltpu.roll(value, HALO * at, 2)
+    left[zs, ys, :] = jnp.where(slot == at, first, left[zs, ys, :])
     at = GROUP * half + v
-    mine = lax.broadcasted_iota(jnp.int32, value.shape, 2) // HALO == at
-    zs = pl.ds(z0 - half * (ZC // 2), 16)
-    first = pltpu.roll(value, HALO * at, 2)
     last = pltpu.roll(value, lax.rem(HALO * at + HALO, XC), 2)
-    left[zs, ys, :] = jnp.where(mine, first, left[zs, ys, :])
-    right[zs, ys, :] = jnp.where(mine, last, right[zs, ys, :])
+    right[zs, ys, :] = jnp.where(slot == at, last, right[zs, ys, :])
 
 
 def blur_kernel(g, taps, est, wy, wown, wpack, blurred, yown, ypack, win):
@@ -207,8 +208,9 @@
     )(data, blurred)
 
 
-def adjoint_x_kernel(ratio, before, after, wown, wha, whb, out, top, bottom):
+def adjoint_x_kernel(ratio, before, after, wown, wside, out, top, bottom):
     planes = 16
+    low_lanes = lax.broadcasted_iota(jnp.int32, (planes * YC, XC), 1) < XC // 2
 
     @pl.loop(0, ZC // planes)
     def _(b):
@@ -217,17 +219,18 @@
         zs = pl.ds(pl.multiple_of(b * planes, planes), planes)
         hs = pl.ds(pl.multiple_of((b - 2 * half) * planes, planes), planes)
         hi, lo = split(ratio[0, zs].reshape(rows, XC))
-        sides = jnp.concatenate([before[hs].reshape(rows, XC), after[hs].reshape(rows, XC)], axis=1)
-        shi, slo = split(sides)
-        two = dot(jnp.concatenate([hi, lo], axis=1), wown[0]) + dot(shi, wha[0, half])
-        value = two[:, :XC] + two[:, XC:] + dot(slo, whb[0, half])
+        is_before = low_lanes == (half == 0)
+        shi, slo = split(jnp.where(is_before, before[hs].reshape(rows, XC), after[hs].reshape(rows, XC)))
+        two = dot(jnp.concatenate([hi, lo], axis=1), wown[0])
+        two = two + dot(jnp.concatenate([shi, slo], axis=1), wside[0, half])
+        value = two[:, :XC] + two[:, XC:]
         value = value.reshape(planes, YC, XC)
         out[0, zs] = value
         top[0, zs] = value[:, :HALO]
         bottom[0, zs] = value[:, YC - HALO :]
 
 
-def adjoint_x(g, ratio, before, after, wown, wha, whb):
+def adjoint_x(g, ratio, before, after, wown, wside):
     view = pl.BlockSpec((1, ZC, YC, XC), lambda v: (v, 0, 0, 0))
     pack = pl.BlockSpec((ZC // 2, YC, XC), lambda v: (0, 0, 0))
     edge = pl.BlockSpec((1, ZC, HALO, XC), lambda v: (v, 0, 0, 0))
@@ -243,11 +246,10 @@
             pack,
             pl.BlockSpec((1, 2 * XC, 2 * XC), lambda v: (v + g * GROUP, 0, 0)),
             pl.BlockSpec((1, 2, 2 * XC, 2 * XC), lambda v: (v + g * GROUP, 0, 0, 0)),
-            pl.BlockSpec((1, 2, 2 * XC, XC), lambda v: (v + g * GROUP, 0, 0, 0)),
         ],
         out_specs=(view, edge, edge),
         **params(8),
-    )(ratio, before, after, wown, wha, whb)
+    )(ratio, before, after, wown, wside)
 
 
 def adjoint_y_kernel(value, before, after, wy, out, low, high):
@@ -261,9 +263,10 @@
         z = 2 * b
         rows = jnp.concatenate([pair(before, z), pair(value, z), pair(after, z), empty], axis=0)
         hi, lo = split(rows)
-        got = dot(wy[0], jnp.concatenate([hi, lo, hi], axis=0))
-        out[0, z] = got[:YC, :XC]
-        out[0, z + 1] = got[:YC, XC:]
+        got = dot(wy[0], jnp.concatenate([hi, lo], axis=0))
+        got = got[:YC] + got[32 : 32 + YC]
+        out[0, z] = got[:, :XC]
+        out[0, z + 1] = got[:, XC:]
 
     low[0] = out[0, :HALO]
     high[0] = out[0, ZC - HALO :]
@@ -279,7 +282,7 @@
         name="adjoint_y",
         grid=(GROUP,),
         out_shape=(jax.ShapeDtypeStruct((GROUP, ZC, YC, XC), F32), face_shape, face_shape),
-        in_specs=[view, edge, edge, pl.BlockSpec((1, 32, 3 * YK), lambda v: (v + g * GROUP, 0, 0))],
+        in_specs=[view, edge, edge, of_view(g, 64, 2 * YK)],
         out_specs=(view, face, face),
         **params(8),
     )(value, before, after, wy)
@@ -375,6 +378,14 @@
     )(*args, logs, estimate)
 
 
+def gather_views(row):
+    mine = jnp.arange(VIEWS)[:, None, None] == lax.axis_index(V)
+    rows = jnp.where(mine, row[None], 0.0)
+    for k in (1, 2, 4):
+        rows = rows + lax.ppermute(rows, V, [(i, i ^ k) for i in range(VIEWS)])
+    return rows
+
+
 def add_z(blocks):
     before, after = exchange(blocks[0], blocks[SLABS - 1], "z", 4)
     return jnp.concatenate([before[None], blocks, after[None]], axis=0)
@@ -408,7 +419,7 @@
     return jnp.concatenate([before, blocks, after], axis=2)
 
 
-def matrices_kernel(taps, fy, fx, fp, ax, sha, shb, ay):
+def matrices_kernel(taps, fy, fx, fp, ax, side, ay):
     v = pl.program_id(0)
 
     def row_column(rows, columns):
@@ -433,19 +444,18 @@
     packed = banded(taps, v, 0, x_of - c + RADIUS)
     for j in range(4):
         stacked(fp, (0, j), jnp.where(r // HALO % 4 == j, packed, 0.0))
-    for side, x_of in enumerate((r % HALO - HALO, r % HALO + XC)):
-        values = banded(taps, v, 0, c - x_of + RADIUS)
-        rows = slice(side * XC, (side + 1) * XC)
-        for half in range(2):
-            hi, lo = split(jnp.where(r // HALO == GROUP * half + v % GROUP, values, 0.0))
-            sha[0, half, rows, :XC] = hi
-            sha[0, half, rows, XC:] = lo
-            shb[0, half, rows, :] = hi
+    before = banded(taps, v, 0, c - (r % HALO - HALO) + RADIUS)
+    after = banded(taps, v, 0, c - (r % HALO + XC) + RADIUS)
+    for half in range(2):
+        value = jnp.where(r // HALO == GROUP * half + v % GROUP, before, 0.0)
+        value = jnp.where(r // HALO == GROUP * (1 - half) + v % GROUP, after, value)
+        stacked(side, (0, half), value)
     r, c = row_column(YC, 3 * YK)
     fy[...] = along_y(banded(taps, v, 1, c % YK - HALO - r + RADIUS))
-    r, c = row_column(32, 3 * YK)
-    values = banded(taps, v, 1, r - (c % YK - HALO) + RADIUS)
-    ay[0] = along_y(jnp.where(r < YC, values, 0.0)).astype(BF16)
+    r, c = row_column(64, 2 * YK)
+    hi, lo = split(banded(taps, v, 1, r % 32 - (c % YK - HALO) + RADIUS))
+    value = jnp.where(r < 32, hi.astype(F32), jnp.where(c < YK, lo.astype(F32), 0.0))
+    ay[0] = value.astype(BF16)
 
 
 def matrices(taps):
@@ -454,10 +464,9 @@
         (4, 2 * XC, 2 * XC),
         (2 * XC, 2 * XC),
         (2, 2 * XC, 2 * XC),
-        (2, 2 * XC, XC),
-        (32, 3 * YK),
+        (64, 2 * YK),
     ]
-    fy, fx, fp, ax, sha, shb, ay = pl.pallas_call(
+    fy, fx, fp, ax, side, ay = pl.pallas_call(
         matrices_kernel,
         name="matrices",
         grid=(VIEWS,),
@@ -467,7 +476,7 @@
         out_specs=[pl.BlockSpec((YC, 3 * YK), lambda v: (v, 0))] + [of_view(0, *shape) for shape in shapes],
         **params(1),
     )(taps)
-    return (fy, fx, fp), (ax, sha, shb), ay
+    return (fy, fx, fp), (ax, side), ay
 
 
 def spread_kernel(got, out):
@@ -490,14 +499,13 @@
 
 
 def per_device(views_data, estimate, kernels):
-    everyone = lax.all_gather(kernels[0], V, axis=0)
-    views_data, estimate, everyone = lax.optimization_barrier((views_data, estimate, everyone))
+    everyone = gather_views(kernels[0])
+    blocks = views_data[0].reshape(DEPTH, SLABS, YC, VIEWS, XC).transpose(3, 1, 0, 2, 4)
+    blocks = blocks.reshape(VIEWS * SLABS, DEPTH, YC, XC)
+    blocks, everyone = lax.optimization_barrier((blocks, everyone))
+    data = lax.all_to_all(blocks, V + S, 0, 0, tiled=True).reshape(VIEWS, ZC, YC, XC)
     taps = (everyone / jnp.sum(everyone, axis=-1, keepdims=True)).reshape(VIEWS, 3 * TAPS)
     w_forward, w_x, w_y = matrices(taps)
-
-    blocks = views_data[0].reshape(DEPTH, SLABS, YC, VIEWS, XC).transpose(3, 1, 0, 2, 4)
-    blocks = blocks.reshape(VIEWS * SLABS, DEPTH, YC, XC)
-    data = lax.all_to_all(blocks, V + S, 0, 0, tiled=True).reshape(VIEWS, ZC, YC, XC)
     window = first_window(estimate)
     chunk = window[1 : 1 + SLABS, :DEPTH, HALO : HALO + YC].reshape(ZC, YC, XC)
     groups = range(VIEWS // GROUP)

time: 603 us -> 569 us (0.944)
  blocking collectives: 116 us -> 89.7 us
  starting transfers between devices: 120 us -> 111 us
  waiting for transfers between devices: 89.4 us -> 95.7 us
    all_gather x1 -> x0, blocking collectives: 26.5 us -> none  [per_device(): everyone = lax.all_gather(kernels[0], V, axis=0)]
    ppermute x0 -> x3, waiting for transfers between devices: none -> 16.5 us  [gather_views(): rows = rows + lax.ppermute(rows, V, [(i, i ^ k) for i in range(VIEWS)])]
    ppermute x3, waiting for transfers between devices: 16.4 us -> 0.01 us  [first_window(): lax.ppermute(rows(me ^ k), S, [(i, i ^ k) for i in range(SLABS)])]
    ppermute x32, starting transfers between devices: 108 us -> 94.7 us  [exchange(): return (lax.ppermute(high, axis, up), lax.ppermute(low, axis, down))]
    ppermute x0 -> x3, starting transfers between devices: none -> 7.86 us  [gather_views(): rows = rows + lax.ppermute(rows, V, [(i, i ^ k) for i in range(VIEWS)])]
    unnamed x59 -> x55, local copies, waits for them, and re-layouts: 21.1 us -> 19.5 us
  transfers between devices with their start and end apart: 36 -> 39, of which waited for: 18 -> 20; matrix products, arithmetic and copies ran while one was open for 3% -> 4% of each run, Pallas kernels for 28% -> 30%
where the time goes in v4:
time: 569 us; the launch traced here: 567 us
  Pallas kernels  229 us (40%)
  starting transfers between devices  111 us (20%)
  waiting for transfers between devices  95.7 us (17%)
  blocking collectives  89.7 us (16%)
  local copies, waits for them, and re-layouts  31.2 us (5%)
  other arithmetic  9.13 us (2%)
    ppermute x32, starting transfers between devices, exchange(): return (lax.ppermute(high, axis, up), lax.ppermute(low, axis, down))  94.7 us
    all_to_all x1, blocking collectives, per_device(): lax.all_to_all(parts, V + S, 0, 0, tiled=True)  89.7 us
    ppermute x32, waiting for transfers between devices, exchange(): return (lax.ppermute(high, axis, up), lax.ppermute(low, axis, down))  75 us
    pallas_call x2, Pallas kernels, forward(): pl.pallas_call(functools.partial(blur_and_divide_kernel, g), name='blur_a...  44.7 us
    pallas_call x2, Pallas kernels, forward(): pl.pallas_call(functools.partial(blur_kernel, g), name='blur', grid=(GROU...  38.1 us
    pallas_call x4, Pallas kernels, adjoint_y(): pl.pallas_call(adjoint_y_kernel, name='adjoint_y', grid=(GROUP,), out_sha...  35.2 us
    pallas_call x4, Pallas kernels, adjoint_x(): pl.pallas_call(adjoint_x_kernel, name='adjoint_x', grid=(GROUP,), out_sha...  32.6 us
    pallas_call x2, Pallas kernels, adjoint_z(): pl.pallas_call(functools.partial(last_logs_kernel, g), name='last_logs',...  24.5 us
  transfers between devices with their start and end apart: 39, of which 20 were waited for; matrix products, arithmetic and copies ran while one was open for 4% of the time, Pallas kernels for 30%

profile of v4, /device:TPU:1, one launch (start us, length us, event | category | flops | bytes accessed | tf_op | source)
XLA Modules:
  0.0 566.8 jit_solution(1499960115713702744)
XLA Ops:
  27.9 16.5 %collective-permute-done.2 = f32[8,3,31]{2,1,0:T(4,128)S(1)} collective-permute-done((f32[8,3,31]{2,1,0:T(4,128)S(1)}, f32[8,3,31]{2,1,0:T(4,128)S(1)}, u32[]{:S(2)}, u32[]{:S(2)}) %collective-permute-start.2) | collective-permute-done | bytes 3008 | tf_op jit(solution)/shard_map/ppermute | solution.py:385
  55.9 11.9 %collective-permute-done.6 = f32[20,56,128]{2,1,0:T(8,128)S(1)} collective-permute-done((f32[20,56,128]{2,1,0:T(8,128)S(1)}, f32[20,56,128]{2,1,0:T(8,128)S(1)}, u32[]{:S(2)}, u32[]{:S(2)}) %collective-permute-start.6) | collective-permute-done | bytes 573472 | tf_op jit(solution)/shard_map/ppermute | solution.py:57
  71.8 10.8 %matrices.1 = (f32[192,192]{1,0:T(8,128)}, bf16[8,256,256]{2,1,0:T(8,128)(2,1)}, bf16[8,4,256,256]{3,2,1,0:T(8,128)(2,1)}, bf16[8,256,256]{2,1,0:T(8,128)(2,1)},...) custom-call(f32[8,93]{1,0:T(8,128)} %reshape.33.taps), custom_call_target="tpu_custom_call" | custom-call | flops 1000000000 | bytes 2000000 | tf_op jit(solution)/shard_map/matrices/pallas_call | solution.py:469
  88.1 19.0 %blur.3.blurred = f32[4,64,24,128]{3,2,1,0:T(8,128)} custom-call(f32[8,93]{1,0:T(8,128)} %reshape.33.taps, f32[6,20,56,128]{3,2,1,0:T(8,128)} %bitcast_dynamic-update-slice_fusion.est, f32[192,192]{1,0:T(8,128)} %get-tuple-element.54.wy, bf16[8,256,256]{2,1,0:T(8,128)(2,1)} %get-tuple-element.55.wown, bf16[8,4,256,256]{3,2,1,0:T(8,128)(2,1)} %get-tuple-element.56.wpack), custom_call_target="tpu_custom_call" | custom-call | flops 17999998976 | bytes 36000000 | tf_op jit(solution)/shard_map/blur/pallas_call | solution.py:177
  107.1 19.1 %blur.2.blurred = f32[4,64,24,128]{3,2,1,0:T(8,128)} custom-call(f32[8,93]{1,0:T(8,128)} %reshape.33.taps, f32[6,20,56,128]{3,2,1,0:T(8,128)} %bitcast_dynamic-update-slice_fusion.est, f32[192,192]{1,0:T(8,128)} %get-tuple-element.54.wy, bf16[8,256,256]{2,1,0:T(8,128)(2,1)} %get-tuple-element.55.wown, bf16[8,4,256,256]{3,2,1,0:T(8,128)(2,1)} %get-tuple-element.56.wpack), custom_call_target="tpu_custom_call" | custom-call | flops 17999998976 | bytes 36000000 | tf_op jit(solution)/shard_map/blur/pallas_call | solution.py:177
  136.9 14.7 %collective-permute-start.14 = (f32[32,24,128]{2,1,0:T(8,128)}, f32[32,24,128]{2,1,0:T(8,128)S(1)}, u32[]{:S(2)}, u32[]{:S(2)}) collective-permute-start(f32[32,24,128]{2,1,0:T(8,128)} %get-tuple-element.70), channel_id=1, source_target_pairs={{0,16},{16,32},{32,48},{48,64},{64,80},{80,96},{96,112},{1,17},{17... | collective-permute-start | bytes 1179656 | tf_op jit(solution)/shard_map/ppermute | solution.py:57
  165.6 8.1 %adjoint_x.5 = (f32[4,64,24,128]{3,2,1,0:T(8,128)}, f32[4,64,16,128]{3,2,1,0:T(8,128)}, f32[4,64,16,128]{3,2,1,0:T(8,128)}) custom-call(f32[4,64,24,128]{3,2,1,0:T(8,128)} %get-tuple-element.69.ratio, f32[32,24,128]{2,1,0:T(8,128)} %copy-done.22, f32[32,24,128]{2,1,0:T(8,128)} %copy-done.23, bf16[8,256,256]{2,1,0:T(8,128)(2,1)} %get-tuple-element.60.wown, ...), custom_call_target="tpu_custom_call" | custom-call | flops 8000000000 | bytes 16000000 | tf_op jit(solution)/shard_map/adjoint_x/pallas_call | solution.py:238
  181.0 8.2 %adjoint_x.4 = (f32[4,64,24,128]{3,2,1,0:T(8,128)}, f32[4,64,16,128]{3,2,1,0:T(8,128)}, f32[4,64,16,128]{3,2,1,0:T(8,128)}) custom-call(f32[4,64,24,128]{3,2,1,0:T(8,128)} %get-tuple-element.57.ratio, f32[32,24,128]{2,1,0:T(8,128)} %copy-done.17, f32[32,24,128]{2,1,0:T(8,128)} %copy-done.19, bf16[8,256,256]{2,1,0:T(8,128)(2,1)} %get-tuple-element.60.wown, ...), custom_call_target="tpu_custom_call" | custom-call | flops 8000000000 | bytes 16000000 | tf_op jit(solution)/shard_map/adjoint_x/pallas_call | solution.py:238
  203.4 8.8 %adjoint_y.5 = (f32[4,64,24,128]{3,2,1,0:T(8,128)}, f32[4,16,24,128]{3,2,1,0:T(8,128)}, f32[4,16,24,128]{3,2,1,0:T(8,128)}) custom-call(f32[4,64,24,128]{3,2,1,0:T(8,128)} %get-tuple-element.72.value, f32[4,64,16,128]{3,2,1,0:T(8,128)} %collective-permute-done.16.before, f32[4,64,16,128]{3,2,1,0:T(8,128)} %collective-permute-done.17.after, ...), custom_call_target="tpu_custom_call" | custom-call | flops 8000000000 | bytes 16000000 | tf_op jit(solution)/shard_map/adjoint_y/pallas_call | solution.py:280
  225.8 8.8 %adjoint_y.4 = (f32[4,64,24,128]{3,2,1,0:T(8,128)}, f32[4,16,24,128]{3,2,1,0:T(8,128)}, f32[4,16,24,128]{3,2,1,0:T(8,128)}) custom-call(f32[4,64,24,128]{3,2,1,0:T(8,128)} %get-tuple-element.62.value, f32[4,64,16,128]{3,2,1,0:T(8,128)} %copy-done.4, f32[4,64,16,128]{3,2,1,0:T(8,128)} %collective-permute-done.11.after, bf16[8,64,128]{2,1,0:T(8,128)(2,1)} %get-tuple-element.65.wy), custom_call_target="tpu_custom_call" | custom-call | flops 8000000000 | bytes 16000000 | tf_op jit(solution)/shard_map/adjoint_y/pallas_call | solution.py:280
  240.9 9.8 %first_logs.2.logs = f32[64,24,128]{2,1,0:T(8,128)} custom-call(f32[8,93]{1,0:T(8,128)} %reshape.33.taps, f32[4,64,24,128]{3,2,1,0:T(8,128)} %get-tuple-element.75.value, f32[4,16,24,128]{3,2,1,0:T(8,128)} %copy-done.8, f32[4,16,24,128]{3,2,1,0:T(8,128)} %copy-done.9), custom_call_target="tpu_custom_call" | custom-call | flops 8999999488 | bytes 18000000 | tf_op jit(solution)/shard_map/first_logs/pallas_call | solution.py:359
  252.4 12.2 %last_logs.2 = (f32[64,24,128]{2,1,0:T(8,128)}, f32[16,24,128]{2,1,0:T(8,128)}) custom-call(f32[8,93]{1,0:T(8,128)} %reshape.33.taps, f32[4,64,24,128]{3,2,1,0:T(8,128)} %get-tuple-element.66.value, f32[4,16,24,128]{3,2,1,0:T(8,128)} %copy-done.13, f32[4,16,24,128]{3,2,1,0:T(8,128)} %copy-done.15, f32[64,24,128]{2,1,0:T(8,128)} %first_logs.2.logs, ...), custom_call_target="tpu_custom_call" | custom-call | flops 10000000000 | bytes 20000000 | tf_op jit(solution)/shard_map/last_logs/pallas_call | solution.py:369
  295.9 9.1 %collective-permute-done.24 = f32[6,20,16,128]{3,2,1,0:T(8,128)S(1)} collective-permute-done((f32[6,20,16,128]{3,2,1,0:T(8,128)S(1)}, f32[6,20,16,128]{3,2,1,0:T(8,128)S(1)}, u32[]{:S(2)}, u32[]{:S(2)}) %collective-permute-start.24) | collective-permute-done | bytes 983072 | tf_op jit(solution)/shard_map/ppermute | solution.py:57
  311.4 22.3 %blur_and_divide.3 = (f32[4,64,24,128]{3,2,1,0:T(8,128)}, f32[32,24,128]{2,1,0:T(8,128)}, f32[32,24,128]{2,1,0:T(8,128)}) custom-call(f32[8,93]{1,0:T(8,128)} %reshape.33.taps, f32[6,20,56,128]{3,2,1,0:T(8,128)} %pad_maximum_fusion.est, f32[192,192]{1,0:T(8,128)} %get-tuple-element.54.wy, bf16[8,256,256]{2,1,0:T(8,128)(2,1)} %get-tuple-element.55.wown, ...), custom_call_target="tpu_custom_call" | custom-call | flops 24000000000 | bytes 48000000 | tf_op jit(solution)/shard_map/blur_and_divide/pallas_call | solution.py:187
  336.9 22.4 %blur_and_divide.2 = (f32[4,64,24,128]{3,2,1,0:T(8,128)}, f32[32,24,128]{2,1,0:T(8,128)}, f32[32,24,128]{2,1,0:T(8,128)}) custom-call(f32[8,93]{1,0:T(8,128)} %reshape.33.taps, f32[6,20,56,128]{3,2,1,0:T(8,128)} %pad_maximum_fusion.est, f32[192,192]{1,0:T(8,128)} %get-tuple-element.54.wy, bf16[8,256,256]{2,1,0:T(8,128)(2,1)} %get-tuple-element.55.wown, ...), custom_call_target="tpu_custom_call" | custom-call | flops 24000000000 | bytes 48000000 | tf_op jit(solution)/shard_map/blur_and_divide/pallas_call | solution.py:187
  368.3 8.1 %adjoint_x.7 = (f32[4,64,24,128]{3,2,1,0:T(8,128)}, f32[4,64,16,128]{3,2,1,0:T(8,128)}, f32[4,64,16,128]{3,2,1,0:T(8,128)}) custom-call(f32[4,64,24,128]{3,2,1,0:T(8,128)} %get-tuple-element.89.ratio, f32[32,24,128]{2,1,0:T(8,128)} %copy-done.20, f32[32,24,128]{2,1,0:T(8,128)} %copy-done.21, bf16[8,256,256]{2,1,0:T(8,128)(2,1)} %get-tuple-element.60.wown, ...), custom_call_target="tpu_custom_call" | custom-call | flops 8000000000 | bytes 16000000 | tf_op jit(solution)/shard_map/adjoint_x/pallas_call | solution.py:238
  381.9 8.1 %adjoint_x.6 = (f32[4,64,24,128]{3,2,1,0:T(8,128)}, f32[4,64,16,128]{3,2,1,0:T(8,128)}, f32[4,64,16,128]{3,2,1,0:T(8,128)}) custom-call(f32[4,64,24,128]{3,2,1,0:T(8,128)} %get-tuple-element.80.ratio, f32[32,24,128]{2,1,0:T(8,128)} %copy-done.16, f32[32,24,128]{2,1,0:T(8,128)} %copy-done.18, bf16[8,256,256]{2,1,0:T(8,128)(2,1)} %get-tuple-element.60.wown, ...), custom_call_target="tpu_custom_call" | custom-call | flops 8000000000 | bytes 16000000 | tf_op jit(solution)/shard_map/adjoint_x/pallas_call | solution.py:238
  395.3 7.6 %collective-permute-done.34.before = f32[4,64,16,128]{3,2,1,0:T(8,128)S(1)} collective-permute-done((f32[4,64,16,128]{3,2,1,0:T(8,128)}, f32[4,64,16,128]{3,2,1,0:T(8,128)S(1)}, u32[]{:S(2)}, u32[]{:S(2)}) %collective-permute-start.34) | collective-permute-done | bytes 2097184 | tf_op jit(solution)/shard_map/ppermute | solution.py:57
  407.6 8.8 %adjoint_y.7 = (f32[4,64,24,128]{3,2,1,0:T(8,128)}, f32[4,16,24,128]{3,2,1,0:T(8,128)}, f32[4,16,24,128]{3,2,1,0:T(8,128)}) custom-call(f32[4,64,24,128]{3,2,1,0:T(8,128)} %get-tuple-element.92.value, f32[4,64,16,128]{3,2,1,0:T(8,128)} %copy-done.5, f32[4,64,16,128]{3,2,1,0:T(8,128)} %copy-done.7, bf16[8,64,128]{2,1,0:T(8,128)(2,1)} %get-tuple-element.65.wy), custom_call_target="tpu_custom_call" | custom-call | flops 8000000000 | bytes 16000000 | tf_op jit(solution)/shard_map/adjoint_y/pallas_call | solution.py:280
  428.9 8.8 %adjoint_y.6 = (f32[4,64,24,128]{3,2,1,0:T(8,128)}, f32[4,16,24,128]{3,2,1,0:T(8,128)}, f32[4,16,24,128]{3,2,1,0:T(8,128)}) custom-call(f32[4,64,24,128]{3,2,1,0:T(8,128)} %get-tuple-element.83.value, f32[4,64,16,128]{3,2,1,0:T(8,128)} %copy-done.6, f32[4,64,16,128]{3,2,1,0:T(8,128)} %collective-permute-done.29.after, bf16[8,64,128]{2,1,0:T(8,128)(2,1)} %get-tuple-element.65.wy), custom_call_target="tpu_custom_call" | custom-call | flops 8000000000 | bytes 16000000 | tf_op jit(solution)/shard_map/adjoint_y/pallas_call | solution.py:280
  443.6 9.9 %first_logs.3.logs = f32[64,24,128]{2,1,0:T(8,128)} custom-call(f32[8,93]{1,0:T(8,128)} %reshape.33.taps, f32[4,64,24,128]{3,2,1,0:T(8,128)} %get-tuple-element.95.value, f32[4,16,24,128]{3,2,1,0:T(8,128)} %copy-done.10, f32[4,16,24,128]{3,2,1,0:T(8,128)} %copy-done.11), custom_call_target="tpu_custom_call" | custom-call | flops 8999999488 | bytes 18000000 | tf_op jit(solution)/shard_map/first_logs/pallas_call | solution.py:359
  455.0 12.2 %last_logs.3 = (f32[64,24,128]{2,1,0:T(8,128)}, f32[16,24,128]{2,1,0:T(8,128)}) custom-call(f32[8,93]{1,0:T(8,128)} %reshape.33.taps, f32[4,64,24,128]{3,2,1,0:T(8,128)} %get-tuple-element.86.value, f32[4,16,24,128]{3,2,1,0:T(8,128)} %copy-done.12, f32[4,16,24,128]{3,2,1,0:T(8,128)} %copy-done.14, f32[64,24,128]{2,1,0:T(8,128)} %first_logs.3.logs, ...), custom_call_target="tpu_custom_call" | custom-call | flops 10000000000 | bytes 20000000 | tf_op jit(solution)/shard_map/last_logs/pallas_call | solution.py:369
  469.1 89.7 %all_to_all.10 = f32[32,16,24,128]{3,2,1,0:T(8,128)} all-to-all(f32[32,16,24,128]{3,2,1,0:T(8,128)S(1)} %bitcast.38), channel_id=1, replica_groups=mesh['yh'=2,'x'=4,'z'=4,'yl'=2,'co'=2] {'yh','x','yl','co'}, dimensions={0} | all-to-all | bytes 12582912 | tf_op jit(solution)/shard_map/all_to_all | solution.py:537
  558.9 8.0 %spread.1 = f32[16,96,1024]{2,1,0:T(8,128)} custom-call(f32[8,4,16,24,128]{4,3,2,1,0:T(8,128)} %bitcast.44), custom_call_target="tpu_custom_call" | custom-call | flops 5000000000 | bytes 10000000 | tf_op jit(solution)/shard_map/spread/pallas_call | solution.py:490
  (153 shorter events, 203.2 us)
Async XLA Ops:
  13.8 36.3 %collective-permute-start.3 = (f32[20,56,128]{2,1,0:T(8,128)}, f32[20,56,128]{2,1,0:T(8,128)S(1)}, u32[]{:S(2)}, u32[]{:S(2)}) collective-permute-start(f32[20,56,128]{2,1,0:T(8,128)} %get-tuple-element.111), channel_id=1, source_target_pairs={{0,1},{1,0},{2,3},{3,2},{4,5},{5,4},{6,7},{7,6},{8,9},{9,8},{10,11... | collective-permute-start | bytes 1720328 | tf_op jit(solution)/shard_map/ppermute | solution.py:406
  15.0 35.0 %collective-permute-start.4 = (f32[20,56,128]{2,1,0:T(8,128)S(1)}, f32[20,56,128]{2,1,0:T(8,128)S(1)}, u32[]{:S(2)}, u32[]{:S(2)}) collective-permute-start(f32[20,56,128]{2,1,0:T(8,128)S(1)} %get-tuple-element.112), channel_id=1, source_target_pairs={{0,2},{1,3},{2,0},{3,1},{4,6},{5,7},{6,4},{7,5},{8,10},{9,11},{10,... | collective-permute-start | bytes 1720328 | tf_op jit(solution)/shard_map/ppermute | solution.py:406
  16.3 33.7 %collective-permute-start.5 = (f32[20,56,128]{2,1,0:T(8,128)S(1)}, f32[20,56,128]{2,1,0:T(8,128)}, u32[]{:S(2)}, u32[]{:S(2)}) collective-permute-start(f32[20,56,128]{2,1,0:T(8,128)S(1)} %get-tuple-element.113), channel_id=1, source_target_pairs={{0,3},{1,2},{2,1},{3,0},{4,7},{5,6},{6,5},{7,4},{8,11},{9,10},{10,... | collective-permute-start | bytes 1720328 | tf_op jit(solution)/shard_map/ppermute | solution.py:406
  16.7 27.7 %collective-permute-start.2 = (f32[8,3,31]{2,1,0:T(4,128)S(1)}, f32[8,3,31]{2,1,0:T(4,128)S(1)}, u32[]{:S(2)}, u32[]{:S(2)}) collective-permute-start(f32[8,3,31]{2,1,0:T(4,128)S(1)} %fusion.12), channel_id=1, source_target_pairs={{0,64},{16,80},{32,96},{48,112},{64,0},{80,16},{96,32},{112,48},{1... | collective-permute-start | bytes 8936 | tf_op jit(solution)/shard_map/ppermute | solution.py:385
  44.4 86.0 %all-to-all-start = ((f32[32,16,24,128]{3,2,1,0:T(8,128)}), f32[32,16,24,128]{3,2,1,0:T(8,128)}, u32[]{:S(2)}, u32[]{:S(2)}) async-start(f32[32,16,24,128]{3,2,1,0:T(8,128)} %bitcast.37), calls=%async_computation | async-start | bytes 12582912 | tf_op jit(solution)/shard_map/all_to_all | solution.py:506
  136.9 27.8 %collective-permute-start.14 = (f32[32,24,128]{2,1,0:T(8,128)}, f32[32,24,128]{2,1,0:T(8,128)S(1)}, u32[]{:S(2)}, u32[]{:S(2)}) collective-permute-start(f32[32,24,128]{2,1,0:T(8,128)} %get-tuple-element.70), channel_id=1, source_target_pairs={{0,16},{16,32},{32,48},{48,64},{64,80},{80,96},{96,112},{1,17},{17... | collective-permute-start | bytes 1179656 | tf_op jit(solution)/shard_map/ppermute | solution.py:57
  159.4 20.6 %collective-permute-start.8 = (f32[32,24,128]{2,1,0:T(8,128)}, f32[32,24,128]{2,1,0:T(8,128)S(1)}, u32[]{:S(2)}, u32[]{:S(2)}) collective-permute-start(f32[32,24,128]{2,1,0:T(8,128)} %get-tuple-element.58), channel_id=1, source_target_pairs={{0,16},{16,32},{32,48},{48,64},{64,80},{80,96},{96,112},{1,17},{17... | collective-permute-start | bytes 1179656 | tf_op jit(solution)/shard_map/ppermute | solution.py:57
  163.4 16.6 %collective-permute-start.9 = (f32[32,24,128]{2,1,0:T(8,128)}, f32[32,24,128]{2,1,0:T(8,128)S(1)}, u32[]{:S(2)}, u32[]{:S(2)}) collective-permute-start(f32[32,24,128]{2,1,0:T(8,128)} %get-tuple-element.59), channel_id=1, source_target_pairs={{16,0},{32,16},{48,32},{64,48},{80,64},{96,80},{112,96},{17,1},{33... | collective-permute-start | bytes 1179656 | tf_op jit(solution)/shard_map/ppermute | solution.py:57
  173.8 25.2 %collective-permute-start.16 = (f32[4,64,16,128]{3,2,1,0:T(8,128)}, f32[4,64,16,128]{3,2,1,0:T(8,128)}, u32[]{:S(2)}, u32[]{:S(2)}) collective-permute-start(f32[4,64,16,128]{3,2,1,0:T(8,128)} %get-tuple-element.73), channel_id=1, source_target_pairs={{0,1},{1,2},{2,3},{4,5},{5,6},{6,7},{8,9},{9,10},{10,11},{12,13},{... | collective-permute-start | bytes 6291464 | tf_op jit(solution)/shard_map/ppermute | solution.py:57
  175.7 27.7 %collective-permute-start.17 = (f32[4,64,16,128]{3,2,1,0:T(8,128)}, f32[4,64,16,128]{3,2,1,0:T(8,128)}, u32[]{:S(2)}, u32[]{:S(2)}) collective-permute-start(f32[4,64,16,128]{3,2,1,0:T(8,128)} %get-tuple-element.74), channel_id=1, source_target_pairs={{1,0},{2,1},{3,2},{5,4},{6,5},{7,6},{9,8},{10,9},{11,10},{13,12},{... | collective-permute-start | bytes 6291464 | tf_op jit(solution)/shard_map/ppermute | solution.py:57
  189.2 32.2 %collective-permute-start.10 = (f32[4,64,16,128]{3,2,1,0:T(8,128)}, f32[4,64,16,128]{3,2,1,0:T(8,128)S(1)}, u32[]{:S(2)}, u32[]{:S(2)}) collective-permute-start(f32[4,64,16,128]{3,2,1,0:T(8,128)} %get-tuple-element.63), channel_id=1, source_target_pairs={{0,1},{1,2},{2,3},{4,5},{5,6},{6,7},{8,9},{9,10},{10,11},{12,13},{... | collective-permute-start | bytes 6291464 | tf_op jit(solution)/shard_map/ppermute | solution.py:57
  191.3 34.5 %collective-permute-start.11 = (f32[4,64,16,128]{3,2,1,0:T(8,128)}, f32[4,64,16,128]{3,2,1,0:T(8,128)}, u32[]{:S(2)}, u32[]{:S(2)}) collective-permute-start(f32[4,64,16,128]{3,2,1,0:T(8,128)} %get-tuple-element.64), channel_id=1, source_target_pairs={{1,0},{2,1},{3,2},{5,4},{6,5},{7,6},{9,8},{10,9},{11,10},{13,12},{... | collective-permute-start | bytes 6291464 | tf_op jit(solution)/shard_map/ppermute | solution.py:57
  212.2 27.5 %collective-permute-start.18 = (f32[4,16,24,128]{3,2,1,0:T(8,128)}, f32[4,16,24,128]{3,2,1,0:T(8,128)S(1)}, u32[]{:S(2)}, u32[]{:S(2)}) collective-permute-start(f32[4,16,24,128]{3,2,1,0:T(8,128)} %get-tuple-element.76), channel_id=1, source_target_pairs={{0,4},{4,8},{8,12},{1,5},{5,9},{9,13},{2,6},{6,10},{10,14},{3,7},{... | collective-permute-start | bytes 2359304 | tf_op jit(solution)/shard_map/ppermute | solution.py:57
  215.8 23.9 %collective-permute-start.19 = (f32[4,16,24,128]{3,2,1,0:T(8,128)}, f32[4,16,24,128]{3,2,1,0:T(8,128)S(1)}, u32[]{:S(2)}, u32[]{:S(2)}) collective-permute-start(f32[4,16,24,128]{3,2,1,0:T(8,128)} %get-tuple-element.77), channel_id=1, source_target_pairs={{4,0},{8,4},{12,8},{5,1},{9,5},{13,9},{6,2},{10,6},{14,10},{7,3},{... | collective-permute-start | bytes 2359304 | tf_op jit(solution)/shard_map/ppermute | solution.py:57
  288.4 16.6 %collective-permute-start.24 = (f32[6,20,16,128]{3,2,1,0:T(8,128)S(1)}, f32[6,20,16,128]{3,2,1,0:T(8,128)S(1)}, u32[]{:S(2)}, u32[]{:S(2)}) collective-permute-start(f32[6,20,16,128]{3,2,1,0:T(8,128)S(1)} %get-tuple-element.108), channel_id=1, source_target_pairs={{0,1},{1,2},{2,3},{4,5},{5,6},{6,7},{8,9},{9,10},{10,11},{12,13},{... | collective-permute-start | bytes 2949128 | tf_op jit(solution)/shard_map/ppermute | solution.py:57
  333.7 33.8 %collective-permute-start.32 = (f32[32,24,128]{2,1,0:T(8,128)}, f32[32,24,128]{2,1,0:T(8,128)S(1)}, u32[]{:S(2)}, u32[]{:S(2)}) collective-permute-start(f32[32,24,128]{2,1,0:T(8,128)} %get-tuple-element.90), channel_id=1, source_target_pairs={{0,16},{16,32},{32,48},{48,64},{64,80},{80,96},{96,112},{1,17},{17... | collective-permute-start | bytes 1179656 | tf_op jit(solution)/shard_map/ppermute | solution.py:57
  335.6 31.9 %collective-permute-start.33 = (f32[32,24,128]{2,1,0:T(8,128)}, f32[32,24,128]{2,1,0:T(8,128)S(1)}, u32[]{:S(2)}, u32[]{:S(2)}) collective-permute-start(f32[32,24,128]{2,1,0:T(8,128)} %get-tuple-element.91), channel_id=1, source_target_pairs={{16,0},{32,16},{48,32},{64,48},{80,64},{96,80},{112,96},{17,1},{33... | collective-permute-start | bytes 1179656 | tf_op jit(solution)/shard_map/ppermute | solution.py:57
  359.2 21.7 %collective-permute-start.26 = (f32[32,24,128]{2,1,0:T(8,128)}, f32[32,24,128]{2,1,0:T(8,128)S(1)}, u32[]{:S(2)}, u32[]{:S(2)}) collective-permute-start(f32[32,24,128]{2,1,0:T(8,128)} %get-tuple-element.81), channel_id=1, source_target_pairs={{0,16},{16,32},{32,48},{48,64},{64,80},{80,96},{96,112},{1,17},{17... | collective-permute-start | bytes 1179656 | tf_op jit(solution)/shard_map/ppermute | solution.py:57
  376.5 26.4 %collective-permute-start.34 = (f32[4,64,16,128]{3,2,1,0:T(8,128)}, f32[4,64,16,128]{3,2,1,0:T(8,128)S(1)}, u32[]{:S(2)}, u32[]{:S(2)}) collective-permute-start(f32[4,64,16,128]{3,2,1,0:T(8,128)} %get-tuple-element.93), channel_id=1, source_target_pairs={{0,1},{1,2},{2,3},{4,5},{5,6},{6,7},{8,9},{9,10},{10,11},{12,13},{... | collective-permute-start | bytes 6291464 | tf_op jit(solution)/shard_map/ppermute | solution.py:57
  378.7 27.6 %collective-permute-start.35 = (f32[4,64,16,128]{3,2,1,0:T(8,128)}, f32[4,64,16,128]{3,2,1,0:T(8,128)S(1)}, u32[]{:S(2)}, u32[]{:S(2)}) collective-permute-start(f32[4,64,16,128]{3,2,1,0:T(8,128)} %get-tuple-element.94), channel_id=1, source_target_pairs={{1,0},{2,1},{3,2},{5,4},{6,5},{7,6},{9,8},{10,9},{11,10},{13,12},{... | collective-permute-start | bytes 6291464 | tf_op jit(solution)/shard_map/ppermute | solution.py:57
  390.0 35.4 %collective-permute-start.28 = (f32[4,64,16,128]{3,2,1,0:T(8,128)}, f32[4,64,16,128]{3,2,1,0:T(8,128)S(1)}, u32[]{:S(2)}, u32[]{:S(2)}) collective-permute-start(f32[4,64,16,128]{3,2,1,0:T(8,128)} %get-tuple-element.84), channel_id=1, source_target_pairs={{0,1},{1,2},{2,3},{4,5},{5,6},{6,7},{8,9},{9,10},{10,11},{12,13},{... | collective-permute-start | bytes 6291464 | tf_op jit(solution)/shard_map/ppermute | solution.py:57
  393.3 35.5 %collective-permute-start.29 = (f32[4,64,16,128]{3,2,1,0:T(8,128)}, f32[4,64,16,128]{3,2,1,0:T(8,128)}, u32[]{:S(2)}, u32[]{:S(2)}) collective-permute-start(f32[4,64,16,128]{3,2,1,0:T(8,128)} %get-tuple-element.85), channel_id=1, source_target_pairs={{1,0},{2,1},{3,2},{5,4},{6,5},{7,6},{9,8},{10,9},{11,10},{13,12},{... | collective-permute-start | bytes 6291464 | tf_op jit(solution)/shard_map/ppermute | solution.py:57
  416.4 26.1 %collective-permute-start.36 = (f32[4,16,24,128]{3,2,1,0:T(8,128)}, f32[4,16,24,128]{3,2,1,0:T(8,128)S(1)}, u32[]{:S(2)}, u32[]{:S(2)}) collective-permute-start(f32[4,16,24,128]{3,2,1,0:T(8,128)} %get-tuple-element.96), channel_id=1, source_target_pairs={{0,4},{4,8},{8,12},{1,5},{5,9},{9,13},{2,6},{6,10},{10,14},{3,7},{... | collective-permute-start | bytes 2359304 | tf_op jit(solution)/shard_map/ppermute | solution.py:57
  419.6 22.9 %collective-permute-start.37 = (f32[4,16,24,128]{3,2,1,0:T(8,128)}, f32[4,16,24,128]{3,2,1,0:T(8,128)S(1)}, u32[]{:S(2)}, u32[]{:S(2)}) collective-permute-start(f32[4,16,24,128]{3,2,1,0:T(8,128)} %get-tuple-element.97), channel_id=1, source_target_pairs={{4,0},{8,4},{12,8},{5,1},{9,5},{13,9},{6,2},{10,6},{14,10},{7,3},{... | collective-permute-start | bytes 2359304 | tf_op jit(solution)/shard_map/ppermute | solution.py:57
  (39 other events, 241.7 us)

commit v5 on v4

--- a/solution.py
+++ b/solution.py
@@ -93,7 +93,7 @@
                     hi, lo = split(jnp.concatenate([one[:, :XC], one[:, XC:]], axis=0))
                     dest[u, rows, :] = jnp.concatenate([hi, lo], axis=1)
 
-    step = 4
+    step = 12
 
     @pl.loop(0, ZW // 4 // step)
     def _(b):
@@ -209,18 +209,16 @@
 
 
 def adjoint_x_kernel(ratio, before, after, wown, wside, out, top, bottom):
-    planes = 16
+    planes = ZC // 2
     low_lanes = lax.broadcasted_iota(jnp.int32, (planes * YC, XC), 1) < XC // 2
 
-    @pl.loop(0, ZC // planes)
-    def _(b):
+    @pl.loop(0, 2)
+    def _(half):
         rows = planes * YC
-        half = b // 2
-        zs = pl.ds(pl.multiple_of(b * planes, planes), planes)
-        hs = pl.ds(pl.multiple_of((b - 2 * half) * planes, planes), planes)
+        zs = pl.ds(pl.multiple_of(half * planes, planes), planes)
         hi, lo = split(ratio[0, zs].reshape(rows, XC))
         is_before = low_lanes == (half == 0)
-        shi, slo = split(jnp.where(is_before, before[hs].reshape(rows, XC), after[hs].reshape(rows, XC)))
+        shi, slo = split(jnp.where(is_before, before[...].reshape(rows, XC), after[...].reshape(rows, XC)))
         two = dot(jnp.concatenate([hi, lo], axis=1), wown[0])
         two = two + dot(jnp.concatenate([shi, slo], axis=1), wside[0, half])
         value = two[:, :XC] + two[:, XC:]
@@ -391,11 +389,14 @@
     return jnp.concatenate([before[None], blocks, after[None]], axis=0)
 
 
-def first_window(slab):
+def first_columns(slab):
     padded = jnp.pad(slab, ((0, 0), (HALO, HALO), (XC, XC)))
     c = lax.axis_index(V)
     before, own, after = (lax.dynamic_slice_in_dim(padded, XC * (c + k), XC, axis=2) for k in range(3))
-    planes = jnp.concatenate([own, pack(before, after)], axis=0)
+    return jnp.concatenate([own, pack(before, after)], axis=0)
+
+
+def first_window(planes, matrix):
     me = lax.axis_index(S)
 
     def rows(k):
@@ -404,6 +405,7 @@
     got = [rows(me)]
     for k in range(1, SLABS):
         got.append(lax.ppermute(rows(me ^ k), S, [(i, i ^ k) for i in range(SLABS)]))
+    *got, _ = lax.optimization_barrier((*got, matrix))
     got = jnp.stack(got)
     blocks = jnp.stack([lax.dynamic_index_in_dim(got, me ^ k, 0, keepdims=False) for k in range(SLABS)])
     return add_z(blocks)
@@ -474,7 +476,7 @@
         + [jax.ShapeDtypeStruct((VIEWS,) + shape, BF16) for shape in shapes],
         in_specs=[pl.BlockSpec(memory_space=pltpu.SMEM)],
         out_specs=[pl.BlockSpec((YC, 3 * YK), lambda v: (v, 0))] + [of_view(0, *shape) for shape in shapes],
-        **params(1),
+        **params(10),
     )(taps)
     return (fy, fx, fp), (ax, side), ay
 
@@ -502,11 +504,12 @@
     everyone = gather_views(kernels[0])
     blocks = views_data[0].reshape(DEPTH, SLABS, YC, VIEWS, XC).transpose(3, 1, 0, 2, 4)
     blocks = blocks.reshape(VIEWS * SLABS, DEPTH, YC, XC)
-    blocks, everyone = lax.optimization_barrier((blocks, everyone))
+    planes = first_columns(estimate)
+    blocks, planes, everyone = lax.optimization_barrier((blocks, planes, everyone))
     data = lax.all_to_all(blocks, V + S, 0, 0, tiled=True).reshape(VIEWS, ZC, YC, XC)
     taps = (everyone / jnp.sum(everyone, axis=-1, keepdims=True)).reshape(VIEWS, 3 * TAPS)
     w_forward, w_x, w_y = matrices(taps)
-    window = first_window(estimate)
+    window = first_window(planes, w_y)
     chunk = window[1 : 1 + SLABS, :DEPTH, HALO : HALO + YC].reshape(ZC, YC, XC)
     groups = range(VIEWS // GROUP)
     for number in range(ITERS):

time: 569 us -> 599 us (1.053)
  waiting for transfers between devices: 95.7 us -> 131 us
  Pallas kernels: 229 us -> 213 us
  starting transfers between devices: 111 us -> 121 us
    ppermute x3, waiting for transfers between devices: 0.01 us -> 42.5 us  [first_window(): lax.ppermute(rows(me ^ k), S, [(i, i ^ k) for i in range(SLABS)])]
    ppermute x3, waiting for transfers between devices: 16.5 us -> 0.01 us  [gather_views(): rows = rows + lax.ppermute(rows, V, [(i, i ^ k) for i in range(VIEWS)])]
    ppermute x32, waiting for transfers between devices: 75 us -> 88.2 us  [exchange(): return (lax.ppermute(high, axis, up), lax.ppermute(low, axis, down))]
    ppermute x32, starting transfers between devices: 94.7 us -> 105 us  [exchange(): return (lax.ppermute(high, axis, up), lax.ppermute(low, axis, down))]
    pallas_call x2, Pallas kernels: 44.7 us -> 38.2 us  [forward(): pl.pallas_call(functools.partial(blur_and_divide_kernel, g), name='blur_a...]
    pallas_call x2, Pallas kernels: 38.1 us -> 31.7 us  [forward(): pl.pallas_call(functools.partial(blur_kernel, g), name='blur', grid=(GROU...]
    unnamed x55 -> x59, local copies, waits for them, and re-layouts: 19.5 us -> 20.7 us
  transfers between devices with their start and end apart: 39 -> 39, of which waited for: 20 -> 19; matrix products, arithmetic and copies ran while one was open for 4% -> 3% of each run, Pallas kernels for 30% -> 26%
where the time goes in v5:
time: 599 us; the launch traced here: 596 us
  Pallas kernels  213 us (36%)
  waiting for transfers between devices  131 us (22%)
  starting transfers between devices  121 us (20%)
  blocking collectives  89.7 us (15%)
  local copies, waits for them, and re-layouts  33.4 us (6%)
  other arithmetic  8.07 us (1%)
    ppermute x32, starting transfers between devices, exchange(): return (lax.ppermute(high, axis, up), lax.ppermute(low, axis, down))  105 us
    all_to_all x1, blocking collectives, per_device(): lax.all_to_all(parts, V + S, 0, 0, tiled=True)  89.7 us
    ppermute x32, waiting for transfers between devices, exchange(): return (lax.ppermute(high, axis, up), lax.ppermute(low, axis, down))  88.2 us
    ppermute x3, waiting for transfers between devices, first_window(): lax.ppermute(rows(me ^ k), S, [(i, i ^ k) for i in range(SLABS)])  42.5 us
    pallas_call x2, Pallas kernels, forward(): pl.pallas_call(functools.partial(blur_and_divide_kernel, g), name='blur_a...  38.2 us
    pallas_call x4, Pallas kernels, adjoint_y(): pl.pallas_call(adjoint_y_kernel, name='adjoint_y', grid=(GROUP,), out_sha...  35.2 us
    pallas_call x2, Pallas kernels, forward(): pl.pallas_call(functools.partial(blur_kernel, g), name='blur', grid=(GROU...  31.7 us
    pallas_call x4, Pallas kernels, adjoint_x(): pl.pallas_call(adjoint_x_kernel, name='adjoint_x', grid=(GROUP,), out_sha...  29.2 us
  transfers between devices with their start and end apart: 39, of which 19 were waited for; matrix products, arithmetic and copies ran while one was open for 3% of the time, Pallas kernels for 26%

profile of v5, /device:TPU:1, one launch (start us, length us, event | category | flops | bytes accessed | tf_op | source)
XLA Modules:
  0.0 596.3 jit_solution(10908561321536249033)
XLA Ops:
  33.8 10.8 %matrices.1 = (f32[192,192]{1,0:T(8,128)}, bf16[8,256,256]{2,1,0:T(8,128)(2,1)}, bf16[8,4,256,256]{3,2,1,0:T(8,128)(2,1)}, bf16[8,256,256]{2,1,0:T(8,128)(2,1)},...) custom-call(f32[8,93]{1,0:T(8,128)} %reshape.33.taps), custom_call_target="tpu_custom_call" | custom-call | flops 10000000000 | bytes 20000000 | tf_op jit(solution)/shard_map/matrices/pallas_call | solution.py:471
  44.6 42.5 %collective-permute-done.5 = f32[20,56,128]{2,1,0:T(8,128)S(1)} collective-permute-done((f32[20,56,128]{2,1,0:T(8,128)S(1)}, f32[20,56,128]{2,1,0:T(8,128)S(1)}, u32[]{:S(2)}, u32[]{:S(2)}) %collective-permute-start.5) | collective-permute-done | bytes 573472 | tf_op jit(solution)/shard_map/ppermute | solution.py:407
  93.0 10.7 %collective-permute-done.6 = f32[20,56,128]{2,1,0:T(8,128)S(1)} collective-permute-done((f32[20,56,128]{2,1,0:T(8,128)S(1)}, f32[20,56,128]{2,1,0:T(8,128)S(1)}, u32[]{:S(2)}, u32[]{:S(2)}) %collective-permute-start.6) | collective-permute-done | bytes 573472 | tf_op jit(solution)/shard_map/ppermute | solution.py:57
  109.7 11.1 %collective-permute-done.7 = f32[20,56,128]{2,1,0:T(8,128)} collective-permute-done((f32[20,56,128]{2,1,0:T(8,128)S(1)}, f32[20,56,128]{2,1,0:T(8,128)}, u32[]{:S(2)}, u32[]{:S(2)}) %collective-permute-start.7) | collective-permute-done | bytes 573472 | tf_op jit(solution)/shard_map/ppermute | solution.py:57
  122.7 15.8 %blur.3.blurred = f32[4,64,24,128]{3,2,1,0:T(8,128)} custom-call(f32[8,93]{1,0:T(8,128)} %reshape.33.taps, f32[6,20,56,128]{3,2,1,0:T(8,128)} %bitcast_dynamic-update-slice_fusion.est, f32[192,192]{1,0:T(8,128)} %get-tuple-element.65.wy, bf16[8,256,256]{2,1,0:T(8,128)(2,1)} %get-tuple-element.66.wown, bf16[8,4,256,256]{3,2,1,0:T(8,128)(2,1)} %get-tuple-element.67.wpack), custom_call_target="tpu_custom_call" | custom-call | flops 17999998976 | bytes 36000000 | tf_op jit(solution)/shard_map/blur/pallas_call | solution.py:177
  138.6 15.9 %blur.2.blurred = f32[4,64,24,128]{3,2,1,0:T(8,128)} custom-call(f32[8,93]{1,0:T(8,128)} %reshape.33.taps, f32[6,20,56,128]{3,2,1,0:T(8,128)} %bitcast_dynamic-update-slice_fusion.est, f32[192,192]{1,0:T(8,128)} %get-tuple-element.65.wy, bf16[8,256,256]{2,1,0:T(8,128)(2,1)} %get-tuple-element.66.wown, bf16[8,4,256,256]{3,2,1,0:T(8,128)(2,1)} %get-tuple-element.67.wpack), custom_call_target="tpu_custom_call" | custom-call | flops 17999998976 | bytes 36000000 | tf_op jit(solution)/shard_map/blur/pallas_call | solution.py:177
  170.4 20.0 %collective-permute-start.8 = (f32[32,24,128]{2,1,0:T(8,128)}, f32[32,24,128]{2,1,0:T(8,128)S(1)}, u32[]{:S(2)}, u32[]{:S(2)}) collective-permute-start(f32[32,24,128]{2,1,0:T(8,128)} %get-tuple-element.69), channel_id=1, source_target_pairs={{0,16},{16,32},{32,48},{48,64},{64,80},{80,96},{96,112},{1,17},{17... | collective-permute-start | bytes 1179656 | tf_op jit(solution)/shard_map/ppermute | solution.py:57
  207.5 7.3 %adjoint_x.4 = (f32[4,64,24,128]{3,2,1,0:T(8,128)}, f32[4,64,16,128]{3,2,1,0:T(8,128)}, f32[4,64,16,128]{3,2,1,0:T(8,128)}) custom-call(f32[4,64,24,128]{3,2,1,0:T(8,128)} %get-tuple-element.68.ratio, f32[32,24,128]{2,1,0:T(8,128)} %copy-done.19, f32[32,24,128]{2,1,0:T(8,128)} %copy-done.21, bf16[8,256,256]{2,1,0:T(8,128)(2,1)} %get-tuple-element.71.wown, ...), custom_call_target="tpu_custom_call" | custom-call | flops 8000000000 | bytes 16000000 | tf_op jit(solution)/shard_map/adjoint_x/pallas_call | solution.py:236
  232.4 8.9 %adjoint_y.5 = (f32[4,64,24,128]{3,2,1,0:T(8,128)}, f32[4,16,24,128]{3,2,1,0:T(8,128)}, f32[4,16,24,128]{3,2,1,0:T(8,128)}) custom-call(f32[4,64,24,128]{3,2,1,0:T(8,128)} %get-tuple-element.82.value, f32[4,64,16,128]{3,2,1,0:T(8,128)} %collective-permute-done.16.before, f32[4,64,16,128]{3,2,1,0:T(8,128)} %collective-permute-done.17.after, ...), custom_call_target="tpu_custom_call" | custom-call | flops 8000000000 | bytes 16000000 | tf_op jit(solution)/shard_map/adjoint_y/pallas_call | solution.py:278
  256.3 8.8 %adjoint_y.4 = (f32[4,64,24,128]{3,2,1,0:T(8,128)}, f32[4,16,24,128]{3,2,1,0:T(8,128)}, f32[4,16,24,128]{3,2,1,0:T(8,128)}) custom-call(f32[4,64,24,128]{3,2,1,0:T(8,128)} %get-tuple-element.73.value, f32[4,64,16,128]{3,2,1,0:T(8,128)} %copy-done.5, f32[4,64,16,128]{3,2,1,0:T(8,128)} %copy-done.6, bf16[8,64,128]{2,1,0:T(8,128)(2,1)} %get-tuple-element.60.wy), custom_call_target="tpu_custom_call" | custom-call | flops 8000000000 | bytes 16000000 | tf_op jit(solution)/shard_map/adjoint_y/pallas_call | solution.py:278
  271.0 9.8 %first_logs.2.logs = f32[64,24,128]{2,1,0:T(8,128)} custom-call(f32[8,93]{1,0:T(8,128)} %reshape.33.taps, f32[4,64,24,128]{3,2,1,0:T(8,128)} %get-tuple-element.85.value, f32[4,16,24,128]{3,2,1,0:T(8,128)} %copy-done.10, f32[4,16,24,128]{3,2,1,0:T(8,128)} %copy-done.11), custom_call_target="tpu_custom_call" | custom-call | flops 8999999488 | bytes 18000000 | tf_op jit(solution)/shard_map/first_logs/pallas_call | solution.py:357
  282.4 12.2 %last_logs.2 = (f32[64,24,128]{2,1,0:T(8,128)}, f32[16,24,128]{2,1,0:T(8,128)}) custom-call(f32[8,93]{1,0:T(8,128)} %reshape.33.taps, f32[4,64,24,128]{3,2,1,0:T(8,128)} %get-tuple-element.76.value, f32[4,16,24,128]{3,2,1,0:T(8,128)} %copy-done.15, f32[4,16,24,128]{3,2,1,0:T(8,128)} %copy-done.17, f32[64,24,128]{2,1,0:T(8,128)} %first_logs.2.logs, ...), custom_call_target="tpu_custom_call" | custom-call | flops 10000000000 | bytes 20000000 | tf_op jit(solution)/shard_map/last_logs/pallas_call | solution.py:367
  328.9 9.1 %collective-permute-done.24 = f32[6,20,16,128]{3,2,1,0:T(8,128)S(1)} collective-permute-done((f32[6,20,16,128]{3,2,1,0:T(8,128)S(1)}, f32[6,20,16,128]{3,2,1,0:T(8,128)S(1)}, u32[]{:S(2)}, u32[]{:S(2)}) %collective-permute-start.24) | collective-permute-done | bytes 983072 | tf_op jit(solution)/shard_map/ppermute | solution.py:57
  344.4 19.1 %blur_and_divide.3 = (f32[4,64,24,128]{3,2,1,0:T(8,128)}, f32[32,24,128]{2,1,0:T(8,128)}, f32[32,24,128]{2,1,0:T(8,128)}) custom-call(f32[8,93]{1,0:T(8,128)} %reshape.33.taps, f32[6,20,56,128]{3,2,1,0:T(8,128)} %pad_maximum_fusion.est, f32[192,192]{1,0:T(8,128)} %get-tuple-element.65.wy, bf16[8,256,256]{2,1,0:T(8,128)(2,1)} %get-tuple-element.66.wown, ...), custom_call_target="tpu_custom_call" | custom-call | flops 24000000000 | bytes 48000000 | tf_op jit(solution)/shard_map/blur_and_divide/pallas_call | solution.py:187
  370.0 19.2 %blur_and_divide.2 = (f32[4,64,24,128]{3,2,1,0:T(8,128)}, f32[32,24,128]{2,1,0:T(8,128)}, f32[32,24,128]{2,1,0:T(8,128)}) custom-call(f32[8,93]{1,0:T(8,128)} %reshape.33.taps, f32[6,20,56,128]{3,2,1,0:T(8,128)} %pad_maximum_fusion.est, f32[192,192]{1,0:T(8,128)} %get-tuple-element.65.wy, bf16[8,256,256]{2,1,0:T(8,128)(2,1)} %get-tuple-element.66.wown, ...), custom_call_target="tpu_custom_call" | custom-call | flops 24000000000 | bytes 48000000 | tf_op jit(solution)/shard_map/blur_and_divide/pallas_call | solution.py:187
  389.2 7.9 %collective-permute-start.26 = (f32[32,24,128]{2,1,0:T(8,128)}, f32[32,24,128]{2,1,0:T(8,128)S(1)}, u32[]{:S(2)}, u32[]{:S(2)}) collective-permute-start(f32[32,24,128]{2,1,0:T(8,128)} %get-tuple-element.91), channel_id=1, source_target_pairs={{0,16},{16,32},{32,48},{48,64},{64,80},{80,96},{96,112},{1,17},{17... | collective-permute-start | bytes 1179656 | tf_op jit(solution)/shard_map/ppermute | solution.py:57
  411.8 7.3 %adjoint_x.6 = (f32[4,64,24,128]{3,2,1,0:T(8,128)}, f32[4,64,16,128]{3,2,1,0:T(8,128)}, f32[4,64,16,128]{3,2,1,0:T(8,128)}) custom-call(f32[4,64,24,128]{3,2,1,0:T(8,128)} %get-tuple-element.90.ratio, f32[32,24,128]{2,1,0:T(8,128)} %copy-done.18, f32[32,24,128]{2,1,0:T(8,128)} %copy-done.20, bf16[8,256,256]{2,1,0:T(8,128)(2,1)} %get-tuple-element.71.wown, ...), custom_call_target="tpu_custom_call" | custom-call | flops 8000000000 | bytes 16000000 | tf_op jit(solution)/shard_map/adjoint_x/pallas_call | solution.py:236
  424.5 9.3 %collective-permute-done.34.before = f32[4,64,16,128]{3,2,1,0:T(8,128)S(1)} collective-permute-done((f32[4,64,16,128]{3,2,1,0:T(8,128)}, f32[4,64,16,128]{3,2,1,0:T(8,128)S(1)}, u32[]{:S(2)}, u32[]{:S(2)}) %collective-permute-start.34) | collective-permute-done | bytes 2097184 | tf_op jit(solution)/shard_map/ppermute | solution.py:57
  437.7 8.8 %adjoint_y.7 = (f32[4,64,24,128]{3,2,1,0:T(8,128)}, f32[4,16,24,128]{3,2,1,0:T(8,128)}, f32[4,16,24,128]{3,2,1,0:T(8,128)}) custom-call(f32[4,64,24,128]{3,2,1,0:T(8,128)} %get-tuple-element.102.value, f32[4,64,16,128]{3,2,1,0:T(8,128)} %copy-done.7, f32[4,64,16,128]{3,2,1,0:T(8,128)} %copy-done.9, bf16[8,64,128]{2,1,0:T(8,128)(2,1)} %get-tuple-element.60.wy), custom_call_target="tpu_custom_call" | custom-call | flops 8000000000 | bytes 16000000 | tf_op jit(solution)/shard_map/adjoint_y/pallas_call | solution.py:278
  459.1 8.8 %adjoint_y.6 = (f32[4,64,24,128]{3,2,1,0:T(8,128)}, f32[4,16,24,128]{3,2,1,0:T(8,128)}, f32[4,16,24,128]{3,2,1,0:T(8,128)}) custom-call(f32[4,64,24,128]{3,2,1,0:T(8,128)} %get-tuple-element.93.value, f32[4,64,16,128]{3,2,1,0:T(8,128)} %copy-done.8, f32[4,64,16,128]{3,2,1,0:T(8,128)} %collective-permute-done.29.after, bf16[8,64,128]{2,1,0:T(8,128)(2,1)} %get-tuple-element.60.wy), custom_call_target="tpu_custom_call" | custom-call | flops 8000000000 | bytes 16000000 | tf_op jit(solution)/shard_map/adjoint_y/pallas_call | solution.py:278
  473.2 9.9 %first_logs.3.logs = f32[64,24,128]{2,1,0:T(8,128)} custom-call(f32[8,93]{1,0:T(8,128)} %reshape.33.taps, f32[4,64,24,128]{3,2,1,0:T(8,128)} %get-tuple-element.105.value, f32[4,16,24,128]{3,2,1,0:T(8,128)} %copy-done.12, f32[4,16,24,128]{3,2,1,0:T(8,128)} %copy-done.13), custom_call_target="tpu_custom_call" | custom-call | flops 8999999488 | bytes 18000000 | tf_op jit(solution)/shard_map/first_logs/pallas_call | solution.py:357
  484.6 12.2 %last_logs.3 = (f32[64,24,128]{2,1,0:T(8,128)}, f32[16,24,128]{2,1,0:T(8,128)}) custom-call(f32[8,93]{1,0:T(8,128)} %reshape.33.taps, f32[4,64,24,128]{3,2,1,0:T(8,128)} %get-tuple-element.96.value, f32[4,16,24,128]{3,2,1,0:T(8,128)} %copy-done.14, f32[4,16,24,128]{3,2,1,0:T(8,128)} %copy-done.16, f32[64,24,128]{2,1,0:T(8,128)} %first_logs.3.logs, ...), custom_call_target="tpu_custom_call" | custom-call | flops 10000000000 | bytes 20000000 | tf_op jit(solution)/shard_map/last_logs/pallas_call | solution.py:367
  498.7 89.7 %all_to_all.10 = f32[32,16,24,128]{3,2,1,0:T(8,128)} all-to-all(f32[32,16,24,128]{3,2,1,0:T(8,128)S(1)} %bitcast.37), channel_id=1, replica_groups=mesh['yh'=2,'x'=4,'z'=4,'yl'=2,'co'=2] {'yh','x','yl','co'}, dimensions={0} | all-to-all | bytes 12582912 | tf_op jit(solution)/shard_map/all_to_all | solution.py:540
  588.4 8.0 %spread.1 = f32[16,96,1024]{2,1,0:T(8,128)} custom-call(f32[8,4,16,24,128]{4,3,2,1,0:T(8,128)} %bitcast.43), custom_call_target="tpu_custom_call" | custom-call | flops 5000000000 | bytes 10000000 | tf_op jit(solution)/shard_map/spread/pallas_call | solution.py:492
  (158 shorter events, 212.7 us)
Async XLA Ops:
  25.8 18.8 %collective-permute-start.3 = (f32[20,56,128]{2,1,0:T(8,128)}, f32[20,56,128]{2,1,0:T(8,128)S(1)}, u32[]{:S(2)}, u32[]{:S(2)}) collective-permute-start(f32[20,56,128]{2,1,0:T(8,128)} %get-tuple-element.122), channel_id=1, source_target_pairs={{0,1},{1,0},{2,3},{3,2},{4,5},{5,4},{6,7},{7,6},{8,9},{9,8},{10,11... | collective-permute-start | bytes 1720328 | tf_op jit(solution)/shard_map/ppermute | solution.py:407
  27.4 17.2 %collective-permute-start.4 = (f32[20,56,128]{2,1,0:T(8,128)S(1)}, f32[20,56,128]{2,1,0:T(8,128)S(1)}, u32[]{:S(2)}, u32[]{:S(2)}) collective-permute-start(f32[20,56,128]{2,1,0:T(8,128)S(1)} %get-tuple-element.121), channel_id=1, source_target_pairs={{0,2},{1,3},{2,0},{3,1},{4,6},{5,7},{6,4},{7,5},{8,10},{9,11},{10,... | collective-permute-start | bytes 1720328 | tf_op jit(solution)/shard_map/ppermute | solution.py:407
  27.8 59.4 %collective-permute-start.5 = (f32[20,56,128]{2,1,0:T(8,128)S(1)}, f32[20,56,128]{2,1,0:T(8,128)S(1)}, u32[]{:S(2)}, u32[]{:S(2)}) collective-permute-start(f32[20,56,128]{2,1,0:T(8,128)S(1)} %get-tuple-element.120), channel_id=1, source_target_pairs={{0,3},{1,2},{2,1},{3,0},{4,7},{5,6},{6,5},{7,4},{8,11},{9,10},{10,... | collective-permute-start | bytes 1720328 | tf_op jit(solution)/shard_map/ppermute | solution.py:407
  29.0 125.4 %all-to-all-start = ((f32[32,16,24,128]{3,2,1,0:T(8,128)}), f32[32,16,24,128]{3,2,1,0:T(8,128)}, u32[]{:S(2)}, u32[]{:S(2)}) async-start(f32[32,16,24,128]{3,2,1,0:T(8,128)} %bitcast.36), calls=%async_computation | async-start | bytes 12582912 | tf_op jit(solution)/shard_map/all_to_all | solution.py:509
  160.9 30.7 %collective-permute-start.14 = (f32[32,24,128]{2,1,0:T(8,128)}, f32[32,24,128]{2,1,0:T(8,128)S(1)}, u32[]{:S(2)}, u32[]{:S(2)}) collective-permute-start(f32[32,24,128]{2,1,0:T(8,128)} %get-tuple-element.80), channel_id=1, source_target_pairs={{0,16},{16,32},{32,48},{48,64},{64,80},{80,96},{96,112},{1,17},{17... | collective-permute-start | bytes 1179656 | tf_op jit(solution)/shard_map/ppermute | solution.py:57
  162.6 29.1 %collective-permute-start.15 = (f32[32,24,128]{2,1,0:T(8,128)}, f32[32,24,128]{2,1,0:T(8,128)S(1)}, u32[]{:S(2)}, u32[]{:S(2)}) collective-permute-start(f32[32,24,128]{2,1,0:T(8,128)} %get-tuple-element.81), channel_id=1, source_target_pairs={{16,0},{32,16},{48,32},{64,48},{80,64},{96,80},{112,96},{17,1},{33... | collective-permute-start | bytes 1179656 | tf_op jit(solution)/shard_map/ppermute | solution.py:57
  170.4 36.2 %collective-permute-start.8 = (f32[32,24,128]{2,1,0:T(8,128)}, f32[32,24,128]{2,1,0:T(8,128)S(1)}, u32[]{:S(2)}, u32[]{:S(2)}) collective-permute-start(f32[32,24,128]{2,1,0:T(8,128)} %get-tuple-element.69), channel_id=1, source_target_pairs={{0,16},{16,32},{32,48},{48,64},{64,80},{80,96},{96,112},{1,17},{17... | collective-permute-start | bytes 1179656 | tf_op jit(solution)/shard_map/ppermute | solution.py:57
  190.3 16.2 %collective-permute-start.9 = (f32[32,24,128]{2,1,0:T(8,128)}, f32[32,24,128]{2,1,0:T(8,128)S(1)}, u32[]{:S(2)}, u32[]{:S(2)}) collective-permute-start(f32[32,24,128]{2,1,0:T(8,128)} %get-tuple-element.70), channel_id=1, source_target_pairs={{16,0},{32,16},{48,32},{64,48},{80,64},{96,80},{112,96},{17,1},{33... | collective-permute-start | bytes 1179656 | tf_op jit(solution)/shard_map/ppermute | solution.py:57
  199.8 27.9 %collective-permute-start.16 = (f32[4,64,16,128]{3,2,1,0:T(8,128)}, f32[4,64,16,128]{3,2,1,0:T(8,128)}, u32[]{:S(2)}, u32[]{:S(2)}) collective-permute-start(f32[4,64,16,128]{3,2,1,0:T(8,128)} %get-tuple-element.83), channel_id=1, source_target_pairs={{0,1},{1,2},{2,3},{4,5},{5,6},{6,7},{8,9},{9,10},{10,11},{12,13},{... | collective-permute-start | bytes 6291464 | tf_op jit(solution)/shard_map/ppermute | solution.py:57
  204.4 27.9 %collective-permute-start.17 = (f32[4,64,16,128]{3,2,1,0:T(8,128)}, f32[4,64,16,128]{3,2,1,0:T(8,128)}, u32[]{:S(2)}, u32[]{:S(2)}) collective-permute-start(f32[4,64,16,128]{3,2,1,0:T(8,128)} %get-tuple-element.84), channel_id=1, source_target_pairs={{1,0},{2,1},{3,2},{5,4},{6,5},{7,6},{9,8},{10,9},{11,10},{13,12},{... | collective-permute-start | bytes 6291464 | tf_op jit(solution)/shard_map/ppermute | solution.py:57
  214.8 35.4 %collective-permute-start.10 = (f32[4,64,16,128]{3,2,1,0:T(8,128)}, f32[4,64,16,128]{3,2,1,0:T(8,128)S(1)}, u32[]{:S(2)}, u32[]{:S(2)}) collective-permute-start(f32[4,64,16,128]{3,2,1,0:T(8,128)} %get-tuple-element.74), channel_id=1, source_target_pairs={{0,1},{1,2},{2,3},{4,5},{5,6},{6,7},{8,9},{9,10},{10,11},{12,13},{... | collective-permute-start | bytes 6291464 | tf_op jit(solution)/shard_map/ppermute | solution.py:57
  218.4 36.6 %collective-permute-start.11 = (f32[4,64,16,128]{3,2,1,0:T(8,128)}, f32[4,64,16,128]{3,2,1,0:T(8,128)S(1)}, u32[]{:S(2)}, u32[]{:S(2)}) collective-permute-start(f32[4,64,16,128]{3,2,1,0:T(8,128)} %get-tuple-element.75), channel_id=1, source_target_pairs={{1,0},{2,1},{3,2},{5,4},{6,5},{7,6},{9,8},{10,9},{11,10},{13,12},{... | collective-permute-start | bytes 6291464 | tf_op jit(solution)/shard_map/ppermute | solution.py:57
  241.2 28.7 %collective-permute-start.18 = (f32[4,16,24,128]{3,2,1,0:T(8,128)}, f32[4,16,24,128]{3,2,1,0:T(8,128)S(1)}, u32[]{:S(2)}, u32[]{:S(2)}) collective-permute-start(f32[4,16,24,128]{3,2,1,0:T(8,128)} %get-tuple-element.86), channel_id=1, source_target_pairs={{0,4},{4,8},{8,12},{1,5},{5,9},{9,13},{2,6},{6,10},{10,14},{3,7},{... | collective-permute-start | bytes 2359304 | tf_op jit(solution)/shard_map/ppermute | solution.py:57
  244.7 25.2 %collective-permute-start.19 = (f32[4,16,24,128]{3,2,1,0:T(8,128)}, f32[4,16,24,128]{3,2,1,0:T(8,128)S(1)}, u32[]{:S(2)}, u32[]{:S(2)}) collective-permute-start(f32[4,16,24,128]{3,2,1,0:T(8,128)} %get-tuple-element.87), channel_id=1, source_target_pairs={{4,0},{8,4},{12,8},{5,1},{9,5},{13,9},{6,2},{10,6},{14,10},{7,3},{... | collective-permute-start | bytes 2359304 | tf_op jit(solution)/shard_map/ppermute | solution.py:57
  321.7 16.3 %collective-permute-start.24 = (f32[6,20,16,128]{3,2,1,0:T(8,128)S(1)}, f32[6,20,16,128]{3,2,1,0:T(8,128)S(1)}, u32[]{:S(2)}, u32[]{:S(2)}) collective-permute-start(f32[6,20,16,128]{3,2,1,0:T(8,128)S(1)} %get-tuple-element.118), channel_id=1, source_target_pairs={{0,1},{1,2},{2,3},{4,5},{5,6},{6,7},{8,9},{9,10},{10,11},{12,13},{... | collective-permute-start | bytes 2949128 | tf_op jit(solution)/shard_map/ppermute | solution.py:57
  363.4 34.9 %collective-permute-start.32 = (f32[32,24,128]{2,1,0:T(8,128)}, f32[32,24,128]{2,1,0:T(8,128)S(1)}, u32[]{:S(2)}, u32[]{:S(2)}) collective-permute-start(f32[32,24,128]{2,1,0:T(8,128)} %get-tuple-element.100), channel_id=1, source_target_pairs={{0,16},{16,32},{32,48},{48,64},{64,80},{80,96},{96,112},{1,17},{17... | collective-permute-start | bytes 1179656 | tf_op jit(solution)/shard_map/ppermute | solution.py:57
  368.7 29.7 %collective-permute-start.33 = (f32[32,24,128]{2,1,0:T(8,128)}, f32[32,24,128]{2,1,0:T(8,128)S(1)}, u32[]{:S(2)}, u32[]{:S(2)}) collective-permute-start(f32[32,24,128]{2,1,0:T(8,128)} %get-tuple-element.101), channel_id=1, source_target_pairs={{16,0},{32,16},{48,32},{64,48},{80,64},{96,80},{112,96},{17,1},{33... | collective-permute-start | bytes 1179656 | tf_op jit(solution)/shard_map/ppermute | solution.py:57
  389.2 21.8 %collective-permute-start.26 = (f32[32,24,128]{2,1,0:T(8,128)}, f32[32,24,128]{2,1,0:T(8,128)S(1)}, u32[]{:S(2)}, u32[]{:S(2)}) collective-permute-start(f32[32,24,128]{2,1,0:T(8,128)} %get-tuple-element.91), channel_id=1, source_target_pairs={{0,16},{16,32},{32,48},{48,64},{64,80},{80,96},{96,112},{1,17},{17... | collective-permute-start | bytes 1179656 | tf_op jit(solution)/shard_map/ppermute | solution.py:57
  406.5 27.3 %collective-permute-start.34 = (f32[4,64,16,128]{3,2,1,0:T(8,128)}, f32[4,64,16,128]{3,2,1,0:T(8,128)S(1)}, u32[]{:S(2)}, u32[]{:S(2)}) collective-permute-start(f32[4,64,16,128]{3,2,1,0:T(8,128)} %get-tuple-element.103), channel_id=1, source_target_pairs={{0,1},{1,2},{2,3},{4,5},{5,6},{6,7},{8,9},{9,10},{10,11},{12,13},{... | collective-permute-start | bytes 6291464 | tf_op jit(solution)/shard_map/ppermute | solution.py:57
  408.8 27.6 %collective-permute-start.35 = (f32[4,64,16,128]{3,2,1,0:T(8,128)}, f32[4,64,16,128]{3,2,1,0:T(8,128)S(1)}, u32[]{:S(2)}, u32[]{:S(2)}) collective-permute-start(f32[4,64,16,128]{3,2,1,0:T(8,128)} %get-tuple-element.104), channel_id=1, source_target_pairs={{1,0},{2,1},{3,2},{5,4},{6,5},{7,6},{9,8},{10,9},{11,10},{13,12},{... | collective-permute-start | bytes 6291464 | tf_op jit(solution)/shard_map/ppermute | solution.py:57
  419.2 37.1 %collective-permute-start.28 = (f32[4,64,16,128]{3,2,1,0:T(8,128)}, f32[4,64,16,128]{3,2,1,0:T(8,128)S(1)}, u32[]{:S(2)}, u32[]{:S(2)}) collective-permute-start(f32[4,64,16,128]{3,2,1,0:T(8,128)} %get-tuple-element.94), channel_id=1, source_target_pairs={{0,1},{1,2},{2,3},{4,5},{5,6},{6,7},{8,9},{9,10},{10,11},{12,13},{... | collective-permute-start | bytes 6291464 | tf_op jit(solution)/shard_map/ppermute | solution.py:57
  422.6 36.6 %collective-permute-start.29 = (f32[4,64,16,128]{3,2,1,0:T(8,128)}, f32[4,64,16,128]{3,2,1,0:T(8,128)}, u32[]{:S(2)}, u32[]{:S(2)}) collective-permute-start(f32[4,64,16,128]{3,2,1,0:T(8,128)} %get-tuple-element.95), channel_id=1, source_target_pairs={{1,0},{2,1},{3,2},{5,4},{6,5},{7,6},{9,8},{10,9},{11,10},{13,12},{... | collective-permute-start | bytes 6291464 | tf_op jit(solution)/shard_map/ppermute | solution.py:57
  446.5 25.6 %collective-permute-start.36 = (f32[4,16,24,128]{3,2,1,0:T(8,128)}, f32[4,16,24,128]{3,2,1,0:T(8,128)S(1)}, u32[]{:S(2)}, u32[]{:S(2)}) collective-permute-start(f32[4,16,24,128]{3,2,1,0:T(8,128)} %get-tuple-element.106), channel_id=1, source_target_pairs={{0,4},{4,8},{8,12},{1,5},{5,9},{9,13},{2,6},{6,10},{10,14},{3,7},{... | collective-permute-start | bytes 2359304 | tf_op jit(solution)/shard_map/ppermute | solution.py:57
  449.2 22.8 %collective-permute-start.37 = (f32[4,16,24,128]{3,2,1,0:T(8,128)}, f32[4,16,24,128]{3,2,1,0:T(8,128)S(1)}, u32[]{:S(2)}, u32[]{:S(2)}) collective-permute-start(f32[4,16,24,128]{3,2,1,0:T(8,128)} %get-tuple-element.107), channel_id=1, source_target_pairs={{4,0},{8,4},{12,8},{5,1},{9,5},{13,9},{6,2},{10,6},{14,10},{7,3},{... | collective-permute-start | bytes 2359304 | tf_op jit(solution)/shard_map/ppermute | solution.py:57
  (41 other events, 277.4 us)

commit v6 on v5

--- a/solution.py
+++ b/solution.py
@@ -27,12 +27,12 @@
 S = ("yl", "co")
 F32 = jnp.float32
 BF16 = jnp.bfloat16
-LIMIT = 56 * 1024 * 1024
-
-
-def params(us):
+MIB = 1024 * 1024
+
+
+def params(us, mib):
     cost = pl.CostEstimate(flops=int(us * 1e9), bytes_accessed=int(us * 2e6), transcendentals=0)
-    return dict(compiler_params=pltpu.CompilerParams(vmem_limit_bytes=LIMIT), cost_estimate=cost)
+    return dict(compiler_params=pltpu.CompilerParams(vmem_limit_bytes=mib * MIB), cost_estimate=cost)
 
 
 def split(value):
@@ -182,7 +182,7 @@
             in_specs=ins,
             out_specs=OUT_VIEW,
             scratch_shapes=scratch,
-            **params(18),
+            **params(18, 32),
         )(taps, window, wy, wown, wpack)
     return pl.pallas_call(
         functools.partial(blur_and_divide_kernel, g),
@@ -192,7 +192,7 @@
         in_specs=ins + [of_view(g, ZC, YC, XC)],
         out_specs=(OUT_VIEW, OUT_SIDES, OUT_SIDES),
         scratch_shapes=scratch,
-        **params(24),
+        **params(24, 32),
     )(taps, window, wy, wown, wpack, data)
 
 
@@ -204,7 +204,7 @@
         out_shape=(VIEW_SHAPE, SIDES_SHAPE, SIDES_SHAPE),
         in_specs=[of_view(g, ZC, YC, XC), OUT_VIEW],
         out_specs=(OUT_VIEW, OUT_SIDES, OUT_SIDES),
-        **params(5),
+        **params(5, 16),
     )(data, blurred)
 
 
@@ -246,7 +246,7 @@
             pl.BlockSpec((1, 2, 2 * XC, 2 * XC), lambda v: (v + g * GROUP, 0, 0, 0)),
         ],
         out_specs=(view, edge, edge),
-        **params(8),
+        **params(8, 20),
     )(ratio, before, after, wown, wside)
 
 
@@ -282,7 +282,7 @@
         out_shape=(jax.ShapeDtypeStruct((GROUP, ZC, YC, XC), F32), face_shape, face_shape),
         in_specs=[view, edge, edge, of_view(g, 64, 2 * YK)],
         out_specs=(view, face, face),
-        **params(8),
+        **params(8, 16),
     )(value, before, after, wy)
 
 
@@ -305,7 +305,7 @@
         sides_kernel,
         name="sides",
         out_shape=jax.ShapeDtypeStruct((first.shape[0] // 4,) + first.shape[1:], F32),
-        **params(1),
+        **params(1, 16),
     )(first, last)
 
 
@@ -362,7 +362,7 @@
             in_specs=ins,
             out_specs=chunk,
             scratch_shapes=[win],
-            **params(9),
+            **params(9, 16),
         )(*args)
     return pl.pallas_call(
         functools.partial(last_logs_kernel, g),
@@ -372,7 +372,7 @@
         in_specs=ins + [chunk, chunk],
         out_specs=(chunk, packed),
         scratch_shapes=[win, pltpu.VMEM((ZC, YC, XC), F32)],
-        **params(10),
+        **params(10, 20),
     )(*args, logs, estimate)
 
 
@@ -389,14 +389,11 @@
     return jnp.concatenate([before[None], blocks, after[None]], axis=0)
 
 
-def first_columns(slab):
+def first_window(slab):
     padded = jnp.pad(slab, ((0, 0), (HALO, HALO), (XC, XC)))
     c = lax.axis_index(V)
     before, own, after = (lax.dynamic_slice_in_dim(padded, XC * (c + k), XC, axis=2) for k in range(3))
-    return jnp.concatenate([own, pack(before, after)], axis=0)
-
-
-def first_window(planes, matrix):
+    planes = jnp.concatenate([own, pack(before, after)], axis=0)
     me = lax.axis_index(S)
 
     def rows(k):
@@ -405,7 +402,6 @@
     got = [rows(me)]
     for k in range(1, SLABS):
         got.append(lax.ppermute(rows(me ^ k), S, [(i, i ^ k) for i in range(SLABS)]))
-    *got, _ = lax.optimization_barrier((*got, matrix))
     got = jnp.stack(got)
     blocks = jnp.stack([lax.dynamic_index_in_dim(got, me ^ k, 0, keepdims=False) for k in range(SLABS)])
     return add_z(blocks)
@@ -476,7 +472,7 @@
         + [jax.ShapeDtypeStruct((VIEWS,) + shape, BF16) for shape in shapes],
         in_specs=[pl.BlockSpec(memory_space=pltpu.SMEM)],
         out_specs=[pl.BlockSpec((YC, 3 * YK), lambda v: (v, 0))] + [of_view(0, *shape) for shape in shapes],
-        **params(10),
+        **params(1, 16),
     )(taps)
     return (fy, fx, fp), (ax, side), ay
 
@@ -496,7 +492,7 @@
         out_shape=jax.ShapeDtypeStruct((DEPTH, SLABS * YC, VIEWS * XC), F32),
         in_specs=[pl.BlockSpec((VIEWS, SLABS, planes, YC, XC), lambda b: (0, 0, b, 0, 0))],
         out_specs=pl.BlockSpec((planes, SLABS * YC, VIEWS * XC), lambda b: (b, 0, 0)),
-        **params(5),
+        **params(5, 16),
     )(got)
 
 
@@ -504,12 +500,11 @@
     everyone = gather_views(kernels[0])
     blocks = views_data[0].reshape(DEPTH, SLABS, YC, VIEWS, XC).transpose(3, 1, 0, 2, 4)
     blocks = blocks.reshape(VIEWS * SLABS, DEPTH, YC, XC)
-    planes = first_columns(estimate)
-    blocks, planes, everyone = lax.optimization_barrier((blocks, planes, everyone))
+    blocks, everyone = lax.optimization_barrier((blocks, everyone))
     data = lax.all_to_all(blocks, V + S, 0, 0, tiled=True).reshape(VIEWS, ZC, YC, XC)
     taps = (everyone / jnp.sum(everyone, axis=-1, keepdims=True)).reshape(VIEWS, 3 * TAPS)
     w_forward, w_x, w_y = matrices(taps)
-    window = first_window(planes, w_y)
+    window = first_window(estimate)
     chunk = window[1 : 1 + SLABS, :DEPTH, HALO : HALO + YC].reshape(ZC, YC, XC)
     groups = range(VIEWS // GROUP)
     for number in range(ITERS):

time: 599 us -> 523 us (0.87)
  Pallas kernels: 213 us -> 163 us
  starting transfers between devices: 121 us -> 113 us
  waiting for transfers between devices: 131 us -> 125 us
    ppermute x3, waiting for transfers between devices: 42.5 us -> 0.01 us  [first_window(): lax.ppermute(rows(me ^ k), S, [(i, i ^ k) for i in range(SLABS)])]
    pallas_call x4, Pallas kernels: 29.2 us -> 12.5 us  [adjoint_x(): pl.pallas_call(adjoint_x_kernel, name='adjoint_x', grid=(GROUP,), out_sha...]
    ppermute x3, waiting for transfers between devices: 0.01 us -> 16.5 us  [gather_views(): rows = rows + lax.ppermute(rows, V, [(i, i ^ k) for i in range(VIEWS)])]
    pallas_call x4, Pallas kernels: 35.2 us -> 23.6 us  [adjoint_y(): pl.pallas_call(adjoint_y_kernel, name='adjoint_y', grid=(GROUP,), out_sha...]
    all_to_all x1, waiting for transfers between devices: 0.01 us -> 10.4 us  [per_device(): lax.all_to_all(blocks, V + S, 0, 0, tiled=True).reshape(VIEWS, ZC, YC, XC)]
    ppermute x32, waiting for transfers between devices: 88.2 us -> 98.2 us  [exchange(): return (lax.ppermute(high, axis, up), lax.ppermute(low, axis, down))]
    ppermute x32, starting transfers between devices: 105 us -> 97.1 us  [exchange(): return (lax.ppermute(high, axis, up), lax.ppermute(low, axis, down))]
    unnamed x59 -> x53, local copies, waits for them, and re-layouts: 20.7 us -> 20.5 us
  transfers between devices with their start and end apart: 39 -> 39, of which waited for: 19 -> 23; matrix products, arithmetic and copies ran while one was open for 3% -> 4% of each run, Pallas kernels for 26% -> 22%
where the time goes in v6:
time: 523 us; the launch traced here: 521 us
  Pallas kernels  163 us (31%)
  waiting for transfers between devices  125 us (24%)
  starting transfers between devices  113 us (22%)
  blocking collectives  86.2 us (16%)
  local copies, waits for them, and re-layouts  29.2 us (6%)
    ppermute x32, waiting for transfers between devices, exchange(): return (lax.ppermute(high, axis, up), lax.ppermute(low, axis, down))  98.2 us
    ppermute x32, starting transfers between devices, exchange(): return (lax.ppermute(high, axis, up), lax.ppermute(low, axis, down))  97.1 us
    all_to_all x1, blocking collectives, per_device(): lax.all_to_all(parts, V + S, 0, 0, tiled=True)  86.2 us
    pallas_call x2, Pallas kernels, forward(): pl.pallas_call(functools.partial(blur_and_divide_kernel, g), name='blur_a...  35.2 us
    pallas_call x2, Pallas kernels, forward(): pl.pallas_call(functools.partial(blur_kernel, g), name='blur', grid=(GROU...  27.7 us
    pallas_call x4, Pallas kernels, adjoint_y(): pl.pallas_call(adjoint_y_kernel, name='adjoint_y', grid=(GROUP,), out_sha...  23.6 us
    pallas_call x2, Pallas kernels, adjoint_z(): pl.pallas_call(functools.partial(last_logs_kernel, g), name='last_logs',...  22 us
    unnamed x53, local copies, waits for them, and re-layouts  20.5 us
  transfers between devices with their start and end apart: 39, of which 23 were waited for; matrix products, arithmetic and copies ran while one was open for 4% of the time, Pallas kernels for 22%

profile of v6, /device:TPU:1, one launch (start us, length us, event | category | flops | bytes accessed | tf_op | source)
XLA Modules:
  0.0 521.4 jit_solution(2463533102100836135)
XLA Ops:
  23.2 16.5 %collective-permute-done.2 = f32[8,3,31]{2,1,0:T(4,128)S(1)} collective-permute-done((f32[8,3,31]{2,1,0:T(4,128)S(1)}, f32[8,3,31]{2,1,0:T(4,128)S(1)}, u32[]{:S(2)}, u32[]{:S(2)}) %collective-permute-start.2) | collective-permute-done | bytes 3008 | tf_op jit(solution)/shard_map/ppermute | solution.py:383
  52.4 11.1 %collective-permute-done.6 = f32[20,56,128]{2,1,0:T(8,128)} collective-permute-done((f32[20,56,128]{2,1,0:T(8,128)S(1)}, f32[20,56,128]{2,1,0:T(8,128)}, u32[]{:S(2)}, u32[]{:S(2)}) %collective-permute-start.6) | collective-permute-done | bytes 573472 | tf_op jit(solution)/shard_map/ppermute | solution.py:57
  68.1 9.7 %matrices.1 = (f32[192,192]{1,0:T(8,128)S(1)}, bf16[8,256,256]{2,1,0:T(8,128)(2,1)S(1)}, bf16[8,4,256,256]{3,2,1,0:T(8,128)(2,1)S(1)}, bf16[8,256,256]{2,1,0:T(8...) custom-call(f32[8,93]{1,0:T(8,128)S(1)} %reshape.33.taps), custom_call_target="tpu_custom_call" | custom-call | flops 1000000000 | bytes 2000000 | tf_op jit(solution)/shard_map/matrices/pallas_call | solution.py:467
  84.3 13.8 %blur.3.blurred = f32[4,64,24,128]{3,2,1,0:T(8,128)S(1)} custom-call(f32[8,93]{1,0:T(8,128)S(1)} %reshape.33.taps, f32[6,20,56,128]{3,2,1,0:T(8,128)S(1)} %bitcast_dynamic-update-slice_fusion.est, f32[192,192]{1,0:T(8,128)S(1)} %get-tuple-element.54.wy, bf16[8,256,256]{2,1,0:T(8,128)(2,1)S(1)} %get-tuple-element.55.wown, ...), custom_call_target="tpu_custom_call" | custom-call | flops 17999998976 | bytes 36000000 | tf_op jit(solution)/shard_map/blur/pallas_call | solution.py:177
  99.7 13.9 %blur.2.blurred = f32[4,64,24,128]{3,2,1,0:T(8,128)S(1)} custom-call(f32[8,93]{1,0:T(8,128)S(1)} %reshape.33.taps, f32[6,20,56,128]{3,2,1,0:T(8,128)S(1)} %bitcast_dynamic-update-slice_fusion.est, f32[192,192]{1,0:T(8,128)S(1)} %get-tuple-element.54.wy, bf16[8,256,256]{2,1,0:T(8,128)(2,1)S(1)} %get-tuple-element.55.wown, ...), custom_call_target="tpu_custom_call" | custom-call | flops 17999998976 | bytes 36000000 | tf_op jit(solution)/shard_map/blur/pallas_call | solution.py:177
  115.4 10.4 %all-to-all-done = f32[32,16,24,128]{3,2,1,0:T(8,128)} async-done(((f32[32,16,24,128]{3,2,1,0:T(8,128)}), f32[32,16,24,128]{3,2,1,0:T(8,128)}, u32[]{:S(2)}, u32[]{:S(2)}) %all-to-all-start) | async-done | bytes 6291488 | tf_op jit(solution)/shard_map/all_to_all | solution.py:504
  132.2 14.7 %collective-permute-start.14 = (f32[32,24,128]{2,1,0:T(8,128)S(1)}, f32[32,24,128]{2,1,0:T(8,128)S(1)}, u32[]{:S(2)}, u32[]{:S(2)}) collective-permute-start(f32[32,24,128]{2,1,0:T(8,128)S(1)} %get-tuple-element.70), channel_id=1, source_target_pairs={{0,16},{16,32},{32,48},{48,64},{64,80},{80,96},{96,112},{1,17},{17... | collective-permute-start | bytes 1179656 | tf_op jit(solution)/shard_map/ppermute | solution.py:57
  178.0 10.5 %collective-permute-done.16.before = f32[4,64,16,128]{3,2,1,0:T(8,128)S(1)} collective-permute-done((f32[4,64,16,128]{3,2,1,0:T(8,128)S(1)}, f32[4,64,16,128]{3,2,1,0:T(8,128)S(1)}, u32[]{:S(2)}, u32[]{:S(2)}) %collective-permute-start.16) | collective-permute-done | bytes 2097184 | tf_op jit(solution)/shard_map/ppermute | solution.py:57
  191.2 5.9 %adjoint_y.5 = (f32[4,64,24,128]{3,2,1,0:T(8,128)S(1)}, f32[4,16,24,128]{3,2,1,0:T(8,128)S(1)}, f32[4,16,24,128]{3,2,1,0:T(8,128)S(1)}) custom-call(f32[4,64,24,128]{3,2,1,0:T(8,128)S(1)} %get-tuple-element.72.value, f32[4,64,16,128]{3,2,1,0:T(8,128)S(1)} %collective-permute-done.16.before, f32[4,64,16,128]{3,2,1,0:T(8,128)S(1)} %collective-permute-done.17.after, ...), custom_call_target="tpu_custom_call" | custom-call | flops 8000000000 | bytes 16000000 | tf_op jit(solution)/shard_map/adjoint_y/pallas_call | solution.py:278
  203.3 7.7 %collective-permute-done.10.before = f32[4,64,16,128]{3,2,1,0:T(8,128)S(1)} collective-permute-done((f32[4,64,16,128]{3,2,1,0:T(8,128)S(1)}, f32[4,64,16,128]{3,2,1,0:T(8,128)S(1)}, u32[]{:S(2)}, u32[]{:S(2)}) %collective-permute-start.10) | collective-permute-done | bytes 2097184 | tf_op jit(solution)/shard_map/ppermute | solution.py:57
  214.0 5.9 %adjoint_y.4 = (f32[4,64,24,128]{3,2,1,0:T(8,128)S(1)}, f32[4,16,24,128]{3,2,1,0:T(8,128)S(1)}, f32[4,16,24,128]{3,2,1,0:T(8,128)S(1)}) custom-call(f32[4,64,24,128]{3,2,1,0:T(8,128)S(1)} %get-tuple-element.62.value, f32[4,64,16,128]{3,2,1,0:T(8,128)S(1)} %collective-permute-done.10.before, f32[4,64,16,128]{3,2,1,0:T(8,128)S(1)} %collective-permute-done.11.after, ...), custom_call_target="tpu_custom_call" | custom-call | flops 8000000000 | bytes 16000000 | tf_op jit(solution)/shard_map/adjoint_y/pallas_call | solution.py:278
  224.8 9.0 %first_logs.2.logs = f32[64,24,128]{2,1,0:T(8,128)S(1)} custom-call(f32[8,93]{1,0:T(8,128)S(1)} %reshape.33.taps, f32[4,64,24,128]{3,2,1,0:T(8,128)S(1)} %get-tuple-element.75.value, f32[4,16,24,128]{3,2,1,0:T(8,128)S(1)} %collective-permute-done.18.before, f32[4,16,24,128]{3,2,1,0:T(8,128)S(1)} %collective-permute-done.19.after), custom_call_target="tpu_custom_call" | custom-call | flops 8999999488 | bytes 18000000 | tf_op jit(solution)/shard_map/first_logs/pallas_call | solution.py:357
  236.3 10.6 %last_logs.2 = (f32[64,24,128]{2,1,0:T(8,128)S(1)}, f32[16,24,128]{2,1,0:T(8,128)S(1)}) custom-call(f32[8,93]{1,0:T(8,128)S(1)} %reshape.33.taps, f32[4,64,24,128]{3,2,1,0:T(8,128)S(1)} %get-tuple-element.66.value, f32[4,16,24,128]{3,2,1,0:T(8,128)S(1)} %collective-permute-done.12.before, f32[4,16,24,128]{3,2,1,0:T(8,128)S(1)} %collective-permute-done.13.after, ...), custom_call_target="tpu_custom_call" | custom-call | flops 10000000000 | bytes 20000000 | tf_op jit(solution)/shard_map/last_logs/pallas_call | solution.py:367
  276.0 8.7 %collective-permute-done.24 = f32[6,20,16,128]{3,2,1,0:T(8,128)S(1)} collective-permute-done((f32[6,20,16,128]{3,2,1,0:T(8,128)S(1)}, f32[6,20,16,128]{3,2,1,0:T(8,128)S(1)}, u32[]{:S(2)}, u32[]{:S(2)}) %collective-permute-start.24) | collective-permute-done | bytes 983072 | tf_op jit(solution)/shard_map/ppermute | solution.py:57
  289.6 17.5 %blur_and_divide.3 = (f32[4,64,24,128]{3,2,1,0:T(8,128)S(1)}, f32[32,24,128]{2,1,0:T(8,128)S(1)}, f32[32,24,128]{2,1,0:T(8,128)S(1)}) custom-call(f32[8,93]{1,0:T(8,128)S(1)} %reshape.33.taps, f32[6,20,56,128]{3,2,1,0:T(8,128)S(1)} %pad_maximum_fusion.est, f32[192,192]{1,0:T(8,128)S(1)} %copy-done.14, bf16[8,256,256]{2,1,0:T(8,128)(2,1)S(1)} %copy-done.8, ...), custom_call_target="tpu_custom_call" | custom-call | flops 24000000000 | bytes 48000000 | tf_op jit(solution)/shard_map/blur_and_divide/pallas_call | solution.py:187
  310.4 17.7 %blur_and_divide.2 = (f32[4,64,24,128]{3,2,1,0:T(8,128)S(1)}, f32[32,24,128]{2,1,0:T(8,128)S(1)}, f32[32,24,128]{2,1,0:T(8,128)S(1)}) custom-call(f32[8,93]{1,0:T(8,128)S(1)} %reshape.33.taps, f32[6,20,56,128]{3,2,1,0:T(8,128)S(1)} %pad_maximum_fusion.est, f32[192,192]{1,0:T(8,128)S(1)} %copy-done.14, bf16[8,256,256]{2,1,0:T(8,128)(2,1)S(1)} %copy-done.8, ...), custom_call_target="tpu_custom_call" | custom-call | flops 24000000000 | bytes 48000000 | tf_op jit(solution)/shard_map/blur_and_divide/pallas_call | solution.py:187
  329.8 6.9 %collective-permute-start.26 = (f32[32,24,128]{2,1,0:T(8,128)S(1)}, f32[32,24,128]{2,1,0:T(8,128)S(1)}, u32[]{:S(2)}, u32[]{:S(2)}) collective-permute-start(f32[32,24,128]{2,1,0:T(8,128)S(1)} %get-tuple-element.81), channel_id=1, source_target_pairs={{0,16},{16,32},{32,48},{48,64},{64,80},{80,96},{96,112},{1,17},{17... | collective-permute-start | bytes 1179656 | tf_op jit(solution)/shard_map/ppermute | solution.py:57
  357.3 13.3 %collective-permute-done.34.before = f32[4,64,16,128]{3,2,1,0:T(8,128)S(1)} collective-permute-done((f32[4,64,16,128]{3,2,1,0:T(8,128)S(1)}, f32[4,64,16,128]{3,2,1,0:T(8,128)S(1)}, u32[]{:S(2)}, u32[]{:S(2)}) %collective-permute-start.34) | collective-permute-done | bytes 2097184 | tf_op jit(solution)/shard_map/ppermute | solution.py:57
  374.6 5.9 %adjoint_y.7 = (f32[4,64,24,128]{3,2,1,0:T(8,128)S(1)}, f32[4,16,24,128]{3,2,1,0:T(8,128)S(1)}, f32[4,16,24,128]{3,2,1,0:T(8,128)S(1)}) custom-call(f32[4,64,24,128]{3,2,1,0:T(8,128)S(1)} %get-tuple-element.92.value, f32[4,64,16,128]{3,2,1,0:T(8,128)S(1)} %collective-permute-done.34.before, f32[4,64,16,128]{3,2,1,0:T(8,128)S(1)} %collective-permute-done.35.after, ...), custom_call_target="tpu_custom_call" | custom-call | flops 8000000000 | bytes 16000000 | tf_op jit(solution)/shard_map/adjoint_y/pallas_call | solution.py:278
  385.1 8.1 %collective-permute-done.28.before = f32[4,64,16,128]{3,2,1,0:T(8,128)S(1)} collective-permute-done((f32[4,64,16,128]{3,2,1,0:T(8,128)S(1)}, f32[4,64,16,128]{3,2,1,0:T(8,128)S(1)}, u32[]{:S(2)}, u32[]{:S(2)}) %collective-permute-start.28) | collective-permute-done | bytes 2097184 | tf_op jit(solution)/shard_map/ppermute | solution.py:57
  396.7 5.9 %adjoint_y.6 = (f32[4,64,24,128]{3,2,1,0:T(8,128)S(1)}, f32[4,16,24,128]{3,2,1,0:T(8,128)S(1)}, f32[4,16,24,128]{3,2,1,0:T(8,128)S(1)}) custom-call(f32[4,64,24,128]{3,2,1,0:T(8,128)S(1)} %get-tuple-element.83.value, f32[4,64,16,128]{3,2,1,0:T(8,128)S(1)} %collective-permute-done.28.before, f32[4,64,16,128]{3,2,1,0:T(8,128)S(1)} %collective-permute-done.29.after, ...), custom_call_target="tpu_custom_call" | custom-call | flops 8000000000 | bytes 16000000 | tf_op jit(solution)/shard_map/adjoint_y/pallas_call | solution.py:278
  407.5 9.0 %first_logs.3.logs = f32[64,24,128]{2,1,0:T(8,128)S(1)} custom-call(f32[8,93]{1,0:T(8,128)S(1)} %reshape.33.taps, f32[4,64,24,128]{3,2,1,0:T(8,128)S(1)} %get-tuple-element.95.value, f32[4,16,24,128]{3,2,1,0:T(8,128)S(1)} %collective-permute-done.36.before, f32[4,16,24,128]{3,2,1,0:T(8,128)S(1)} %collective-permute-done.37.after), custom_call_target="tpu_custom_call" | custom-call | flops 8999999488 | bytes 18000000 | tf_op jit(solution)/shard_map/first_logs/pallas_call | solution.py:357
  418.7 11.4 %last_logs.3 = (f32[64,24,128]{2,1,0:T(8,128)S(1)}, f32[16,24,128]{2,1,0:T(8,128)}) custom-call(f32[8,93]{1,0:T(8,128)S(1)} %reshape.33.taps, f32[4,64,24,128]{3,2,1,0:T(8,128)S(1)} %get-tuple-element.86.value, f32[4,16,24,128]{3,2,1,0:T(8,128)S(1)} %collective-permute-done.30.before, f32[4,16,24,128]{3,2,1,0:T(8,128)S(1)} %collective-permute-done.31.after, ...), custom_call_target="tpu_custom_call" | custom-call | flops 10000000000 | bytes 20000000 | tf_op jit(solution)/shard_map/last_logs/pallas_call | solution.py:367
  430.8 86.2 %all_to_all.10 = f32[32,16,24,128]{3,2,1,0:T(8,128)S(1)} all-to-all(f32[32,16,24,128]{3,2,1,0:T(8,128)S(1)} %bitcast.44), channel_id=1, replica_groups=mesh['yh'=2,'x'=4,'z'=4,'yl'=2,'co'=2] {'yh','x','yl','co'}, dimensions={0} | all-to-all | bytes 12582912 | tf_op jit(solution)/shard_map/all_to_all | solution.py:535
  (151 shorter events, 190.5 us)
Async XLA Ops:
  9.1 36.2 %collective-permute-start.3 = (f32[20,56,128]{2,1,0:T(8,128)}, f32[20,56,128]{2,1,0:T(8,128)S(1)}, u32[]{:S(2)}, u32[]{:S(2)}) collective-permute-start(f32[20,56,128]{2,1,0:T(8,128)} %get-tuple-element.111), channel_id=1, source_target_pairs={{0,1},{1,0},{2,3},{3,2},{4,5},{5,4},{6,7},{7,6},{8,9},{9,8},{10,11... | collective-permute-start | bytes 1720328 | tf_op jit(solution)/shard_map/ppermute | solution.py:404
  10.3 35.0 %collective-permute-start.4 = (f32[20,56,128]{2,1,0:T(8,128)S(1)}, f32[20,56,128]{2,1,0:T(8,128)S(1)}, u32[]{:S(2)}, u32[]{:S(2)}) collective-permute-start(f32[20,56,128]{2,1,0:T(8,128)S(1)} %get-tuple-element.112), channel_id=1, source_target_pairs={{0,2},{1,3},{2,0},{3,1},{4,6},{5,7},{6,4},{7,5},{8,10},{9,11},{10,... | collective-permute-start | bytes 1720328 | tf_op jit(solution)/shard_map/ppermute | solution.py:404
  11.6 33.7 %collective-permute-start.5 = (f32[20,56,128]{2,1,0:T(8,128)S(1)}, f32[20,56,128]{2,1,0:T(8,128)}, u32[]{:S(2)}, u32[]{:S(2)}) collective-permute-start(f32[20,56,128]{2,1,0:T(8,128)S(1)} %get-tuple-element.113), channel_id=1, source_target_pairs={{0,3},{1,2},{2,1},{3,0},{4,7},{5,6},{6,5},{7,4},{8,11},{9,10},{10,... | collective-permute-start | bytes 1720328 | tf_op jit(solution)/shard_map/ppermute | solution.py:404
  12.0 27.7 %collective-permute-start.2 = (f32[8,3,31]{2,1,0:T(4,128)S(1)}, f32[8,3,31]{2,1,0:T(4,128)S(1)}, u32[]{:S(2)}, u32[]{:S(2)}) collective-permute-start(f32[8,3,31]{2,1,0:T(4,128)S(1)} %fusion.12), channel_id=1, source_target_pairs={{0,64},{16,80},{32,96},{48,112},{64,0},{80,16},{96,32},{112,48},{1... | collective-permute-start | bytes 8936 | tf_op jit(solution)/shard_map/ppermute | solution.py:383
  39.7 86.0 %all-to-all-start = ((f32[32,16,24,128]{3,2,1,0:T(8,128)}), f32[32,16,24,128]{3,2,1,0:T(8,128)}, u32[]{:S(2)}, u32[]{:S(2)}) async-start(f32[32,16,24,128]{3,2,1,0:T(8,128)} %bitcast.43), calls=%async_computation | async-start | bytes 12582912 | tf_op jit(solution)/shard_map/all_to_all | solution.py:504
  66.6 16.6 %collective-permute-start.7 = (f32[20,56,128]{2,1,0:T(8,128)}, f32[20,56,128]{2,1,0:T(8,128)}, u32[]{:S(2)}, u32[]{:S(2)}) collective-permute-start(f32[20,56,128]{2,1,0:T(8,128)} %bitcast.9), channel_id=1, source_target_pairs={{4,0},{8,4},{12,8},{5,1},{9,5},{13,9},{6,2},{10,6},{14,10},{7,3},{... | collective-permute-start | bytes 1720328 | tf_op jit(solution)/shard_map/ppermute | solution.py:57
  132.2 26.1 %collective-permute-start.14 = (f32[32,24,128]{2,1,0:T(8,128)S(1)}, f32[32,24,128]{2,1,0:T(8,128)S(1)}, u32[]{:S(2)}, u32[]{:S(2)}) collective-permute-start(f32[32,24,128]{2,1,0:T(8,128)S(1)} %get-tuple-element.70), channel_id=1, source_target_pairs={{0,16},{16,32},{32,48},{48,64},{64,80},{80,96},{96,112},{1,17},{17... | collective-permute-start | bytes 1179656 | tf_op jit(solution)/shard_map/ppermute | solution.py:57
  161.8 26.8 %collective-permute-start.16 = (f32[4,64,16,128]{3,2,1,0:T(8,128)S(1)}, f32[4,64,16,128]{3,2,1,0:T(8,128)S(1)}, u32[]{:S(2)}, u32[]{:S(2)}) collective-permute-start(f32[4,64,16,128]{3,2,1,0:T(8,128)S(1)} %get-tuple-element.73), channel_id=1, source_target_pairs={{0,1},{1,2},{2,3},{4,5},{5,6},{6,7},{8,9},{9,10},{10,11},{12,13},{... | collective-permute-start | bytes 6291464 | tf_op jit(solution)/shard_map/ppermute | solution.py:57
  163.9 27.4 %collective-permute-start.17 = (f32[4,64,16,128]{3,2,1,0:T(8,128)S(1)}, f32[4,64,16,128]{3,2,1,0:T(8,128)S(1)}, u32[]{:S(2)}, u32[]{:S(2)}) collective-permute-start(f32[4,64,16,128]{3,2,1,0:T(8,128)S(1)} %get-tuple-element.74), channel_id=1, source_target_pairs={{1,0},{2,1},{3,2},{5,4},{6,5},{7,6},{9,8},{10,9},{11,10},{13,12},{... | collective-permute-start | bytes 6291464 | tf_op jit(solution)/shard_map/ppermute | solution.py:57
  170.9 40.1 %collective-permute-start.10 = (f32[4,64,16,128]{3,2,1,0:T(8,128)S(1)}, f32[4,64,16,128]{3,2,1,0:T(8,128)S(1)}, u32[]{:S(2)}, u32[]{:S(2)}) collective-permute-start(f32[4,64,16,128]{3,2,1,0:T(8,128)S(1)} %get-tuple-element.63), channel_id=1, source_target_pairs={{0,1},{1,2},{2,3},{4,5},{5,6},{6,7},{8,9},{9,10},{10,11},{12,13},{... | collective-permute-start | bytes 6291464 | tf_op jit(solution)/shard_map/ppermute | solution.py:57
  172.9 41.1 %collective-permute-start.11 = (f32[4,64,16,128]{3,2,1,0:T(8,128)S(1)}, f32[4,64,16,128]{3,2,1,0:T(8,128)S(1)}, u32[]{:S(2)}, u32[]{:S(2)}) collective-permute-start(f32[4,64,16,128]{3,2,1,0:T(8,128)S(1)} %get-tuple-element.64), channel_id=1, source_target_pairs={{1,0},{2,1},{3,2},{5,4},{6,5},{7,6},{9,8},{10,9},{11,10},{13,12},{... | collective-permute-start | bytes 6291464 | tf_op jit(solution)/shard_map/ppermute | solution.py:57
  197.1 27.6 %collective-permute-start.18 = (f32[4,16,24,128]{3,2,1,0:T(8,128)S(1)}, f32[4,16,24,128]{3,2,1,0:T(8,128)S(1)}, u32[]{:S(2)}, u32[]{:S(2)}) collective-permute-start(f32[4,16,24,128]{3,2,1,0:T(8,128)S(1)} %get-tuple-element.76), channel_id=1, source_target_pairs={{0,4},{4,8},{8,12},{1,5},{5,9},{9,13},{2,6},{6,10},{10,14},{3,7},{... | collective-permute-start | bytes 2359304 | tf_op jit(solution)/shard_map/ppermute | solution.py:57
  201.0 23.7 %collective-permute-start.19 = (f32[4,16,24,128]{3,2,1,0:T(8,128)S(1)}, f32[4,16,24,128]{3,2,1,0:T(8,128)S(1)}, u32[]{:S(2)}, u32[]{:S(2)}) collective-permute-start(f32[4,16,24,128]{3,2,1,0:T(8,128)S(1)} %get-tuple-element.77), channel_id=1, source_target_pairs={{4,0},{8,4},{12,8},{5,1},{9,5},{13,9},{6,2},{10,6},{14,10},{7,3},{... | collective-permute-start | bytes 2359304 | tf_op jit(solution)/shard_map/ppermute | solution.py:57
  268.1 16.5 %collective-permute-start.24 = (f32[6,20,16,128]{3,2,1,0:T(8,128)S(1)}, f32[6,20,16,128]{3,2,1,0:T(8,128)S(1)}, u32[]{:S(2)}, u32[]{:S(2)}) collective-permute-start(f32[6,20,16,128]{3,2,1,0:T(8,128)S(1)} %get-tuple-element.108), channel_id=1, source_target_pairs={{0,1},{1,2},{2,3},{4,5},{5,6},{6,7},{8,9},{9,10},{10,11},{12,13},{... | collective-permute-start | bytes 2949128 | tf_op jit(solution)/shard_map/ppermute | solution.py:57
  273.6 15.7 %collective-permute-start.25 = (f32[6,20,16,128]{3,2,1,0:T(8,128)S(1)}, f32[6,20,16,128]{3,2,1,0:T(8,128)S(1)}, u32[]{:S(2)}, u32[]{:S(2)}) collective-permute-start(f32[6,20,16,128]{3,2,1,0:T(8,128)S(1)} %get-tuple-element.109), channel_id=1, source_target_pairs={{1,0},{2,1},{3,2},{5,4},{6,5},{7,6},{9,8},{10,9},{11,10},{13,12},{... | collective-permute-start | bytes 2949128 | tf_op jit(solution)/shard_map/ppermute | solution.py:57
  307.1 30.9 %collective-permute-start.32 = (f32[32,24,128]{2,1,0:T(8,128)S(1)}, f32[32,24,128]{2,1,0:T(8,128)S(1)}, u32[]{:S(2)}, u32[]{:S(2)}) collective-permute-start(f32[32,24,128]{2,1,0:T(8,128)S(1)} %get-tuple-element.90), channel_id=1, source_target_pairs={{0,16},{16,32},{32,48},{48,64},{64,80},{80,96},{96,112},{1,17},{17... | collective-permute-start | bytes 1179656 | tf_op jit(solution)/shard_map/ppermute | solution.py:57
  309.0 29.0 %collective-permute-start.33 = (f32[32,24,128]{2,1,0:T(8,128)S(1)}, f32[32,24,128]{2,1,0:T(8,128)S(1)}, u32[]{:S(2)}, u32[]{:S(2)}) collective-permute-start(f32[32,24,128]{2,1,0:T(8,128)S(1)} %get-tuple-element.91), channel_id=1, source_target_pairs={{16,0},{32,16},{48,32},{64,48},{80,64},{96,80},{112,96},{17,1},{33... | collective-permute-start | bytes 1179656 | tf_op jit(solution)/shard_map/ppermute | solution.py:57
  329.8 15.8 %collective-permute-start.26 = (f32[32,24,128]{2,1,0:T(8,128)S(1)}, f32[32,24,128]{2,1,0:T(8,128)S(1)}, u32[]{:S(2)}, u32[]{:S(2)}) collective-permute-start(f32[32,24,128]{2,1,0:T(8,128)S(1)} %get-tuple-element.81), channel_id=1, source_target_pairs={{0,16},{16,32},{32,48},{48,64},{64,80},{80,96},{96,112},{1,17},{17... | collective-permute-start | bytes 1179656 | tf_op jit(solution)/shard_map/ppermute | solution.py:57
  341.2 29.5 %collective-permute-start.34 = (f32[4,64,16,128]{3,2,1,0:T(8,128)S(1)}, f32[4,64,16,128]{3,2,1,0:T(8,128)S(1)}, u32[]{:S(2)}, u32[]{:S(2)}) collective-permute-start(f32[4,64,16,128]{3,2,1,0:T(8,128)S(1)} %get-tuple-element.93), channel_id=1, source_target_pairs={{0,1},{1,2},{2,3},{4,5},{5,6},{6,7},{8,9},{9,10},{10,11},{12,13},{... | collective-permute-start | bytes 6291464 | tf_op jit(solution)/shard_map/ppermute | solution.py:57
  343.5 31.1 %collective-permute-start.35 = (f32[4,64,16,128]{3,2,1,0:T(8,128)S(1)}, f32[4,64,16,128]{3,2,1,0:T(8,128)S(1)}, u32[]{:S(2)}, u32[]{:S(2)}) collective-permute-start(f32[4,64,16,128]{3,2,1,0:T(8,128)S(1)} %get-tuple-element.94), channel_id=1, source_target_pairs={{1,0},{2,1},{3,2},{5,4},{6,5},{7,6},{9,8},{10,9},{11,10},{13,12},{... | collective-permute-start | bytes 6291464 | tf_op jit(solution)/shard_map/ppermute | solution.py:57
  352.2 40.9 %collective-permute-start.28 = (f32[4,64,16,128]{3,2,1,0:T(8,128)S(1)}, f32[4,64,16,128]{3,2,1,0:T(8,128)S(1)}, u32[]{:S(2)}, u32[]{:S(2)}) collective-permute-start(f32[4,64,16,128]{3,2,1,0:T(8,128)S(1)} %get-tuple-element.84), channel_id=1, source_target_pairs={{0,1},{1,2},{2,3},{4,5},{5,6},{6,7},{8,9},{9,10},{10,11},{12,13},{... | collective-permute-start | bytes 6291464 | tf_op jit(solution)/shard_map/ppermute | solution.py:57
  355.4 41.4 %collective-permute-start.29 = (f32[4,64,16,128]{3,2,1,0:T(8,128)S(1)}, f32[4,64,16,128]{3,2,1,0:T(8,128)S(1)}, u32[]{:S(2)}, u32[]{:S(2)}) collective-permute-start(f32[4,64,16,128]{3,2,1,0:T(8,128)S(1)} %get-tuple-element.85), channel_id=1, source_target_pairs={{1,0},{2,1},{3,2},{5,4},{6,5},{7,6},{9,8},{10,9},{11,10},{13,12},{... | collective-permute-start | bytes 6291464 | tf_op jit(solution)/shard_map/ppermute | solution.py:57
  380.5 27.0 %collective-permute-start.36 = (f32[4,16,24,128]{3,2,1,0:T(8,128)S(1)}, f32[4,16,24,128]{3,2,1,0:T(8,128)S(1)}, u32[]{:S(2)}, u32[]{:S(2)}) collective-permute-start(f32[4,16,24,128]{3,2,1,0:T(8,128)S(1)} %get-tuple-element.96), channel_id=1, source_target_pairs={{0,4},{4,8},{8,12},{1,5},{5,9},{9,13},{2,6},{6,10},{10,14},{3,7},{... | collective-permute-start | bytes 2359304 | tf_op jit(solution)/shard_map/ppermute | solution.py:57
  383.8 23.7 %collective-permute-start.37 = (f32[4,16,24,128]{3,2,1,0:T(8,128)S(1)}, f32[4,16,24,128]{3,2,1,0:T(8,128)S(1)}, u32[]{:S(2)}, u32[]{:S(2)}) collective-permute-start(f32[4,16,24,128]{3,2,1,0:T(8,128)S(1)} %get-tuple-element.97), channel_id=1, source_target_pairs={{4,0},{8,4},{12,8},{5,1},{9,5},{13,9},{6,2},{10,6},{14,10},{7,3},{... | collective-permute-start | bytes 2359304 | tf_op jit(solution)/shard_map/ppermute | solution.py:57
  (38 other events, 435.0 us)

commit v7 on v6

--- a/solution.py
+++ b/solution.py
@@ -192,7 +192,7 @@
         in_specs=ins + [of_view(g, ZC, YC, XC)],
         out_specs=(OUT_VIEW, OUT_SIDES, OUT_SIDES),
         scratch_shapes=scratch,
-        **params(24, 32),
+        **params(1, 32),
     )(taps, window, wy, wown, wpack, data)
 
 
@@ -246,7 +246,7 @@
             pl.BlockSpec((1, 2, 2 * XC, 2 * XC), lambda v: (v + g * GROUP, 0, 0, 0)),
         ],
         out_specs=(view, edge, edge),
-        **params(8, 20),
+        **params(1, 20),
     )(ratio, before, after, wown, wside)
 
 
@@ -512,17 +512,23 @@
             window = next_window(chunk, sides)
         if not number:
             blurred = [forward(g, taps, window, None, *w_forward) for g in groups]
-        faces = []
-        for g in groups:
-            if number:
+            data, *blurred = lax.optimization_barrier((data, *blurred))
+        edges = []
+        if number:
+            for g in groups:
                 ratio, left, right = forward(g, taps, window, data, *w_forward)
-            else:
-                ratio, left, right = divide_by(g, data, blurred[g])
-            faces.append((ratio,) + exchange(left, right, V, VIEWS))
-        edges = []
-        for g in groups:
-            value, top, bottom = adjoint_x(g, *faces[g], *w_x)
-            edges.append((value,) + exchange(top, bottom, S, SLABS))
+                value, top, bottom = adjoint_x(g, ratio, *exchange(left, right, V, VIEWS), *w_x)
+                if g == 0:
+                    window, top, bottom = lax.optimization_barrier((window, top, bottom))
+                edges.append((value,) + exchange(top, bottom, S, SLABS))
+        else:
+            divided = [divide_by(g, data, blurred[g]) for g in groups]
+            for g in groups:
+                ratio, left, right = divided[g]
+                if g:
+                    left, right, *_ = lax.optimization_barrier((left, right, top, bottom))
+                value, top, bottom = adjoint_x(g, ratio, *exchange(left, right, V, VIEWS), *w_x)
+                edges.append((value,) + exchange(top, bottom, S, SLABS))
         ends = []
         for g in groups:
             value, low, high = adjoint_y(g, *edges[g], w_y)

time: 523 us -> 534 us (1.021)
  waiting for transfers between devices: 125 us -> 137 us
    ppermute x32, waiting for transfers between devices: 98.2 us -> 112 us  [exchange(): return (lax.ppermute(high, axis, up), lax.ppermute(low, axis, down))]
    unnamed x53 -> x35, local copies, waits for them, and re-layouts: 20.5 us -> 17.1 us
  transfers between devices with their start and end apart: 39 -> 39, of which waited for: 23 -> 25; matrix products, arithmetic and copies ran while one was open for 4% -> 4% of each run, Pallas kernels for 22% -> 21%
where the time goes in v7:
time: 534 us; the launch traced here: 533 us
  Pallas kernels  167 us (31%)
  waiting for transfers between devices  137 us (26%)
  starting transfers between devices  111 us (21%)
  blocking collectives  86.9 us (16%)
  local copies, waits for them, and re-layouts  26.6 us (5%)
    ppermute x32, waiting for transfers between devices, exchange(): return (lax.ppermute(high, axis, up), lax.ppermute(low, axis, down))  112 us
    ppermute x32, starting transfers between devices, exchange(): return (lax.ppermute(high, axis, up), lax.ppermute(low, axis, down))  94.3 us
    all_to_all x1, blocking collectives, per_device(): lax.all_to_all(parts, V + S, 0, 0, tiled=True)  86.9 us
    pallas_call x2, Pallas kernels, forward(): pl.pallas_call(functools.partial(blur_and_divide_kernel, g), name='blur_a...  35.1 us
    pallas_call x2, Pallas kernels, forward(): pl.pallas_call(functools.partial(blur_kernel, g), name='blur', grid=(GROU...  30.4 us
    pallas_call x4, Pallas kernels, adjoint_y(): pl.pallas_call(adjoint_y_kernel, name='adjoint_y', grid=(GROUP,), out_sha...  24.5 us
    pallas_call x2, Pallas kernels, adjoint_z(): pl.pallas_call(functools.partial(last_logs_kernel, g), name='last_logs',...  22 us
    pallas_call x2, Pallas kernels, adjoint_z(): pl.pallas_call(functools.partial(first_logs_kernel, g), name='first_logs'...  17.9 us
  transfers between devices with their start and end apart: 39, of which 25 were waited for; matrix products, arithmetic and copies ran while one was open for 4% of the time, Pallas kernels for 21%

profile of v7, /device:TPU:1, one launch (start us, length us, event | category | flops | bytes accessed | tf_op | source)
XLA Modules:
  0.0 532.9 jit_solution(14133086502004477649)
XLA Ops:
  23.3 16.5 %collective-permute-done.2 = f32[8,3,31]{2,1,0:T(4,128)S(1)} collective-permute-done((f32[8,3,31]{2,1,0:T(4,128)S(1)}, f32[8,3,31]{2,1,0:T(4,128)S(1)}, u32[]{:S(2)}, u32[]{:S(2)}) %collective-permute-start.2) | collective-permute-done | bytes 3008 | tf_op jit(solution)/shard_map/ppermute | solution.py:383
  51.7 11.9 %collective-permute-done.6 = f32[20,56,128]{2,1,0:T(8,128)S(1)} collective-permute-done((f32[20,56,128]{2,1,0:T(8,128)S(1)}, f32[20,56,128]{2,1,0:T(8,128)S(1)}, u32[]{:S(2)}, u32[]{:S(2)}) %collective-permute-start.6) | collective-permute-done | bytes 573472 | tf_op jit(solution)/shard_map/ppermute | solution.py:57
  66.9 9.7 %matrices.1 = (f32[192,192]{1,0:T(8,128)S(1)}, bf16[8,256,256]{2,1,0:T(8,128)(2,1)S(1)}, bf16[8,4,256,256]{3,2,1,0:T(8,128)(2,1)S(1)}, bf16[8,256,256]{2,1,0:T(8...) custom-call(f32[8,93]{1,0:T(8,128)S(1)} %reshape.33.taps), custom_call_target="tpu_custom_call" | custom-call | flops 1000000000 | bytes 2000000 | tf_op jit(solution)/shard_map/matrices/pallas_call | solution.py:467
  84.1 15.3 %blur.3.blurred = f32[4,64,24,128]{3,2,1,0:T(8,128)S(1)} custom-call(f32[8,93]{1,0:T(8,128)S(1)} %reshape.33.taps, f32[6,20,56,128]{3,2,1,0:T(8,128)} %bitcast_dynamic-update-slice_fusion.est, f32[192,192]{1,0:T(8,128)S(1)} %get-tuple-element.62.wy, bf16[8,256,256]{2,1,0:T(8,128)(2,1)S(1)} %get-tuple-element.63.wown, ...), custom_call_target="tpu_custom_call" | custom-call | flops 17999998976 | bytes 36000000 | tf_op jit(solution)/shard_map/blur/pallas_call | solution.py:177
  101.0 15.1 %blur.2.blurred = f32[4,64,24,128]{3,2,1,0:T(8,128)S(1)} custom-call(f32[8,93]{1,0:T(8,128)S(1)} %reshape.33.taps, f32[6,20,56,128]{3,2,1,0:T(8,128)} %bitcast_dynamic-update-slice_fusion.est, f32[192,192]{1,0:T(8,128)S(1)} %get-tuple-element.62.wy, bf16[8,256,256]{2,1,0:T(8,128)(2,1)S(1)} %get-tuple-element.63.wown, ...), custom_call_target="tpu_custom_call" | custom-call | flops 17999998976 | bytes 36000000 | tf_op jit(solution)/shard_map/blur/pallas_call | solution.py:177
  117.9 7.9 %all-to-all-done = f32[32,16,24,128]{3,2,1,0:T(8,128)} async-done(((f32[32,16,24,128]{3,2,1,0:T(8,128)}), f32[32,16,24,128]{3,2,1,0:T(8,128)}, u32[]{:S(2)}, u32[]{:S(2)}) %all-to-all-start) | async-done | bytes 6291488 | tf_op jit(solution)/shard_map/all_to_all | solution.py:504
  132.1 14.7 %collective-permute-start.8 = (f32[32,24,128]{2,1,0:T(8,128)S(1)}, f32[32,24,128]{2,1,0:T(8,128)S(1)}, u32[]{:S(2)}, u32[]{:S(2)}) collective-permute-start(f32[32,24,128]{2,1,0:T(8,128)S(1)} %get-tuple-element.72), channel_id=1, source_target_pairs={{0,16},{16,32},{32,48},{48,64},{64,80},{80,96},{96,112},{1,17},{17... | collective-permute-start | bytes 1179656 | tf_op jit(solution)/shard_map/ppermute | solution.py:57
  148.1 6.2 %collective-permute-done.8.before = f32[32,24,128]{2,1,0:T(8,128)S(1)} collective-permute-done((f32[32,24,128]{2,1,0:T(8,128)S(1)}, f32[32,24,128]{2,1,0:T(8,128)S(1)}, u32[]{:S(2)}, u32[]{:S(2)}) %collective-permute-start.8) | collective-permute-done | bytes 393248 | tf_op jit(solution)/shard_map/ppermute | solution.py:57
  175.0 6.5 %collective-permute-done.10.before = f32[32,24,128]{2,1,0:T(8,128)S(1)} collective-permute-done((f32[32,24,128]{2,1,0:T(8,128)S(1)}, f32[32,24,128]{2,1,0:T(8,128)S(1)}, u32[]{:S(2)}, u32[]{:S(2)}) %collective-permute-start.10) | collective-permute-done | bytes 393248 | tf_op jit(solution)/shard_map/ppermute | solution.py:57
  198.5 5.8 %adjoint_y.5 = (f32[4,64,24,128]{3,2,1,0:T(8,128)S(1)}, f32[4,16,24,128]{3,2,1,0:T(8,128)S(1)}, f32[4,16,24,128]{3,2,1,0:T(8,128)S(1)}) custom-call(f32[4,64,24,128]{3,2,1,0:T(8,128)S(1)} %get-tuple-element.87.value, f32[4,64,16,128]{3,2,1,0:T(8,128)S(1)} %collective-permute-done.16.before, f32[4,64,16,128]{3,2,1,0:T(8,128)S(1)} %collective-permute-done.17.after, ...), custom_call_target="tpu_custom_call" | custom-call | flops 8000000000 | bytes 16000000 | tf_op jit(solution)/shard_map/adjoint_y/pallas_call | solution.py:278
  210.3 10.7 %collective-permute-done.12.before = f32[4,64,16,128]{3,2,1,0:T(8,128)S(1)} collective-permute-done((f32[4,64,16,128]{3,2,1,0:T(8,128)S(1)}, f32[4,64,16,128]{3,2,1,0:T(8,128)S(1)}, u32[]{:S(2)}, u32[]{:S(2)}) %collective-permute-start.12) | collective-permute-done | bytes 2097184 | tf_op jit(solution)/shard_map/ppermute | solution.py:57
  231.8 9.0 %first_logs.2.logs = f32[64,24,128]{2,1,0:T(8,128)S(1)} custom-call(f32[8,93]{1,0:T(8,128)S(1)} %reshape.33.taps, f32[4,64,24,128]{3,2,1,0:T(8,128)S(1)} %get-tuple-element.88.value, f32[4,16,24,128]{3,2,1,0:T(8,128)S(1)} %collective-permute-done.18.before, f32[4,16,24,128]{3,2,1,0:T(8,128)S(1)} %collective-permute-done.19.after), custom_call_target="tpu_custom_call" | custom-call | flops 8999999488 | bytes 18000000 | tf_op jit(solution)/shard_map/first_logs/pallas_call | solution.py:357
  243.3 10.6 %last_logs.2 = (f32[64,24,128]{2,1,0:T(8,128)S(1)}, f32[16,24,128]{2,1,0:T(8,128)S(1)}) custom-call(f32[8,93]{1,0:T(8,128)S(1)} %reshape.33.taps, f32[4,64,24,128]{3,2,1,0:T(8,128)S(1)} %get-tuple-element.84.value, f32[4,16,24,128]{3,2,1,0:T(8,128)S(1)} %collective-permute-done.14.before, f32[4,16,24,128]{3,2,1,0:T(8,128)S(1)} %collective-permute-done.15.after, ...), custom_call_target="tpu_custom_call" | custom-call | flops 10000000000 | bytes 20000000 | tf_op jit(solution)/shard_map/last_logs/pallas_call | solution.py:367
  272.5 8.4 %collective-permute-start.24 = (f32[6,20,16,128]{3,2,1,0:T(8,128)S(1)}, f32[6,20,16,128]{3,2,1,0:T(8,128)S(1)}, u32[]{:S(2)}, u32[]{:S(2)}) collective-permute-start(f32[6,20,16,128]{3,2,1,0:T(8,128)S(1)} %get-tuple-element.124), channel_id=1, source_target_pairs={{0,1},{1,2},{2,3},{4,5},{5,6},{6,7},{8,9},{9,10},{10,11},{12,13},{... | collective-permute-start | bytes 2949128 | tf_op jit(solution)/shard_map/ppermute | solution.py:57
  283.2 8.7 %collective-permute-done.24 = f32[6,20,16,128]{3,2,1,0:T(8,128)S(1)} collective-permute-done((f32[6,20,16,128]{3,2,1,0:T(8,128)S(1)}, f32[6,20,16,128]{3,2,1,0:T(8,128)S(1)}, u32[]{:S(2)}, u32[]{:S(2)}) %collective-permute-start.24) | collective-permute-done | bytes 983072 | tf_op jit(solution)/shard_map/ppermute | solution.py:57
  296.8 17.5 %blur_and_divide.2 = (f32[4,64,24,128]{3,2,1,0:T(8,128)S(1)}, f32[32,24,128]{2,1,0:T(8,128)S(1)}, f32[32,24,128]{2,1,0:T(8,128)S(1)}) custom-call(f32[8,93]{1,0:T(8,128)S(1)} %reshape.33.taps, f32[6,20,56,128]{3,2,1,0:T(8,128)S(1)} %pad_maximum_fusion.est, f32[192,192]{1,0:T(8,128)S(1)} %get-tuple-element.62.wy, bf16[8,256,256]{2,1,0:T(8,128)(2,1)S(1)} %copy-done.3, ...), custom_call_target="tpu_custom_call" | custom-call | flops 1000000000 | bytes 2000000 | tf_op jit(solution)/shard_map/blur_and_divide/pallas_call | solution.py:187
  336.4 17.7 %blur_and_divide.3 = (f32[4,64,24,128]{3,2,1,0:T(8,128)S(1)}, f32[32,24,128]{2,1,0:T(8,128)S(1)}, f32[32,24,128]{2,1,0:T(8,128)S(1)}) custom-call(f32[8,93]{1,0:T(8,128)S(1)} %reshape.33.taps, f32[6,20,56,128]{3,2,1,0:T(8,128)S(1)} %pad_maximum_fusion.est, f32[192,192]{1,0:T(8,128)S(1)} %get-tuple-element.62.wy, bf16[8,256,256]{2,1,0:T(8,128)(2,1)S(1)} %copy-done.3, ...), custom_call_target="tpu_custom_call" | custom-call | flops 1000000000 | bytes 2000000 | tf_op jit(solution)/shard_map/blur_and_divide/pallas_call | solution.py:187
  357.3 7.1 %collective-permute-done.28.before = f32[32,24,128]{2,1,0:T(8,128)S(1)} collective-permute-done((f32[32,24,128]{2,1,0:T(8,128)S(1)}, f32[32,24,128]{2,1,0:T(8,128)S(1)}, u32[]{:S(2)}, u32[]{:S(2)}) %collective-permute-start.28) | collective-permute-done | bytes 393248 | tf_op jit(solution)/shard_map/ppermute | solution.py:57
  364.3 8.9 %collective-permute-done.29.after = f32[32,24,128]{2,1,0:T(8,128)S(1)} collective-permute-done((f32[32,24,128]{2,1,0:T(8,128)S(1)}, f32[32,24,128]{2,1,0:T(8,128)S(1)}, u32[]{:S(2)}, u32[]{:S(2)}) %collective-permute-start.29) | collective-permute-done | bytes 393248 | tf_op jit(solution)/shard_map/ppermute | solution.py:57
  382.0 7.0 %adjoint_y.7 = (f32[4,64,24,128]{3,2,1,0:T(8,128)S(1)}, f32[4,16,24,128]{3,2,1,0:T(8,128)S(1)}, f32[4,16,24,128]{3,2,1,0:T(8,128)S(1)}) custom-call(f32[4,64,24,128]{3,2,1,0:T(8,128)S(1)} %get-tuple-element.108.value, f32[4,64,16,128]{3,2,1,0:T(8,128)S(1)} %collective-permute-done.34.before, f32[4,64,16,128]{3,2,1,0:T(8,128)} %collective-permute-done.35.after, ...), custom_call_target="tpu_custom_call" | custom-call | flops 8000000000 | bytes 16000000 | tf_op jit(solution)/shard_map/adjoint_y/pallas_call | solution.py:278
  393.6 9.4 %collective-permute-done.30.before = f32[4,64,16,128]{3,2,1,0:T(8,128)S(1)} collective-permute-done((f32[4,64,16,128]{3,2,1,0:T(8,128)S(1)}, f32[4,64,16,128]{3,2,1,0:T(8,128)S(1)}, u32[]{:S(2)}, u32[]{:S(2)}) %collective-permute-start.30) | collective-permute-done | bytes 2097184 | tf_op jit(solution)/shard_map/ppermute | solution.py:57
  418.4 9.0 %first_logs.3.logs = f32[64,24,128]{2,1,0:T(8,128)S(1)} custom-call(f32[8,93]{1,0:T(8,128)S(1)} %reshape.33.taps, f32[4,64,24,128]{3,2,1,0:T(8,128)S(1)} %get-tuple-element.111.value, f32[4,16,24,128]{3,2,1,0:T(8,128)S(1)} %collective-permute-done.36.before, f32[4,16,24,128]{3,2,1,0:T(8,128)S(1)} %collective-permute-done.37.after), custom_call_target="tpu_custom_call" | custom-call | flops 8999999488 | bytes 18000000 | tf_op jit(solution)/shard_map/first_logs/pallas_call | solution.py:357
  429.6 11.4 %last_logs.3 = (f32[64,24,128]{2,1,0:T(8,128)S(1)}, f32[16,24,128]{2,1,0:T(8,128)}) custom-call(f32[8,93]{1,0:T(8,128)S(1)} %reshape.33.taps, f32[4,64,24,128]{3,2,1,0:T(8,128)S(1)} %get-tuple-element.105.value, f32[4,16,24,128]{3,2,1,0:T(8,128)S(1)} %collective-permute-done.32.before, f32[4,16,24,128]{3,2,1,0:T(8,128)S(1)} %collective-permute-done.33.after, ...), custom_call_target="tpu_custom_call" | custom-call | flops 10000000000 | bytes 20000000 | tf_op jit(solution)/shard_map/last_logs/pallas_call | solution.py:367
  441.6 86.9 %all_to_all.10 = f32[32,16,24,128]{3,2,1,0:T(8,128)S(1)} all-to-all(f32[32,16,24,128]{3,2,1,0:T(8,128)S(1)} %bitcast.44), channel_id=1, replica_groups=mesh['yh'=2,'x'=4,'z'=4,'yl'=2,'co'=2] {'yh','x','yl','co'}, dimensions={0} | all-to-all | bytes 12582912 | tf_op jit(solution)/shard_map/all_to_all | solution.py:541
  (133 shorter events, 200.4 us)
Async XLA Ops:
  9.2 36.2 %collective-permute-start.3 = (f32[20,56,128]{2,1,0:T(8,128)}, f32[20,56,128]{2,1,0:T(8,128)}, u32[]{:S(2)}, u32[]{:S(2)}) collective-permute-start(f32[20,56,128]{2,1,0:T(8,128)} %get-tuple-element.127), channel_id=1, source_target_pairs={{0,1},{1,0},{2,3},{3,2},{4,5},{5,4},{6,7},{7,6},{8,9},{9,8},{10,11... | collective-permute-start | bytes 1720328 | tf_op jit(solution)/shard_map/ppermute | solution.py:404
  10.4 35.0 %collective-permute-start.4 = (f32[20,56,128]{2,1,0:T(8,128)S(1)}, f32[20,56,128]{2,1,0:T(8,128)S(1)}, u32[]{:S(2)}, u32[]{:S(2)}) collective-permute-start(f32[20,56,128]{2,1,0:T(8,128)S(1)} %get-tuple-element.128), channel_id=1, source_target_pairs={{0,2},{1,3},{2,0},{3,1},{4,6},{5,7},{6,4},{7,5},{8,10},{9,11},{10,... | collective-permute-start | bytes 1720328 | tf_op jit(solution)/shard_map/ppermute | solution.py:404
  11.7 33.7 %collective-permute-start.5 = (f32[20,56,128]{2,1,0:T(8,128)S(1)}, f32[20,56,128]{2,1,0:T(8,128)S(1)}, u32[]{:S(2)}, u32[]{:S(2)}) collective-permute-start(f32[20,56,128]{2,1,0:T(8,128)S(1)} %get-tuple-element.129), channel_id=1, source_target_pairs={{0,3},{1,2},{2,1},{3,0},{4,7},{5,6},{6,5},{7,4},{8,11},{9,10},{10,... | collective-permute-start | bytes 1720328 | tf_op jit(solution)/shard_map/ppermute | solution.py:404
  12.1 27.7 %collective-permute-start.2 = (f32[8,3,31]{2,1,0:T(4,128)S(1)}, f32[8,3,31]{2,1,0:T(4,128)S(1)}, u32[]{:S(2)}, u32[]{:S(2)}) collective-permute-start(f32[8,3,31]{2,1,0:T(4,128)S(1)} %fusion.12), channel_id=1, source_target_pairs={{0,64},{16,80},{32,96},{48,112},{64,0},{80,16},{96,32},{112,48},{1... | collective-permute-start | bytes 8936 | tf_op jit(solution)/shard_map/ppermute | solution.py:383
  39.8 86.0 %all-to-all-start = ((f32[32,16,24,128]{3,2,1,0:T(8,128)}), f32[32,16,24,128]{3,2,1,0:T(8,128)}, u32[]{:S(2)}, u32[]{:S(2)}) async-start(f32[32,16,24,128]{3,2,1,0:T(8,128)} %bitcast.43), calls=%async_computation | async-start | bytes 12582912 | tf_op jit(solution)/shard_map/all_to_all | solution.py:504
  48.1 15.5 %collective-permute-start.6 = (f32[20,56,128]{2,1,0:T(8,128)S(1)}, f32[20,56,128]{2,1,0:T(8,128)S(1)}, u32[]{:S(2)}, u32[]{:S(2)}) collective-permute-start(f32[20,56,128]{2,1,0:T(8,128)S(1)} %fusion.11), channel_id=1, source_target_pairs={{0,4},{4,8},{8,12},{1,5},{5,9},{9,13},{2,6},{6,10},{10,14},{3,7},{... | collective-permute-start | bytes 1720328 | tf_op jit(solution)/shard_map/ppermute | solution.py:57
  65.5 16.7 %collective-permute-start.7 = (f32[20,56,128]{2,1,0:T(8,128)}, f32[20,56,128]{2,1,0:T(8,128)}, u32[]{:S(2)}, u32[]{:S(2)}) collective-permute-start(f32[20,56,128]{2,1,0:T(8,128)} %bitcast.9), channel_id=1, source_target_pairs={{4,0},{8,4},{12,8},{5,1},{9,5},{13,9},{6,2},{10,6},{14,10},{7,3},{... | collective-permute-start | bytes 1720328 | tf_op jit(solution)/shard_map/ppermute | solution.py:57
  132.1 22.2 %collective-permute-start.8 = (f32[32,24,128]{2,1,0:T(8,128)S(1)}, f32[32,24,128]{2,1,0:T(8,128)S(1)}, u32[]{:S(2)}, u32[]{:S(2)}) collective-permute-start(f32[32,24,128]{2,1,0:T(8,128)S(1)} %get-tuple-element.72), channel_id=1, source_target_pairs={{0,16},{16,32},{32,48},{48,64},{64,80},{80,96},{96,112},{1,17},{17... | collective-permute-start | bytes 1179656 | tf_op jit(solution)/shard_map/ppermute | solution.py:57
  161.2 35.8 %collective-permute-start.17 = (f32[4,64,16,128]{3,2,1,0:T(8,128)S(1)}, f32[4,64,16,128]{3,2,1,0:T(8,128)S(1)}, u32[]{:S(2)}, u32[]{:S(2)}) collective-permute-start(f32[4,64,16,128]{3,2,1,0:T(8,128)S(1)} %get-tuple-element.76), channel_id=1, source_target_pairs={{1,0},{2,1},{3,2},{5,4},{6,5},{7,6},{9,8},{10,9},{11,10},{13,12},{... | collective-permute-start | bytes 6291464 | tf_op jit(solution)/shard_map/ppermute | solution.py:57
  165.2 33.3 %collective-permute-start.16 = (f32[4,64,16,128]{3,2,1,0:T(8,128)S(1)}, f32[4,64,16,128]{3,2,1,0:T(8,128)S(1)}, u32[]{:S(2)}, u32[]{:S(2)}) collective-permute-start(f32[4,64,16,128]{3,2,1,0:T(8,128)S(1)} %get-tuple-element.77), channel_id=1, source_target_pairs={{0,1},{1,2},{2,3},{4,5},{5,6},{6,7},{8,9},{9,10},{10,11},{12,13},{... | collective-permute-start | bytes 6291464 | tf_op jit(solution)/shard_map/ppermute | solution.py:57
  188.4 32.6 %collective-permute-start.12 = (f32[4,64,16,128]{3,2,1,0:T(8,128)S(1)}, f32[4,64,16,128]{3,2,1,0:T(8,128)S(1)}, u32[]{:S(2)}, u32[]{:S(2)}) collective-permute-start(f32[4,64,16,128]{3,2,1,0:T(8,128)S(1)} %get-tuple-element.81), channel_id=1, source_target_pairs={{0,1},{1,2},{2,3},{4,5},{5,6},{6,7},{8,9},{9,10},{10,11},{12,13},{... | collective-permute-start | bytes 6291464 | tf_op jit(solution)/shard_map/ppermute | solution.py:57
  190.3 30.7 %collective-permute-start.13 = (f32[4,64,16,128]{3,2,1,0:T(8,128)S(1)}, f32[4,64,16,128]{3,2,1,0:T(8,128)S(1)}, u32[]{:S(2)}, u32[]{:S(2)}) collective-permute-start(f32[4,64,16,128]{3,2,1,0:T(8,128)S(1)} %get-tuple-element.82), channel_id=1, source_target_pairs={{1,0},{2,1},{3,2},{5,4},{6,5},{7,6},{9,8},{10,9},{11,10},{13,12},{... | collective-permute-start | bytes 6291464 | tf_op jit(solution)/shard_map/ppermute | solution.py:57
  204.4 27.4 %collective-permute-start.18 = (f32[4,16,24,128]{3,2,1,0:T(8,128)S(1)}, f32[4,16,24,128]{3,2,1,0:T(8,128)S(1)}, u32[]{:S(2)}, u32[]{:S(2)}) collective-permute-start(f32[4,16,24,128]{3,2,1,0:T(8,128)S(1)} %get-tuple-element.89), channel_id=1, source_target_pairs={{0,4},{4,8},{8,12},{1,5},{5,9},{9,13},{2,6},{6,10},{10,14},{3,7},{... | collective-permute-start | bytes 2359304 | tf_op jit(solution)/shard_map/ppermute | solution.py:57
  208.0 23.8 %collective-permute-start.19 = (f32[4,16,24,128]{3,2,1,0:T(8,128)S(1)}, f32[4,16,24,128]{3,2,1,0:T(8,128)S(1)}, u32[]{:S(2)}, u32[]{:S(2)}) collective-permute-start(f32[4,16,24,128]{3,2,1,0:T(8,128)S(1)} %get-tuple-element.90), channel_id=1, source_target_pairs={{4,0},{8,4},{12,8},{5,1},{9,5},{13,9},{6,2},{10,6},{14,10},{7,3},{... | collective-permute-start | bytes 2359304 | tf_op jit(solution)/shard_map/ppermute | solution.py:57
  226.8 13.9 %collective-permute-start.14 = (f32[4,16,24,128]{3,2,1,0:T(8,128)S(1)}, f32[4,16,24,128]{3,2,1,0:T(8,128)S(1)}, u32[]{:S(2)}, u32[]{:S(2)}) collective-permute-start(f32[4,16,24,128]{3,2,1,0:T(8,128)S(1)} %get-tuple-element.85), channel_id=1, source_target_pairs={{0,4},{4,8},{8,12},{1,5},{5,9},{9,13},{2,6},{6,10},{10,14},{3,7},{... | collective-permute-start | bytes 2359304 | tf_op jit(solution)/shard_map/ppermute | solution.py:57
  272.5 19.4 %collective-permute-start.24 = (f32[6,20,16,128]{3,2,1,0:T(8,128)S(1)}, f32[6,20,16,128]{3,2,1,0:T(8,128)S(1)}, u32[]{:S(2)}, u32[]{:S(2)}) collective-permute-start(f32[6,20,16,128]{3,2,1,0:T(8,128)S(1)} %get-tuple-element.124), channel_id=1, source_target_pairs={{0,1},{1,2},{2,3},{4,5},{5,6},{6,7},{8,9},{9,10},{10,11},{12,13},{... | collective-permute-start | bytes 2949128 | tf_op jit(solution)/shard_map/ppermute | solution.py:57
  280.9 15.7 %collective-permute-start.25 = (f32[6,20,16,128]{3,2,1,0:T(8,128)S(1)}, f32[6,20,16,128]{3,2,1,0:T(8,128)S(1)}, u32[]{:S(2)}, u32[]{:S(2)}) collective-permute-start(f32[6,20,16,128]{3,2,1,0:T(8,128)S(1)} %get-tuple-element.125), channel_id=1, source_target_pairs={{1,0},{2,1},{3,2},{5,4},{6,5},{7,6},{9,8},{10,9},{11,10},{13,12},{... | collective-permute-start | bytes 2949128 | tf_op jit(solution)/shard_map/ppermute | solution.py:57
  331.3 50.6 %collective-permute-start.34 = (f32[4,64,16,128]{3,2,1,0:T(8,128)}, f32[4,64,16,128]{3,2,1,0:T(8,128)S(1)}, u32[]{:S(2)}, u32[]{:S(2)}) collective-permute-start(f32[4,64,16,128]{3,2,1,0:T(8,128)} %get-tuple-element.109), channel_id=1, source_target_pairs={{0,1},{1,2},{2,3},{4,5},{5,6},{6,7},{8,9},{9,10},{10,11},{12,13},{... | collective-permute-start | bytes 6291464 | tf_op jit(solution)/shard_map/ppermute | solution.py:57
  334.5 47.5 %collective-permute-start.35 = (f32[4,64,16,128]{3,2,1,0:T(8,128)}, f32[4,64,16,128]{3,2,1,0:T(8,128)}, u32[]{:S(2)}, u32[]{:S(2)}) collective-permute-start(f32[4,64,16,128]{3,2,1,0:T(8,128)} %get-tuple-element.110), channel_id=1, source_target_pairs={{1,0},{2,1},{3,2},{5,4},{6,5},{7,6},{9,8},{10,9},{11,10},{13,12},{... | collective-permute-start | bytes 6291464 | tf_op jit(solution)/shard_map/ppermute | solution.py:57
  356.0 17.3 %collective-permute-start.29 = (f32[32,24,128]{2,1,0:T(8,128)S(1)}, f32[32,24,128]{2,1,0:T(8,128)S(1)}, u32[]{:S(2)}, u32[]{:S(2)}) collective-permute-start(f32[32,24,128]{2,1,0:T(8,128)S(1)} %get-tuple-element.101), channel_id=1, source_target_pairs={{16,0},{32,16},{48,32},{64,48},{80,64},{96,80},{112,96},{17,1},{33... | collective-permute-start | bytes 1179656 | tf_op jit(solution)/shard_map/ppermute | solution.py:57
  376.4 26.6 %collective-permute-start.30 = (f32[4,64,16,128]{3,2,1,0:T(8,128)S(1)}, f32[4,64,16,128]{3,2,1,0:T(8,128)S(1)}, u32[]{:S(2)}, u32[]{:S(2)}) collective-permute-start(f32[4,64,16,128]{3,2,1,0:T(8,128)S(1)} %get-tuple-element.103), channel_id=1, source_target_pairs={{0,1},{1,2},{2,3},{4,5},{5,6},{6,7},{8,9},{9,10},{10,11},{12,13},{... | collective-permute-start | bytes 6291464 | tf_op jit(solution)/shard_map/ppermute | solution.py:57
  380.0 27.6 %collective-permute-start.31 = (f32[4,64,16,128]{3,2,1,0:T(8,128)S(1)}, f32[4,64,16,128]{3,2,1,0:T(8,128)S(1)}, u32[]{:S(2)}, u32[]{:S(2)}) collective-permute-start(f32[4,64,16,128]{3,2,1,0:T(8,128)S(1)} %get-tuple-element.104), channel_id=1, source_target_pairs={{1,0},{2,1},{3,2},{5,4},{6,5},{7,6},{9,8},{10,9},{11,10},{13,12},{... | collective-permute-start | bytes 6291464 | tf_op jit(solution)/shard_map/ppermute | solution.py:57
  389.0 29.4 %collective-permute-start.36 = (f32[4,16,24,128]{3,2,1,0:T(8,128)S(1)}, f32[4,16,24,128]{3,2,1,0:T(8,128)S(1)}, u32[]{:S(2)}, u32[]{:S(2)}) collective-permute-start(f32[4,16,24,128]{3,2,1,0:T(8,128)S(1)} %get-tuple-element.112), channel_id=1, source_target_pairs={{0,4},{4,8},{8,12},{1,5},{5,9},{9,13},{2,6},{6,10},{10,14},{3,7},{... | collective-permute-start | bytes 2359304 | tf_op jit(solution)/shard_map/ppermute | solution.py:57
  392.3 26.1 %collective-permute-start.37 = (f32[4,16,24,128]{3,2,1,0:T(8,128)S(1)}, f32[4,16,24,128]{3,2,1,0:T(8,128)S(1)}, u32[]{:S(2)}, u32[]{:S(2)}) collective-permute-start(f32[4,16,24,128]{3,2,1,0:T(8,128)S(1)} %get-tuple-element.113), channel_id=1, source_target_pairs={{4,0},{8,4},{12,8},{5,1},{9,5},{13,9},{6,2},{10,6},{14,10},{7,3},{... | collective-permute-start | bytes 2359304 | tf_op jit(solution)/shard_map/ppermute | solution.py:57
  (29 other events, 280.9 us)

commit v8 on v6

--- a/solution.py
+++ b/solution.py
@@ -93,7 +93,7 @@
                     hi, lo = split(jnp.concatenate([one[:, :XC], one[:, XC:]], axis=0))
                     dest[u, rows, :] = jnp.concatenate([hi, lo], axis=1)
 
-    step = 12
+    step = 24
 
     @pl.loop(0, ZW // 4 // step)
     def _(b):
@@ -256,7 +256,7 @@
     def pair(ref, z):
         return jnp.concatenate([ref[0, z], ref[0, z + 1]], axis=1)
 
-    @pl.loop(0, ZC // 2, unroll=4)
+    @pl.loop(0, ZC // 2, unroll=8)
     def _(b):
         z = 2 * b
         rows = jnp.concatenate([pair(before, z), pair(value, z), pair(after, z), empty], axis=0)

time: 523 us -> 517 us (0.989)
  Pallas kernels: 163 us -> 151 us
  waiting for transfers between devices: 125 us -> 131 us
    pallas_call x4, Pallas kernels: 23.6 us -> 14.9 us  [adjoint_y(): pl.pallas_call(adjoint_y_kernel, name='adjoint_y', grid=(GROUP,), out_sha...]
  transfers between devices with their start and end apart: 39 -> 39, of which waited for: 23 -> 22; matrix products, arithmetic and copies ran while one was open for 4% -> 4% of each run, Pallas kernels for 22% -> 20%
where the time goes in v8:
time: 517 us; the launch traced here: 515 us
  Pallas kernels  151 us (29%)
  waiting for transfers between devices  131 us (25%)
  starting transfers between devices  113 us (22%)
  blocking collectives  86.2 us (17%)
  local copies, waits for them, and re-layouts  29.2 us (6%)
    ppermute x32, waiting for transfers between devices, exchange(): return (lax.ppermute(high, axis, up), lax.ppermute(low, axis, down))  103 us
    ppermute x32, starting transfers between devices, exchange(): return (lax.ppermute(high, axis, up), lax.ppermute(low, axis, down))  96.7 us
    all_to_all x1, blocking collectives, per_device(): lax.all_to_all(parts, V + S, 0, 0, tiled=True)  86.2 us
    pallas_call x2, Pallas kernels, forward(): pl.pallas_call(functools.partial(blur_and_divide_kernel, g), name='blur_a...  33.5 us
    pallas_call x2, Pallas kernels, forward(): pl.pallas_call(functools.partial(blur_kernel, g), name='blur', grid=(GROU...  26 us
    pallas_call x2, Pallas kernels, adjoint_z(): pl.pallas_call(functools.partial(last_logs_kernel, g), name='last_logs',...  22 us
    unnamed x53, local copies, waits for them, and re-layouts  20.5 us
    pallas_call x2, Pallas kernels, adjoint_z(): pl.pallas_call(functools.partial(first_logs_kernel, g), name='first_logs'...  17.9 us
  transfers between devices with their start and end apart: 39, of which 22 were waited for; matrix products, arithmetic and copies ran while one was open for 4% of the time, Pallas kernels for 20%

profile of v8, /device:TPU:1, one launch (start us, length us, event | category | flops | bytes accessed | tf_op | source)
XLA Modules:
  0.0 515.4 jit_solution(15332390827875007734)
XLA Ops:
  23.2 16.5 %collective-permute-done.2 = f32[8,3,31]{2,1,0:T(4,128)S(1)} collective-permute-done((f32[8,3,31]{2,1,0:T(4,128)S(1)}, f32[8,3,31]{2,1,0:T(4,128)S(1)}, u32[]{:S(2)}, u32[]{:S(2)}) %collective-permute-start.2) | collective-permute-done | bytes 3008 | tf_op jit(solution)/shard_map/ppermute | solution.py:383
  39.7 5.6 %all-to-all-start = ((f32[32,16,24,128]{3,2,1,0:T(8,128)}), f32[32,16,24,128]{3,2,1,0:T(8,128)}, u32[]{:S(2)}, u32[]{:S(2)}) async-start(f32[32,16,24,128]{3,2,1,0:T(8,128)} %bitcast.43), calls=%async_computation | async-start | bytes 12582912 | tf_op jit(solution)/shard_map/all_to_all | solution.py:504
  52.4 11.1 %collective-permute-done.6 = f32[20,56,128]{2,1,0:T(8,128)} collective-permute-done((f32[20,56,128]{2,1,0:T(8,128)S(1)}, f32[20,56,128]{2,1,0:T(8,128)}, u32[]{:S(2)}, u32[]{:S(2)}) %collective-permute-start.6) | collective-permute-done | bytes 573472 | tf_op jit(solution)/shard_map/ppermute | solution.py:57
  68.1 9.7 %matrices.1 = (f32[192,192]{1,0:T(8,128)S(1)}, bf16[8,256,256]{2,1,0:T(8,128)(2,1)S(1)}, bf16[8,4,256,256]{3,2,1,0:T(8,128)(2,1)S(1)}, bf16[8,256,256]{2,1,0:T(8...) custom-call(f32[8,93]{1,0:T(8,128)S(1)} %reshape.33.taps), custom_call_target="tpu_custom_call" | custom-call | flops 1000000000 | bytes 2000000 | tf_op jit(solution)/shard_map/matrices/pallas_call | solution.py:467
  84.3 13.0 %blur.3.blurred = f32[4,64,24,128]{3,2,1,0:T(8,128)S(1)} custom-call(f32[8,93]{1,0:T(8,128)S(1)} %reshape.33.taps, f32[6,20,56,128]{3,2,1,0:T(8,128)S(1)} %bitcast_dynamic-update-slice_fusion.est, f32[192,192]{1,0:T(8,128)S(1)} %get-tuple-element.54.wy, bf16[8,256,256]{2,1,0:T(8,128)(2,1)S(1)} %get-tuple-element.55.wown, ...), custom_call_target="tpu_custom_call" | custom-call | flops 17999998976 | bytes 36000000 | tf_op jit(solution)/shard_map/blur/pallas_call | solution.py:177
  99.0 13.0 %blur.2.blurred = f32[4,64,24,128]{3,2,1,0:T(8,128)S(1)} custom-call(f32[8,93]{1,0:T(8,128)S(1)} %reshape.33.taps, f32[6,20,56,128]{3,2,1,0:T(8,128)S(1)} %bitcast_dynamic-update-slice_fusion.est, f32[192,192]{1,0:T(8,128)S(1)} %get-tuple-element.54.wy, bf16[8,256,256]{2,1,0:T(8,128)(2,1)S(1)} %get-tuple-element.55.wown, ...), custom_call_target="tpu_custom_call" | custom-call | flops 17999998976 | bytes 36000000 | tf_op jit(solution)/shard_map/blur/pallas_call | solution.py:177
  113.7 12.0 %all-to-all-done = f32[32,16,24,128]{3,2,1,0:T(8,128)} async-done(((f32[32,16,24,128]{3,2,1,0:T(8,128)}), f32[32,16,24,128]{3,2,1,0:T(8,128)}, u32[]{:S(2)}, u32[]{:S(2)}) %all-to-all-start) | async-done | bytes 6291488 | tf_op jit(solution)/shard_map/all_to_all | solution.py:504
  127.6 4.6 divide.3
  132.2 14.7 %collective-permute-start.14 = (f32[32,24,128]{2,1,0:T(8,128)S(1)}, f32[32,24,128]{2,1,0:T(8,128)S(1)}, u32[]{:S(2)}, u32[]{:S(2)}) collective-permute-start(f32[32,24,128]{2,1,0:T(8,128)S(1)} %get-tuple-element.70), channel_id=1, source_target_pairs={{0,16},{16,32},{32,48},{48,64},{64,80},{80,96},{96,112},{1,17},{17... | collective-permute-start | bytes 1179656 | tf_op jit(solution)/shard_map/ppermute | solution.py:57
  178.0 10.5 %collective-permute-done.16.before = f32[4,64,16,128]{3,2,1,0:T(8,128)S(1)} collective-permute-done((f32[4,64,16,128]{3,2,1,0:T(8,128)S(1)}, f32[4,64,16,128]{3,2,1,0:T(8,128)S(1)}, u32[]{:S(2)}, u32[]{:S(2)}) %collective-permute-start.16) | collective-permute-done | bytes 2097184 | tf_op jit(solution)/shard_map/ppermute | solution.py:57
  201.0 10.0 %collective-permute-done.10.before = f32[4,64,16,128]{3,2,1,0:T(8,128)S(1)} collective-permute-done((f32[4,64,16,128]{3,2,1,0:T(8,128)S(1)}, f32[4,64,16,128]{3,2,1,0:T(8,128)S(1)}, u32[]{:S(2)}, u32[]{:S(2)}) %collective-permute-start.10) | collective-permute-done | bytes 2097184 | tf_op jit(solution)/shard_map/ppermute | solution.py:57
  222.4 9.0 %first_logs.2.logs = f32[64,24,128]{2,1,0:T(8,128)S(1)} custom-call(f32[8,93]{1,0:T(8,128)S(1)} %reshape.33.taps, f32[4,64,24,128]{3,2,1,0:T(8,128)S(1)} %get-tuple-element.75.value, f32[4,16,24,128]{3,2,1,0:T(8,128)S(1)} %collective-permute-done.18.before, f32[4,16,24,128]{3,2,1,0:T(8,128)S(1)} %collective-permute-done.19.after), custom_call_target="tpu_custom_call" | custom-call | flops 8999999488 | bytes 18000000 | tf_op jit(solution)/shard_map/first_logs/pallas_call | solution.py:357
  234.3 10.6 %last_logs.2 = (f32[64,24,128]{2,1,0:T(8,128)S(1)}, f32[16,24,128]{2,1,0:T(8,128)S(1)}) custom-call(f32[8,93]{1,0:T(8,128)S(1)} %reshape.33.taps, f32[4,64,24,128]{3,2,1,0:T(8,128)S(1)} %get-tuple-element.66.value, f32[4,16,24,128]{3,2,1,0:T(8,128)S(1)} %collective-permute-done.12.before, f32[4,16,24,128]{3,2,1,0:T(8,128)S(1)} %collective-permute-done.13.after, ...), custom_call_target="tpu_custom_call" | custom-call | flops 10000000000 | bytes 20000000 | tf_op jit(solution)/shard_map/last_logs/pallas_call | solution.py:367
  265.4 6.0 %collective-permute-start.24 = (f32[6,20,16,128]{3,2,1,0:T(8,128)S(1)}, f32[6,20,16,128]{3,2,1,0:T(8,128)S(1)}, u32[]{:S(2)}, u32[]{:S(2)}) collective-permute-start(f32[6,20,16,128]{3,2,1,0:T(8,128)S(1)} %get-tuple-element.108), channel_id=1, source_target_pairs={{0,1},{1,2},{2,3},{4,5},{5,6},{6,7},{8,9},{9,10},{10,11},{12,13},{... | collective-permute-start | bytes 2949128 | tf_op jit(solution)/shard_map/ppermute | solution.py:57
  273.8 8.7 %collective-permute-done.24 = f32[6,20,16,128]{3,2,1,0:T(8,128)S(1)} collective-permute-done((f32[6,20,16,128]{3,2,1,0:T(8,128)S(1)}, f32[6,20,16,128]{3,2,1,0:T(8,128)S(1)}, u32[]{:S(2)}, u32[]{:S(2)}) %collective-permute-start.24) | collective-permute-done | bytes 983072 | tf_op jit(solution)/shard_map/ppermute | solution.py:57
  282.5 4.7 collective-permute-done.25
  287.4 16.8 %blur_and_divide.3 = (f32[4,64,24,128]{3,2,1,0:T(8,128)S(1)}, f32[32,24,128]{2,1,0:T(8,128)S(1)}, f32[32,24,128]{2,1,0:T(8,128)S(1)}) custom-call(f32[8,93]{1,0:T(8,128)S(1)} %reshape.33.taps, f32[6,20,56,128]{3,2,1,0:T(8,128)S(1)} %pad_maximum_fusion.est, f32[192,192]{1,0:T(8,128)S(1)} %copy-done.14, bf16[8,256,256]{2,1,0:T(8,128)(2,1)S(1)} %copy-done.8, ...), custom_call_target="tpu_custom_call" | custom-call | flops 24000000000 | bytes 48000000 | tf_op jit(solution)/shard_map/blur_and_divide/pallas_call | solution.py:187
  307.6 16.7 %blur_and_divide.2 = (f32[4,64,24,128]{3,2,1,0:T(8,128)S(1)}, f32[32,24,128]{2,1,0:T(8,128)S(1)}, f32[32,24,128]{2,1,0:T(8,128)S(1)}) custom-call(f32[8,93]{1,0:T(8,128)S(1)} %reshape.33.taps, f32[6,20,56,128]{3,2,1,0:T(8,128)S(1)} %pad_maximum_fusion.est, f32[192,192]{1,0:T(8,128)S(1)} %copy-done.14, bf16[8,256,256]{2,1,0:T(8,128)(2,1)S(1)} %copy-done.8, ...), custom_call_target="tpu_custom_call" | custom-call | flops 24000000000 | bytes 48000000 | tf_op jit(solution)/shard_map/blur_and_divide/pallas_call | solution.py:187
  326.0 6.9 %collective-permute-start.26 = (f32[32,24,128]{2,1,0:T(8,128)S(1)}, f32[32,24,128]{2,1,0:T(8,128)S(1)}, u32[]{:S(2)}, u32[]{:S(2)}) collective-permute-start(f32[32,24,128]{2,1,0:T(8,128)S(1)} %get-tuple-element.81), channel_id=1, source_target_pairs={{0,16},{16,32},{32,48},{48,64},{64,80},{80,96},{96,112},{1,17},{17... | collective-permute-start | bytes 1179656 | tf_op jit(solution)/shard_map/ppermute | solution.py:57
  353.5 13.3 %collective-permute-done.34.before = f32[4,64,16,128]{3,2,1,0:T(8,128)S(1)} collective-permute-done((f32[4,64,16,128]{3,2,1,0:T(8,128)S(1)}, f32[4,64,16,128]{3,2,1,0:T(8,128)S(1)}, u32[]{:S(2)}, u32[]{:S(2)}) %collective-permute-start.34) | collective-permute-done | bytes 2097184 | tf_op jit(solution)/shard_map/ppermute | solution.py:57
  379.3 10.0 %collective-permute-done.28.before = f32[4,64,16,128]{3,2,1,0:T(8,128)S(1)} collective-permute-done((f32[4,64,16,128]{3,2,1,0:T(8,128)S(1)}, f32[4,64,16,128]{3,2,1,0:T(8,128)S(1)}, u32[]{:S(2)}, u32[]{:S(2)}) %collective-permute-start.28) | collective-permute-done | bytes 2097184 | tf_op jit(solution)/shard_map/ppermute | solution.py:57
  401.3 9.0 %first_logs.3.logs = f32[64,24,128]{2,1,0:T(8,128)S(1)} custom-call(f32[8,93]{1,0:T(8,128)S(1)} %reshape.33.taps, f32[4,64,24,128]{3,2,1,0:T(8,128)S(1)} %get-tuple-element.95.value, f32[4,16,24,128]{3,2,1,0:T(8,128)S(1)} %collective-permute-done.36.before, f32[4,16,24,128]{3,2,1,0:T(8,128)S(1)} %collective-permute-done.37.after), custom_call_target="tpu_custom_call" | custom-call | flops 8999999488 | bytes 18000000 | tf_op jit(solution)/shard_map/first_logs/pallas_call | solution.py:357
  412.7 11.4 %last_logs.3 = (f32[64,24,128]{2,1,0:T(8,128)S(1)}, f32[16,24,128]{2,1,0:T(8,128)}) custom-call(f32[8,93]{1,0:T(8,128)S(1)} %reshape.33.taps, f32[4,64,24,128]{3,2,1,0:T(8,128)S(1)} %get-tuple-element.86.value, f32[4,16,24,128]{3,2,1,0:T(8,128)S(1)} %collective-permute-done.30.before, f32[4,16,24,128]{3,2,1,0:T(8,128)S(1)} %collective-permute-done.31.after, ...), custom_call_target="tpu_custom_call" | custom-call | flops 10000000000 | bytes 20000000 | tf_op jit(solution)/shard_map/last_logs/pallas_call | solution.py:367
  424.8 86.2 %all_to_all.10 = f32[32,16,24,128]{3,2,1,0:T(8,128)S(1)} all-to-all(f32[32,16,24,128]{3,2,1,0:T(8,128)S(1)} %bitcast.44), channel_id=1, replica_groups=mesh['yh'=2,'x'=4,'z'=4,'yl'=2,'co'=2] {'yh','x','yl','co'}, dimensions={0} | all-to-all | bytes 12582912 | tf_op jit(solution)/shard_map/all_to_all | solution.py:535
  (151 shorter events, 184.6 us)
Async XLA Ops:
  9.1 36.2 %collective-permute-start.3 = (f32[20,56,128]{2,1,0:T(8,128)}, f32[20,56,128]{2,1,0:T(8,128)S(1)}, u32[]{:S(2)}, u32[]{:S(2)}) collective-permute-start(f32[20,56,128]{2,1,0:T(8,128)} %get-tuple-element.111), channel_id=1, source_target_pairs={{0,1},{1,0},{2,3},{3,2},{4,5},{5,4},{6,7},{7,6},{8,9},{9,8},{10,11... | collective-permute-start | bytes 1720328 | tf_op jit(solution)/shard_map/ppermute | solution.py:404
  10.3 35.0 %collective-permute-start.4 = (f32[20,56,128]{2,1,0:T(8,128)S(1)}, f32[20,56,128]{2,1,0:T(8,128)S(1)}, u32[]{:S(2)}, u32[]{:S(2)}) collective-permute-start(f32[20,56,128]{2,1,0:T(8,128)S(1)} %get-tuple-element.112), channel_id=1, source_target_pairs={{0,2},{1,3},{2,0},{3,1},{4,6},{5,7},{6,4},{7,5},{8,10},{9,11},{10,... | collective-permute-start | bytes 1720328 | tf_op jit(solution)/shard_map/ppermute | solution.py:404
  11.6 33.7 %collective-permute-start.5 = (f32[20,56,128]{2,1,0:T(8,128)S(1)}, f32[20,56,128]{2,1,0:T(8,128)}, u32[]{:S(2)}, u32[]{:S(2)}) collective-permute-start(f32[20,56,128]{2,1,0:T(8,128)S(1)} %get-tuple-element.113), channel_id=1, source_target_pairs={{0,3},{1,2},{2,1},{3,0},{4,7},{5,6},{6,5},{7,4},{8,11},{9,10},{10,... | collective-permute-start | bytes 1720328 | tf_op jit(solution)/shard_map/ppermute | solution.py:404
  12.0 27.7 %collective-permute-start.2 = (f32[8,3,31]{2,1,0:T(4,128)S(1)}, f32[8,3,31]{2,1,0:T(4,128)S(1)}, u32[]{:S(2)}, u32[]{:S(2)}) collective-permute-start(f32[8,3,31]{2,1,0:T(4,128)S(1)} %fusion.12), channel_id=1, source_target_pairs={{0,64},{16,80},{32,96},{48,112},{64,0},{80,16},{96,32},{112,48},{1... | collective-permute-start | bytes 8936 | tf_op jit(solution)/shard_map/ppermute | solution.py:383
  39.7 86.0 %all-to-all-start = ((f32[32,16,24,128]{3,2,1,0:T(8,128)}), f32[32,16,24,128]{3,2,1,0:T(8,128)}, u32[]{:S(2)}, u32[]{:S(2)}) async-start(f32[32,16,24,128]{3,2,1,0:T(8,128)} %bitcast.43), calls=%async_computation | async-start | bytes 12582912 | tf_op jit(solution)/shard_map/all_to_all | solution.py:504
  66.6 16.6 %collective-permute-start.7 = (f32[20,56,128]{2,1,0:T(8,128)}, f32[20,56,128]{2,1,0:T(8,128)}, u32[]{:S(2)}, u32[]{:S(2)}) collective-permute-start(f32[20,56,128]{2,1,0:T(8,128)} %bitcast.9), channel_id=1, source_target_pairs={{4,0},{8,4},{12,8},{5,1},{9,5},{13,9},{6,2},{10,6},{14,10},{7,3},{... | collective-permute-start | bytes 1720328 | tf_op jit(solution)/shard_map/ppermute | solution.py:57
  132.2 26.3 %collective-permute-start.14 = (f32[32,24,128]{2,1,0:T(8,128)S(1)}, f32[32,24,128]{2,1,0:T(8,128)S(1)}, u32[]{:S(2)}, u32[]{:S(2)}) collective-permute-start(f32[32,24,128]{2,1,0:T(8,128)S(1)} %get-tuple-element.70), channel_id=1, source_target_pairs={{0,16},{16,32},{32,48},{48,64},{64,80},{80,96},{96,112},{1,17},{17... | collective-permute-start | bytes 1179656 | tf_op jit(solution)/shard_map/ppermute | solution.py:57
  161.8 26.8 %collective-permute-start.16 = (f32[4,64,16,128]{3,2,1,0:T(8,128)S(1)}, f32[4,64,16,128]{3,2,1,0:T(8,128)S(1)}, u32[]{:S(2)}, u32[]{:S(2)}) collective-permute-start(f32[4,64,16,128]{3,2,1,0:T(8,128)S(1)} %get-tuple-element.73), channel_id=1, source_target_pairs={{0,1},{1,2},{2,3},{4,5},{5,6},{6,7},{8,9},{9,10},{10,11},{12,13},{... | collective-permute-start | bytes 6291464 | tf_op jit(solution)/shard_map/ppermute | solution.py:57
  163.7 27.6 %collective-permute-start.17 = (f32[4,64,16,128]{3,2,1,0:T(8,128)S(1)}, f32[4,64,16,128]{3,2,1,0:T(8,128)S(1)}, u32[]{:S(2)}, u32[]{:S(2)}) collective-permute-start(f32[4,64,16,128]{3,2,1,0:T(8,128)S(1)} %get-tuple-element.74), channel_id=1, source_target_pairs={{1,0},{2,1},{3,2},{5,4},{6,5},{7,6},{9,8},{10,9},{11,10},{13,12},{... | collective-permute-start | bytes 6291464 | tf_op jit(solution)/shard_map/ppermute | solution.py:57
  170.9 40.1 %collective-permute-start.10 = (f32[4,64,16,128]{3,2,1,0:T(8,128)S(1)}, f32[4,64,16,128]{3,2,1,0:T(8,128)S(1)}, u32[]{:S(2)}, u32[]{:S(2)}) collective-permute-start(f32[4,64,16,128]{3,2,1,0:T(8,128)S(1)} %get-tuple-element.63), channel_id=1, source_target_pairs={{0,1},{1,2},{2,3},{4,5},{5,6},{6,7},{8,9},{9,10},{10,11},{12,13},{... | collective-permute-start | bytes 6291464 | tf_op jit(solution)/shard_map/ppermute | solution.py:57
  172.9 41.0 %collective-permute-start.11 = (f32[4,64,16,128]{3,2,1,0:T(8,128)S(1)}, f32[4,64,16,128]{3,2,1,0:T(8,128)S(1)}, u32[]{:S(2)}, u32[]{:S(2)}) collective-permute-start(f32[4,64,16,128]{3,2,1,0:T(8,128)S(1)} %get-tuple-element.64), channel_id=1, source_target_pairs={{1,0},{2,1},{3,2},{5,4},{6,5},{7,6},{9,8},{10,9},{11,10},{13,12},{... | collective-permute-start | bytes 6291464 | tf_op jit(solution)/shard_map/ppermute | solution.py:57
  195.1 27.3 %collective-permute-start.18 = (f32[4,16,24,128]{3,2,1,0:T(8,128)S(1)}, f32[4,16,24,128]{3,2,1,0:T(8,128)S(1)}, u32[]{:S(2)}, u32[]{:S(2)}) collective-permute-start(f32[4,16,24,128]{3,2,1,0:T(8,128)S(1)} %get-tuple-element.76), channel_id=1, source_target_pairs={{0,4},{4,8},{8,12},{1,5},{5,9},{9,13},{2,6},{6,10},{10,14},{3,7},{... | collective-permute-start | bytes 2359304 | tf_op jit(solution)/shard_map/ppermute | solution.py:57
  198.7 23.7 %collective-permute-start.19 = (f32[4,16,24,128]{3,2,1,0:T(8,128)S(1)}, f32[4,16,24,128]{3,2,1,0:T(8,128)S(1)}, u32[]{:S(2)}, u32[]{:S(2)}) collective-permute-start(f32[4,16,24,128]{3,2,1,0:T(8,128)S(1)} %get-tuple-element.77), channel_id=1, source_target_pairs={{4,0},{8,4},{12,8},{5,1},{9,5},{13,9},{6,2},{10,6},{14,10},{7,3},{... | collective-permute-start | bytes 2359304 | tf_op jit(solution)/shard_map/ppermute | solution.py:57
  265.4 17.1 %collective-permute-start.24 = (f32[6,20,16,128]{3,2,1,0:T(8,128)S(1)}, f32[6,20,16,128]{3,2,1,0:T(8,128)S(1)}, u32[]{:S(2)}, u32[]{:S(2)}) collective-permute-start(f32[6,20,16,128]{3,2,1,0:T(8,128)S(1)} %get-tuple-element.108), channel_id=1, source_target_pairs={{0,1},{1,2},{2,3},{4,5},{5,6},{6,7},{8,9},{9,10},{10,11},{12,13},{... | collective-permute-start | bytes 2949128 | tf_op jit(solution)/shard_map/ppermute | solution.py:57
  271.5 15.7 %collective-permute-start.25 = (f32[6,20,16,128]{3,2,1,0:T(8,128)S(1)}, f32[6,20,16,128]{3,2,1,0:T(8,128)S(1)}, u32[]{:S(2)}, u32[]{:S(2)}) collective-permute-start(f32[6,20,16,128]{3,2,1,0:T(8,128)S(1)} %get-tuple-element.109), channel_id=1, source_target_pairs={{1,0},{2,1},{3,2},{5,4},{6,5},{7,6},{9,8},{10,9},{11,10},{13,12},{... | collective-permute-start | bytes 2949128 | tf_op jit(solution)/shard_map/ppermute | solution.py:57
  304.2 30.0 %collective-permute-start.32 = (f32[32,24,128]{2,1,0:T(8,128)S(1)}, f32[32,24,128]{2,1,0:T(8,128)S(1)}, u32[]{:S(2)}, u32[]{:S(2)}) collective-permute-start(f32[32,24,128]{2,1,0:T(8,128)S(1)} %get-tuple-element.90), channel_id=1, source_target_pairs={{0,16},{16,32},{32,48},{48,64},{64,80},{80,96},{96,112},{1,17},{17... | collective-permute-start | bytes 1179656 | tf_op jit(solution)/shard_map/ppermute | solution.py:57
  306.1 28.1 %collective-permute-start.33 = (f32[32,24,128]{2,1,0:T(8,128)S(1)}, f32[32,24,128]{2,1,0:T(8,128)S(1)}, u32[]{:S(2)}, u32[]{:S(2)}) collective-permute-start(f32[32,24,128]{2,1,0:T(8,128)S(1)} %get-tuple-element.91), channel_id=1, source_target_pairs={{16,0},{32,16},{48,32},{64,48},{80,64},{96,80},{112,96},{17,1},{33... | collective-permute-start | bytes 1179656 | tf_op jit(solution)/shard_map/ppermute | solution.py:57
  326.0 15.9 %collective-permute-start.26 = (f32[32,24,128]{2,1,0:T(8,128)S(1)}, f32[32,24,128]{2,1,0:T(8,128)S(1)}, u32[]{:S(2)}, u32[]{:S(2)}) collective-permute-start(f32[32,24,128]{2,1,0:T(8,128)S(1)} %get-tuple-element.81), channel_id=1, source_target_pairs={{0,16},{16,32},{32,48},{48,64},{64,80},{80,96},{96,112},{1,17},{17... | collective-permute-start | bytes 1179656 | tf_op jit(solution)/shard_map/ppermute | solution.py:57
  337.4 29.5 %collective-permute-start.34 = (f32[4,64,16,128]{3,2,1,0:T(8,128)S(1)}, f32[4,64,16,128]{3,2,1,0:T(8,128)S(1)}, u32[]{:S(2)}, u32[]{:S(2)}) collective-permute-start(f32[4,64,16,128]{3,2,1,0:T(8,128)S(1)} %get-tuple-element.93), channel_id=1, source_target_pairs={{0,1},{1,2},{2,3},{4,5},{5,6},{6,7},{8,9},{9,10},{10,11},{12,13},{... | collective-permute-start | bytes 6291464 | tf_op jit(solution)/shard_map/ppermute | solution.py:57
  339.7 31.1 %collective-permute-start.35 = (f32[4,64,16,128]{3,2,1,0:T(8,128)S(1)}, f32[4,64,16,128]{3,2,1,0:T(8,128)S(1)}, u32[]{:S(2)}, u32[]{:S(2)}) collective-permute-start(f32[4,64,16,128]{3,2,1,0:T(8,128)S(1)} %get-tuple-element.94), channel_id=1, source_target_pairs={{1,0},{2,1},{3,2},{5,4},{6,5},{7,6},{9,8},{10,9},{11,10},{13,12},{... | collective-permute-start | bytes 6291464 | tf_op jit(solution)/shard_map/ppermute | solution.py:57
  348.4 40.9 %collective-permute-start.28 = (f32[4,64,16,128]{3,2,1,0:T(8,128)S(1)}, f32[4,64,16,128]{3,2,1,0:T(8,128)S(1)}, u32[]{:S(2)}, u32[]{:S(2)}) collective-permute-start(f32[4,64,16,128]{3,2,1,0:T(8,128)S(1)} %get-tuple-element.84), channel_id=1, source_target_pairs={{0,1},{1,2},{2,3},{4,5},{5,6},{6,7},{8,9},{9,10},{10,11},{12,13},{... | collective-permute-start | bytes 6291464 | tf_op jit(solution)/shard_map/ppermute | solution.py:57
  351.6 41.3 %collective-permute-start.29 = (f32[4,64,16,128]{3,2,1,0:T(8,128)S(1)}, f32[4,64,16,128]{3,2,1,0:T(8,128)S(1)}, u32[]{:S(2)}, u32[]{:S(2)}) collective-permute-start(f32[4,64,16,128]{3,2,1,0:T(8,128)S(1)} %get-tuple-element.85), channel_id=1, source_target_pairs={{1,0},{2,1},{3,2},{5,4},{6,5},{7,6},{9,8},{10,9},{11,10},{13,12},{... | collective-permute-start | bytes 6291464 | tf_op jit(solution)/shard_map/ppermute | solution.py:57
  374.5 26.8 %collective-permute-start.36 = (f32[4,16,24,128]{3,2,1,0:T(8,128)S(1)}, f32[4,16,24,128]{3,2,1,0:T(8,128)S(1)}, u32[]{:S(2)}, u32[]{:S(2)}) collective-permute-start(f32[4,16,24,128]{3,2,1,0:T(8,128)S(1)} %get-tuple-element.96), channel_id=1, source_target_pairs={{0,4},{4,8},{8,12},{1,5},{5,9},{9,13},{2,6},{6,10},{10,14},{3,7},{... | collective-permute-start | bytes 2359304 | tf_op jit(solution)/shard_map/ppermute | solution.py:57
  378.0 23.3 %collective-permute-start.37 = (f32[4,16,24,128]{3,2,1,0:T(8,128)S(1)}, f32[4,16,24,128]{3,2,1,0:T(8,128)S(1)}, u32[]{:S(2)}, u32[]{:S(2)}) collective-permute-start(f32[4,16,24,128]{3,2,1,0:T(8,128)S(1)} %get-tuple-element.97), channel_id=1, source_target_pairs={{4,0},{8,4},{12,8},{5,1},{9,5},{13,9},{6,2},{10,6},{14,10},{7,3},{... | collective-permute-start | bytes 2359304 | tf_op jit(solution)/shard_map/ppermute | solution.py:57
  (38 other events, 425.4 us)
